TPU v7x, 128 devices: a whole 4x4x4 slice. The times are simulated.
128 devices in a mesh: seq: 32 (over x, z, core), head: 4 (over y).
Axes of the slice: x: 4, y: 4, z: 4, core: 2. Of those that a mesh axis runs over, the one named last changes fastest.
Arguments:
- patches: bfloat16 [131072, 768], P('seq'), may hold values from -6 to 6
- slot_image: int32 [512], P('seq'), may hold values from -1 to 255, as said below
- slot_dest: int32 [512], P('seq'), may hold values from -1 to 255, as said below
- enc_gain: float32 [768], replicated, may hold values from 0.1 to 1.9
- w_qkv: bfloat16 [3, 768, 768], P(None, None, 'head'), may hold values from -1.2 to 1.2
- w_out: bfloat16 [768, 768], P('head'), may hold values from -0.21875 to 0.21875
- fast_gain: float32 [768], replicated, may hold values from 0.1 to 1.9
- w_fast: bfloat16 [3, 768, 768], P(None, None, 'head'), may hold values from -0.21875 to 0.21875
- w_rate: bfloat16 [768, 4], P(None, 'head'), may hold values from -0.21875 to 0.21875
- fast_gate_up: float32 [4, 2, 192, 384], P('head'), may hold values from -0.4375 to 0.4375
- fast_down: float32 [4, 384, 192], P('head'), may hold values from -0.3125 to 0.3125
Outputs:
- view_out: bfloat16 [65536, 768], P('seq', 'head')
Inputs may be any that keep to these rules, and one draw needn't show every extreme that they name: slot_dest gives for each slot the view-order block that its block becomes, or -1 for an empty slot; every view-order block is named by exactly one slot. Slots 2i and 2i + 1 of one seq index are both empty or name view blocks 2m and 2m + 1. The slots of one seq index name at most 2 blocks of any one view shard (blocks s * 8 to (s + 1) * 8 - 1), and some seq index uses all of its slots. slot_image is -1 exactly where slot_dest is -1; an image is one block or the two blocks of a slot pair, and different images have different ids.
All inputs are finite; a program needn't handle non-finite values.
Results may differ from a plain program's by a relative error of at most 0.035.
Values may be sent and summed in bfloat16 or wider, within the bound.
No kernel may reach another device: no remote copies, remote signals or barrier semaphores. Data moves between devices by JAX's collectives and lax.ppermute only.
A program may use at most 128 MiB of HBM per device.

v0:
```python
import jax
import jax.numpy as jnp
from jax import lax
from jax.experimental import pallas as pl
from jax.experimental.pallas import tpu as pltpu
from jax.sharding import Mesh, PartitionSpec as P

D = 768
HDIM = 64
BLK = 256
SPAN = 512
FW = 192
FH = 384
SEQ = 32
HEADS = 4
PAIRS = 8
LT = 3
GT = 224
EPSILON = 1e-06
RATE_SCALE = 0.1
VTOKENS = 65536
BF = jnp.bfloat16
F32 = jnp.float32
SEQ_AXES = ("x", "z", "core")
ALL_AXES = ("x", "z", "core", "head")
PARAMS = pltpu.CompilerParams(vmem_limit_bytes=48 << 20)

ANY = pl.BlockSpec(memory_space=pl.ANY)
SMEM = pl.BlockSpec(memory_space=pltpu.SMEM)
VMEM = pl.BlockSpec(memory_space=pltpu.VMEM)


def mm(a, b):
    return jnp.dot(a, b, preferred_element_type=F32)


def mm_nt(a, b):
    return lax.dot_general(a, b, (((1,), (1,)), ((), ())), preferred_element_type=F32)


def mm_tn(a, b):
    return lax.dot_general(a, b, (((0,), (0,)), ((), ())), preferred_element_type=F32)


def norm(rows, gain):
    factor = lax.rsqrt(jnp.mean(rows * rows, axis=-1, keepdims=True) + EPSILON)
    return (rows * factor * gain).astype(BF)


def spread_body(where_ref, x_ref, meta_ref, o_ref, sem):
    parity = where_ref[0]
    half = where_ref[1]
    for p in range(PAIRS):
        for t in range(LT):
            pltpu.make_async_copy(
                x_ref.at[
                    pl.ds(p * 64 + parity * 32, SEQ),
                    :,
                    pl.ds(pl.multiple_of(half * FH + t * 128, 128), 128),
                ],
                o_ref.at[:, p * LT + t],
                sem,
            ).start()
    pltpu.make_async_copy(meta_ref, o_ref.at[:, PAIRS * LT], sem).start()
    pltpu.make_async_copy(o_ref, o_ref, sem).wait()


def spread(where, x, meta):
    return pl.pallas_call(
        spread_body,
        out_shape=jax.ShapeDtypeStruct((SEQ, PAIRS * LT + 1, 8, 128), BF),
        in_specs=[SMEM, ANY, ANY],
        out_specs=ANY,
        scratch_shapes=[pltpu.SemaphoreType.DMA(())],
        compiler_params=PARAMS,
        name="spread",
    )(where, x, meta)


def pick_body(dest_ref, x_ref, o_ref, sem):
    def step(q, carry):
        first = dest_ref[q]

        @pl.when(first >= 0)
        def _():
            pltpu.make_async_copy(
                x_ref.at[q // PAIRS, pl.ds((q % PAIRS) * LT, LT)],
                o_ref.at[jnp.minimum(first // 2, SEQ * HEADS - 1)],
                sem,
            ).start()

        return carry

    lax.fori_loop(0, SEQ * PAIRS, step, 0, unroll=8)
    pltpu.make_async_copy(o_ref, o_ref, sem).wait()


def pick(dest, x):
    return pl.pallas_call(
        pick_body,
        out_shape=jax.ShapeDtypeStruct((SEQ * HEADS, LT, 8, 128), BF),
        in_specs=[SMEM, ANY],
        out_specs=ANY,
        scratch_shapes=[pltpu.SemaphoreType.DMA(())],
        compiler_params=PARAMS,
        name="pick",
    )(dest, x)


def encode_body(flag_ref, x_ref, gain_ref, wqkv_ref, wout_ref, o_ref, xs, ns, att):
    flip = flag_ref[0]
    bias = jnp.where(flag_ref[1] != 0, 0.0, -1e30).astype(F32)
    for b in range(2):
        base = pl.multiple_of(jnp.bitwise_xor(flip, b) * BLK, BLK)
        for c in range(2):
            for t in range(LT):
                xs[pl.ds(base, BLK), pl.ds(c * FH + t * 128, 128)] = (
                    x_ref[:, 2 * b + c, t].astype(F32).reshape(BLK, 128)
                )
    gain = gain_ref[...]
    for r in range(4):
        ns[pl.ds(r * 128, 128), :] = norm(xs[pl.ds(r * 128, 128), :], gain)
    for g in range(HEADS):
        y = mm(ns[:, :FH], wqkv_ref[0, g]) + mm(ns[:, FH:], wqkv_ref[1, g])
        q_all = (y[:, :FW] * HDIM**-0.5).astype(BF)
        k_all = y[:, FW : 2 * FW].astype(BF)
        v_all = y[:, 2 * FW :].astype(BF)
        for j in range(FW // HDIM):
            cut = slice(j * HDIM, (j + 1) * HDIM)
            k, v = k_all[:, cut], v_all[:, cut]
            for b in range(2):
                rows = slice(b * BLK, (b + 1) * BLK)
                other = slice((1 - b) * BLK, (2 - b) * BLK)
                q = q_all[rows, cut]
                s_own = mm_nt(q, k[rows])
                s_off = mm_nt(q, k[other]) + bias
                top = jnp.maximum(
                    jnp.max(s_own, axis=-1, keepdims=True), jnp.max(s_off, axis=-1, keepdims=True)
                )
                p_own = jnp.exp(s_own - top)
                p_off = jnp.exp(s_off - top)
                total = jnp.sum(p_own, axis=-1, keepdims=True) + jnp.sum(
                    p_off, axis=-1, keepdims=True
                )
                o = mm(p_own.astype(BF), v[rows]) + mm(p_off.astype(BF), v[other])
                att[rows, pl.ds((g * 3 + j) * HDIM, HDIM)] = (o / total).astype(BF)
    for c in range(2):
        mixed = mm(att[...], wout_ref[c].reshape(D, FH))
        o_ref[:, pl.ds(c * FH, FH)] = (xs[:, pl.ds(c * FH, FH)] + mixed).astype(BF)


def encode(flags, x, gain, wqkv, wout):
    return pl.pallas_call(
        encode_body,
        out_shape=jax.ShapeDtypeStruct((SPAN, D), BF),
        in_specs=[SMEM, VMEM, VMEM, VMEM, VMEM],
        out_specs=VMEM,
        scratch_shapes=[
            pltpu.VMEM((SPAN, D), F32),
            pltpu.VMEM((SPAN, D), BF),
            pltpu.VMEM((SPAN, D), BF),
        ],
        compiler_params=PARAMS,
        name="encode",
    )(flags, x, gain, wqkv, wout)


def make_fast_body(chunks, first, last):
    def body(*refs):
        rows_in = refs[:chunks]
        gain_ref, pick_ref, w_ref, rate_ref, init_ref = refs[chunks : chunks + 5]
        at = chunks + 5
        if not first:
            sum_ref = refs[at]
            at += 1
        q_refs = refs[at : at + chunks]
        e_refs = refs[at + chunks : at + 2 * chunks]
        g_ref = refs[at + 2 * chunks]
        gain = gain_ref[...]
        total_gu = total_d = None
        for x_ref, q_ref, e_ref in zip(rows_in, q_refs, e_refs):
            x = x_ref[...]
            n = norm(x.astype(F32), gain)
            e_ref[...] = mm(x, pick_ref[...]).astype(BF)
            q_ref[...] = mm(n, w_ref[0]).astype(BF)
            key = mm(n, w_ref[1]).astype(BF)
            value = mm(n, w_ref[2]).astype(BF).astype(F32)
            z = mm(n, rate_ref[...])
            soft = jnp.maximum(z, 0.0) + jnp.log1p(jnp.exp(-jnp.abs(z)))
            out_grad = (-(RATE_SCALE * VTOKENS**-0.5) * soft * value).astype(BF)
            gate = mm(key, init_ref[:, :FH])
            up = mm(key, init_ref[:, FH : 2 * FH])
            hidden_grad = mm(out_grad, init_ref[:, 2 * FH :])
            s = jax.nn.sigmoid(gate)
            silu = gate * s
            hidden = (silu * up).astype(BF)
            gate_grad = (hidden_grad * up * s * (1.0 + gate * (1.0 - s))).astype(BF)
            up_grad = (hidden_grad * silu).astype(BF)
            gu = mm_tn(key, jnp.concatenate([gate_grad, up_grad], axis=1))
            dn = mm_tn(out_grad, hidden)
            total_gu = gu if total_gu is None else total_gu + gu
            total_d = dn if total_d is None else total_d + dn
        if not first:
            total_gu = total_gu + sum_ref[:, : 2 * FH]
            total_d = total_d + sum_ref[:, 2 * FH :]
        if last:
            for t in range(6):
                g_ref[pl.ds(t * 24, 24)] = (
                    total_gu[:, t * 128 : (t + 1) * 128].astype(BF).reshape(24, 8, 128)
                )
            for t in range(3):
                g_ref[pl.ds((6 + t) * 24, 24)] = (
                    total_d[:, t * 128 : (t + 1) * 128].astype(BF).reshape(24, 8, 128)
                )
            g_ref[pl.ds(216, 8)] = jnp.zeros((8, 8, 128), BF)
        else:
            g_ref[:, : 2 * FH] = total_gu
            g_ref[:, 2 * FH :] = total_d

    return body


def fast(rows_in, shared, sums, last):
    chunks = len(rows_in)
    first = sums is None
    operands = (*rows_in, *shared) + (() if first else (sums,))
    sizes = [jax.ShapeDtypeStruct((r.shape[0], FW), BF) for r in rows_in]
    grad = (
        jax.ShapeDtypeStruct((GT, 8, 128), BF)
        if last
        else jax.ShapeDtypeStruct((FW, 3 * FH), F32)
    )
    outs = pl.pallas_call(
        make_fast_body(chunks, first, last),
        out_shape=(*sizes, *sizes, grad),
        in_specs=[VMEM] * len(operands),
        out_specs=[VMEM] * (2 * chunks + 1),
        compiler_params=PARAMS,
        name="fast_grad",
    )(*operands)
    return outs[:chunks], outs[chunks : 2 * chunks], outs[-1]


def sum_body(x_ref, o_ref):
    total = x_ref[0].astype(F32)
    for i in range(1, SEQ):
        total = total + x_ref[i].astype(F32)
    total = total.astype(BF)
    for i in range(SEQ):
        o_ref[i] = total


def sum_pieces(x):
    return pl.pallas_call(
        sum_body,
        out_shape=jax.ShapeDtypeStruct(x.shape, BF),
        in_specs=[VMEM],
        out_specs=VMEM,
        compiler_params=PARAMS,
        name="sum_pieces",
    )(x)


def renorm(updated, initial, axis):
    target = jnp.sqrt(jnp.sum(initial * initial, axis=axis, keepdims=True))
    return updated * target * lax.rsqrt(jnp.sum(updated * updated, axis=axis, keepdims=True) + EPSILON)


def make_apply_body(starts):
    def body(head_ref, g_ref, init_ref, *refs):
        n = len(starts)
        q_refs, e_refs = refs[:n], refs[n : 2 * n]
        o_ref, gs, ws = refs[2 * n :]
        for t in range(9):
            gs[:, pl.ds(t * 128, 128)] = g_ref[pl.ds(t * 24, 24)].astype(F32).reshape(FW, 128)
        for part, axis in ((0, 1), (1, 1), (2, 0)):
            cut = pl.ds(part * FH, FH)
            init = init_ref[:, cut]
            ws[:, cut] = renorm(init - gs[:, cut], init, axis).astype(BF)
        for (shift, offset), q_ref, e_ref in zip(starts, q_refs, e_refs):
            q = q_ref[...]
            gate = mm(q, ws[:, :FH])
            up = mm(q, ws[:, FH : 2 * FH])
            hidden = (gate * jax.nn.sigmoid(gate) * up).astype(BF)
            out = e_ref[...].astype(F32) + mm_nt(hidden, ws[:, 2 * FH :])
            base = pl.multiple_of(lax.rem(head_ref[0] + shift, HEADS) * SPAN + offset, BLK)
            o_ref[pl.ds(base, q.shape[0]), :] = out.astype(BF)

    return body


def apply(head, grads, init, queries, columns, starts):
    return pl.pallas_call(
        make_apply_body(starts),
        out_shape=jax.ShapeDtypeStruct((HEADS * SPAN, FW), BF),
        in_specs=[SMEM] + [VMEM] * (2 + 2 * len(queries)),
        out_specs=VMEM,
        scratch_shapes=[pltpu.VMEM((FW, 3 * FH), F32), pltpu.VMEM((FW, 3 * FH), BF)],
        compiler_params=PARAMS,
        name="apply_fast",
    )(head, grads, init, *queries, *columns)


def exchange(x, axes):
    return lax.all_to_all(x, axes, split_axis=0, concat_axis=0, tiled=True)


def shifted(x, by):
    return lax.ppermute(x, "head", [(i, (i + by) % HEADS) for i in range(HEADS)])


def on_device(
    patches,
    slot_image,
    slot_dest,
    enc_gain,
    w_qkv,
    w_out,
    fast_gain,
    w_fast,
    w_rate,
    fast_gate_up,
    fast_down,
):
    head = lax.axis_index("head")
    core = lax.axis_index("core")
    seq = lax.axis_index(SEQ_AXES)

    wide = jnp.concatenate([w_qkv[0], w_qkv[1], w_qkv[2]], axis=1)
    qkv_half = lax.dynamic_slice_in_dim(wide, core * FH, FH, 0)
    out_half = jnp.where(core == 0, w_out[:, :FH], w_out[:, FH:])
    wqkv = lax.all_gather(qkv_half, ("core", "head"), axis=0, tiled=False)
    wout = lax.all_gather(out_half, ("core", "head"), axis=0, tiled=False)
    wqkv = wqkv.reshape(2, HEADS, FH, 3 * FW)
    wout = wout.reshape(2, HEADS, FW, FH)

    where = jnp.stack([head // 2, head % 2]).astype(jnp.int32)
    ids = jnp.stack([slot_dest, slot_image]).astype(BF)
    tile = jnp.zeros((8, 128), BF).at[:2, :16].set(ids)
    meta = jnp.broadcast_to(tile[None], (SEQ, 8, 128))
    pieces = exchange(spread(where, patches.reshape(-1, 8, D), meta), SEQ_AXES)

    ids_all = pieces[:, PAIRS * LT, :2, :16].astype(jnp.int32)
    first = ids_all[:, 0, 0::2].reshape(-1)
    mine = exchange(pick(first, pieces), ALL_AXES)

    same = (ids_all[:, 1, 0::2] == ids_all[:, 1, 1::2]).reshape(-1)
    here = (first // 2 == seq * HEADS + head) & (first >= 0)
    flags = jnp.stack(
        [jnp.sum(jnp.where(here, first % 2, 0)), jnp.sum(jnp.where(here & same, 1, 0))]
    ).astype(jnp.int32)

    embedded = encode(
        flags, mine.reshape(SEQ, 4, LT, 8, 128), enc_gain.reshape(1, D), wqkv, wout
    )

    before = shifted(embedded, 1)
    after = shifted(embedded, -1)
    init = jnp.concatenate([fast_gate_up[0, 0], fast_gate_up[0, 1], fast_down[0].T], axis=1)
    pick_cols = (jnp.arange(D)[:, None] == head * FW + jnp.arange(FW)[None, :]).astype(BF)
    shared = (
        fast_gain.reshape(1, D),
        pick_cols,
        w_fast,
        jnp.broadcast_to(w_rate, (D, FW)),
        init.astype(BF),
    )
    q0, e0, sums = fast((embedded,), shared, None, False)
    far_low = shifted(after[:BLK], -1)
    far_high = shifted(before[BLK:], 1)
    q1, e1, sums = fast((before, after), shared, sums, False)
    q2, e2, grads = fast((far_low, far_high), shared, sums, True)

    summed = sum_pieces(exchange(grads, SEQ_AXES).reshape(SEQ, GT // SEQ, 8, 128))
    whole = exchange(summed, SEQ_AXES).reshape(GT, 8, 128)
    starts = ((0, 0), (3, 0), (1, 0), (2, 0), (2, BLK))
    return apply(
        head.astype(jnp.int32).reshape(1),
        whole,
        init,
        (*q0, *q1, *q2),
        (*e0, *e1, *e2),
        starts,
    )


def solution(mesh):
    fine = Mesh(mesh.devices.reshape(4, 4, 2, HEADS), ALL_AXES)
    in_specs = (
        P(SEQ_AXES, None),
        P(SEQ_AXES),
        P(SEQ_AXES),
        P(),
        P(None, None, "head"),
        P("head", None),
        P(),
        P(None, None, "head"),
        P(None, "head"),
        P("head", None, None, None),
        P("head", None, None),
    )
    return jax.shard_map(
        on_device, mesh=fine, in_specs=in_specs, out_specs=P(SEQ_AXES, "head"), check_vma=False
    )
```

profile of v0, /device:TPU:1, one launch (start us, length us, event | category | flops | bytes accessed | tf_op | source)
XLA Modules:
  0.0 218.0 jit_solution(9158664928500566297)
XLA Ops:
  6.5 1.2 slice_bitcast_fusion.2
  7.8 0.8 fusion.2
  8.6 0.0 all-gather.5.cloned.1.call-update
  8.6 0.1 pad_add_fusion.where_ref
  8.7 0.0 copy-done.33
  8.8 49.3 %spread.1 = bf16[32,25,8,128]{3,2,1,0:T(8,128)(2,1)} custom-call(s32[2]{0:T(128)S(1)} %pad_add_fusion.where_ref, bf16[512,8,768]{2,1,0:T(8,128)(2,1)} %bitcast.38, bf16[32,8,128]{2,1,0:T(8,128)(2,1)S(1)} %broadcast_in_dim.12.meta_ref), custom_call_target="tpu_custom_call" | custom-call | tf_op jit(solution)/shard_map/spread/pallas_call | solution.py:69
  58.1 0.0 copy-start.29
  58.1 9.6 %all-to-all-start = ((bf16[32,25,8,128]{3,2,1,0:T(8,128)(2,1)}), bf16[32,25,8,128]{3,2,1,0:T(8,128)(2,1)S(1)}, u32[]{:S(2)}, u32[]{:S(2)}) async-start(bf16[32,25,8,128]{3,2,1,0:T(8,128)(2,1)} %spread.1), calls=%async_computation | async-start | bytes 3276800 | tf_op jit(solution)/shard_map/all_to_all | solution.py:305
  67.7 0.0 all-gather.7.cloned.1.call-start
  67.7 0.7 slice_select_fusion
  68.4 0.0 all-gather.7.cloned.1.call-update
  68.4 22.6 %all-to-all-done.x_ref = bf16[32,25,8,128]{3,2,1,0:T(8,128)(2,1)S(1)} async-done(((bf16[32,25,8,128]{3,2,1,0:T(8,128)(2,1)}), bf16[32,25,8,128]{3,2,1,0:T(8,128)(2,1)S(1)}, u32[]{:S(2)}, u32[]{:S(2)}) %all-to-all-start) | async-done | bytes 1638432 | tf_op jit(solution)/shard_map/all_to_all | solution.py:305
  91.1 0.3 slice.60
  91.3 0.5 broadcast.106
  91.8 0.7 reduce.8
  92.5 0.1 reshape_squeeze.3.dest_ref
  92.6 0.0 copy-start.30
  92.6 4.5 %pick.1 = bf16[128,3,8,128]{3,2,1,0:T(8,128)(2,1)} custom-call(s32[256]{0:T(256)S(1)} %reshape_squeeze.3.dest_ref, bf16[32,25,8,128]{3,2,1,0:T(8,128)(2,1)S(1)} %all-to-all-done.x_ref), custom_call_target="tpu_custom_call" | custom-call | tf_op jit(solution)/shard_map/pick/pallas_call | solution.py:99
  97.2 5.9 %all-to-all-start.1 = ((bf16[128,3,8,128]{3,2,1,0:T(8,128)(2,1)}), bf16[128,3,8,128]{3,2,1,0:T(8,128)(2,1)S(1)}, u32[]{:S(2)}, u32[]{:S(2)}) async-start(bf16[128,3,8,128]{3,2,1,0:T(8,128)(2,1)} %pick.1), calls=%async_computation.1 | async-start | bytes 1572864 | tf_op jit(solution)/shard_map/all_to_all | solution.py:305
  103.1 0.3 slice.61
  103.4 0.3 slice.62
  103.7 0.1 compare_and_fusion
  103.8 0.7 fusion.6
  104.5 1.2 pad_add_fusion.1.flag_ref
  105.8 6.1 %copy.17 = bf16[3072,576]{1,0:T(8,128)(2,1)} copy(bf16[3072,576]{0,1:T(8,128)(2,1)} %all-gather.5.cloned.1.call-done) | data formatting | bytes 7077888 | tf_op jit(solution)/shard_map/all_gather | solution.py:332
  111.9 8.2 %all-to-all-done.1 = bf16[128,3,8,128]{3,2,1,0:T(8,128)(2,1)S(1)} async-done(((bf16[128,3,8,128]{3,2,1,0:T(8,128)(2,1)}), bf16[128,3,8,128]{3,2,1,0:T(8,128)(2,1)S(1)}, u32[]{:S(2)}, u32[]{:S(2)}) %all-to-all-start.1) | async-done | bytes 786464 | tf_op jit(solution)/shard_map/all_to_all | solution.py:305
  120.0 1.3 copy-done.2
  121.3 14.7 %encode.1.refs_0_ = bf16[512,768]{1,0:T(8,128)(2,1)S(1)} custom-call(s32[2]{0:T(128)S(1)} %pad_add_fusion.1.flag_ref, bf16[32,4,3,8,128]{4,3,2,1,0:T(8,128)(2,1)S(1)} %bitcast.33, f32[1,768]{1,0:T(1,128)S(1)} %reshape.81.gain_ref, bf16[2,4,384,576]{3,2,1,0:T(8,128)(2,1)} %bitcast.37, bf16[2,4,192,384]{3,2,1,0:T(8,128)(2,1)S(1)} %bitcast.36), custom_call_target="tpu_custom_call" | custom-call | tf_op jit(solution)/shard_map/encode/pallas_call | solution.py:153
  136.0 0.0 copy-start.31
  136.0 0.0 copy-start.32
  136.0 0.7 collective-permute-start
  136.7 0.9 collective-permute-start.2
  137.6 1.5 copy.20.refs_3_.refs_4_
  139.2 0.0 copy-start.27
  139.2 1.5 slice_bitcast_fusion.1
  140.7 14.3 %collective-permute-done.refs_1_ = bf16[512,768]{1,0:T(8,128)(2,1)S(1)} collective-permute-done((bf16[512,768]{1,0:T(8,128)(2,1)S(1)}, bf16[512,768]{1,0:T(8,128)(2,1)S(1)}, u32[]{:S(2)}, u32[]{:S(2)}) %collective-permute-start) | collective-permute-done | bytes 786464 | tf_op jit(solution)/shard_map/ppermute | solution.py:309
  155.0 1.1 collective-permute-start.1
  156.1 0.0 collective-permute-done.2.refs_0_
  156.2 0.5 collective-permute-start.3
  156.7 0.1 fusion.refs_2_.refs_3_
  156.9 0.1 fusion.13.refs_5_.refs_6_
  156.9 0.2 broadcast_in_dim.14.refs_4_.refs_5_
  157.1 2.3 %fast_grad.3 = (bf16[512,192]{1,0:T(8,128)(2,1)S(1)}, bf16[512,192]{1,0:T(8,128)(2,1)S(1)}, f32[192,1152]{1,0:T(8,128)S(1)}) custom-call(bf16[512,768]{1,0:T(8,128)(2,1)S(1)} %encode.1.refs_0_, f32[1,768]{1,0:T(1,128)S(1)} %reshape.84.refs_1_.refs_2_, bf16[768,192]{1,0:T(8,128)(2,1)S(1)} %fusion.refs_2_.refs_3_, ...), custom_call_target="tpu_custom_call" | custom-call | tf_op jit(solution)/shard_map/fast_grad/pallas_call | solution.py:233
  159.4 5.8 %fast_grad.4 = (bf16[512,192]{1,0:T(8,128)(2,1)S(1)}, bf16[512,192]{1,0:T(8,128)(2,1)S(1)}, bf16[512,192]{1,0:T(8,128)(2,1)S(1)}, bf16[512,192]{1,0:T(8,128)(2,1)S(1)}, f32[192,1152]{1,0:T(8,128)S(1)}) custom-call(bf16[512,768]{1,0:T(8,128)(2,1)S(1)} %collective-permute-done.2.refs_0_, bf16[512,768]{1,0:T(8,128)(2,1)S(1)} %collective-permute-done.refs_1_, ...), custom_call_target="tpu_custom_call" | custom-call | tf_op jit(solution)/shard_map/fast_grad/pallas_call | solution.py:233
  165.3 0.0 collective-permute-done.1.refs_0_
  165.3 0.6 collective-permute-done.3.refs_1_
  165.9 0.0 copy-done.1
  166.0 2.5 %fast_grad.5 = (bf16[256,192]{1,0:T(8,128)(2,1)S(1)}, bf16[256,192]{1,0:T(8,128)(2,1)S(1)}, bf16[256,192]{1,0:T(8,128)(2,1)S(1)}, bf16[256,192]{1,0:T(8,128)(2,1)S(1)}, bf16[224,8,128]{2,1,0:T(8,128)(2,1)S(1)}) custom-call(bf16[256,768]{1,0:T(8,128)(2,1)S(1)} %collective-permute-done.1.refs_0_, bf16[256,768]{1,0:T(8,128)(2,1)S(1)} %collective-permute-done.3.refs_1_, ...), custom_call_target="tpu_custom_call" | custom-call | tf_op jit(solution)/shard_map/fast_grad/pallas_call | solution.py:233
  168.5 0.0 copy-start.28
  168.5 18.2 %all_to_all.20 = bf16[224,8,128]{2,1,0:T(8,128)(2,1)S(1)} all-to-all(bf16[224,8,128]{2,1,0:T(8,128)(2,1)S(1)} %get-tuple-element.32), channel_id=1, replica_groups=mesh['x'=4,'z'=4,'core'=2,'head'=4] {'x','z','core'}, dimensions={0} | all-to-all | bytes 917504 | tf_op jit(solution)/shard_map/all_to_all | solution.py:305
  186.8 0.0 copy-done.15
  186.8 0.0 copy-done.19
  186.8 0.9 sum_pieces.1
  187.7 3.9 %all-to-all-start.3 = ((bf16[32,7,8,128]{3,2,1,0:T(8,128)(2,1)}), bf16[32,7,8,128]{3,2,1,0:T(8,128)(2,1)S(1)}, u32[]{:S(2)}, u32[]{:S(2)}) async-start(bf16[32,7,8,128]{3,2,1,0:T(8,128)(2,1)} %sum_pieces.1), calls=%async_computation.3 | async-start | bytes 917504 | tf_op jit(solution)/shard_map/all_to_all | solution.py:305
  191.6 0.1 pad_maximum_fusion.init_ref
  191.7 10.6 %all-to-all-done.3 = bf16[32,7,8,128]{3,2,1,0:T(8,128)(2,1)S(1)} async-done(((bf16[32,7,8,128]{3,2,1,0:T(8,128)(2,1)}), bf16[32,7,8,128]{3,2,1,0:T(8,128)(2,1)S(1)}, u32[]{:S(2)}, u32[]{:S(2)}) %all-to-all-start.3) | async-done | bytes 458784 | tf_op jit(solution)/shard_map/all_to_all | solution.py:305
  202.3 0.9 copy-done.12
  203.2 0.9 copy-done.14
  204.2 0.9 copy-done.16
  205.1 0.9 copy-done.18
  206.0 0.9 copy-done.20
  206.9 0.9 copy-done.22
  207.8 2.1 apply_fast.1
  209.9 1.2 copy.21
  (66 shorter events, 0.2 us)
Async XLA Ops:
  6.5 99.2 %all-gather.5.cloned.1.call-start = ((), (), s32[]{:S(2)}) async-start(), calls=%async_computation.4 | async-start | bytes 3981312 | tf_op jit(solution)/shard_map/all_gather | solution.py:332
  6.5 2.2 copy-start.33
  6.5 2.2 copy-start.34
  58.1 9.7 %copy-start.29 = (bf16[192,768]{1,0:T(8,128)(2,1)S(1)}, bf16[192,768]{1,0:T(8,128)(2,1)}, u32[]{:S(2)}) copy-start(bf16[192,768]{1,0:T(8,128)(2,1)} %param.18) | copy-start | bytes 884740
  58.1 33.0 %all-to-all-start = ((bf16[32,25,8,128]{3,2,1,0:T(8,128)(2,1)}), bf16[32,25,8,128]{3,2,1,0:T(8,128)(2,1)S(1)}, u32[]{:S(2)}, u32[]{:S(2)}) async-start(bf16[32,25,8,128]{3,2,1,0:T(8,128)(2,1)} %spread.1), calls=%async_computation | async-start | bytes 3276800 | tf_op jit(solution)/shard_map/all_to_all | solution.py:305
  67.7 44.2 %all-gather.7.cloned.1.call-start = ((), (), s32[]{:S(2)}) async-start(), calls=%async_computation.5 | async-start | bytes 1327104 | tf_op jit(solution)/shard_map/all_gather | solution.py:333
  92.6 10.5 %copy-start.30 = (f32[768]{0:T(1024)S(1)}, f32[768]{0:T(1024)}, u32[]{:S(2)}) copy-start(f32[768]{0:T(1024)} %param.16) | copy-start | bytes 9220
  97.2 22.9 %all-to-all-start.1 = ((bf16[128,3,8,128]{3,2,1,0:T(8,128)(2,1)}), bf16[128,3,8,128]{3,2,1,0:T(8,128)(2,1)S(1)}, u32[]{:S(2)}, u32[]{:S(2)}) async-start(bf16[128,3,8,128]{3,2,1,0:T(8,128)(2,1)} %pick.1), calls=%async_computation.1 | async-start | bytes 1572864 | tf_op jit(solution)/shard_map/all_to_all | solution.py:305
  120.0 1.3 copy-start.2
  136.0 3.1 %copy-start.31 = (f32[768]{0:T(1024)S(1)}, f32[768]{0:T(1024)}, u32[]{:S(2)}) copy-start(f32[768]{0:T(1024)} %param.19) | copy-start | bytes 9220
  136.0 3.1 %copy-start.32 = (bf16[768,1]{0,1:T(2,128)(2,1)S(1)}, bf16[768,1]{0,1:T(2,128)(2,1)}, u32[]{:S(2)}) copy-start(bf16[768,1]{0,1:T(2,128)(2,1)} %param.21) | copy-start | bytes 4612
  136.0 19.0 %collective-permute-start = (bf16[512,768]{1,0:T(8,128)(2,1)S(1)}, bf16[512,768]{1,0:T(8,128)(2,1)S(1)}, u32[]{:S(2)}, u32[]{:S(2)}) collective-permute-start(bf16[512,768]{1,0:T(8,128)(2,1)S(1)} %encode.1.refs_0_), channel_id=1, source_target_pairs={{0,3},{1,0},{2,1},{3,2},{4,7},{5,4},{6,5},{7,6},{8,11},{9,8},{10,9... | collective-permute-start | bytes 2359304 | tf_op jit(solution)/shard_map/ppermute | solution.py:309
  136.7 19.4 %collective-permute-start.2 = (bf16[512,768]{1,0:T(8,128)(2,1)S(1)}, bf16[512,768]{1,0:T(8,128)(2,1)S(1)}, u32[]{:S(2)}, u32[]{:S(2)}) collective-permute-start(bf16[512,768]{1,0:T(8,128)(2,1)S(1)} %encode.1.refs_0_), channel_id=1, source_target_pairs={{0,1},{1,2},{2,3},{3,0},{4,5},{5,6},{6,7},{7,4},{8,9},{9,10},{10,1... | collective-permute-start | bytes 2359304 | tf_op jit(solution)/shard_map/ppermute | solution.py:309
  139.1 18.0 %copy-start = (bf16[3,768,192]{2,1,0:T(8,128)(2,1)}, bf16[3,768,192]{2,1,0:T(8,128)(2,1)S(1)}, u32[]{:S(2)}) copy-start(bf16[3,768,192]{2,1,0:T(8,128)(2,1)S(1)} %copy.20.refs_3_.refs_4_) | copy-start | bytes 2654212
  139.2 17.7 %copy-start.27 = (f32[1,384,192]{1,2,0:T(8,128)S(1)}, f32[1,384,192]{1,2,0:T(8,128)}, u32[]{:S(2)}) copy-start(f32[1,384,192]{1,2,0:T(8,128)} %param.23) | copy-start | bytes 884740
  140.7 16.1 %copy-start.23 = (f32[192,384]{1,0:T(8,128)}, f32[192,384]{1,0:T(8,128)S(1)}, u32[]{:S(2)}) copy-start(f32[192,384]{1,0:T(8,128)S(1)} %get-tuple-element.50) | copy-start | bytes 884740
  140.7 16.1 %copy-start.25 = (f32[192,384]{1,0:T(8,128)}, f32[192,384]{1,0:T(8,128)S(1)}, u32[]{:S(2)}) copy-start(f32[192,384]{1,0:T(8,128)S(1)} %get-tuple-element.51) | copy-start | bytes 884740
  155.0 10.3 %collective-permute-start.1 = (bf16[256,768]{1,0:T(8,128)(2,1)S(1)}, bf16[256,768]{1,0:T(8,128)(2,1)S(1)}, u32[]{:S(2)}, u32[]{:S(2)}) collective-permute-start(bf16[256,768]{1,0:T(8,128)(2,1)S(1)} %slice.73), channel_id=1, source_target_pairs={{0,3},{1,0},{2,1},{3,2},{4,7},{5,4},{6,5},{7,6},{8,11},{9,8},{10,9... | collective-permute-start | bytes 1179656 | tf_op jit(solution)/shard_map/ppermute | solution.py:309
  156.2 9.8 %collective-permute-start.3 = (bf16[256,768]{1,0:T(8,128)(2,1)S(1)}, bf16[256,768]{1,0:T(8,128)(2,1)S(1)}, u32[]{:S(2)}, u32[]{:S(2)}) collective-permute-start(bf16[256,768]{1,0:T(8,128)(2,1)S(1)} %slice.74), channel_id=1, source_target_pairs={{0,1},{1,2},{2,3},{3,0},{4,5},{5,6},{6,7},{7,4},{8,9},{9,10},{10,1... | collective-permute-start | bytes 1179656 | tf_op jit(solution)/shard_map/ppermute | solution.py:309
  159.4 5.8 %copy-start.3 = (bf16[512,192]{1,0:T(8,128)(2,1)}, bf16[512,192]{1,0:T(8,128)(2,1)S(1)}, u32[]{:S(2)}) copy-start(bf16[512,192]{1,0:T(8,128)(2,1)S(1)} %get-tuple-element.33.refs_0_) | copy-start | bytes 589828
  159.4 5.8 %copy-start.5 = (bf16[512,192]{1,0:T(8,128)(2,1)}, bf16[512,192]{1,0:T(8,128)(2,1)S(1)}, u32[]{:S(2)}) copy-start(bf16[512,192]{1,0:T(8,128)(2,1)S(1)} %get-tuple-element.38.refs_5_) | copy-start | bytes 589828
  159.4 6.5 %copy-start.1 = (bf16[3,768,192]{2,1,0:T(8,128)(2,1)S(1)}, bf16[3,768,192]{2,1,0:T(8,128)(2,1)}, u32[]{:S(2)}) copy-start(bf16[3,768,192]{2,1,0:T(8,128)(2,1)} %copy-done) | copy-start | bytes 2654212
  165.3 3.2 %copy-start.7 = (bf16[512,192]{1,0:T(8,128)(2,1)}, bf16[512,192]{1,0:T(8,128)(2,1)S(1)}, u32[]{:S(2)}) copy-start(bf16[512,192]{1,0:T(8,128)(2,1)S(1)} %get-tuple-element.34.refs_1_) | copy-start | bytes 589828
  165.3 3.2 %copy-start.9 = (bf16[512,192]{1,0:T(8,128)(2,1)}, bf16[512,192]{1,0:T(8,128)(2,1)S(1)}, u32[]{:S(2)}) copy-start(bf16[512,192]{1,0:T(8,128)(2,1)S(1)} %get-tuple-element.35.refs_2_) | copy-start | bytes 589828
  165.3 3.2 %copy-start.11 = (bf16[512,192]{1,0:T(8,128)(2,1)}, bf16[512,192]{1,0:T(8,128)(2,1)S(1)}, u32[]{:S(2)}) copy-start(bf16[512,192]{1,0:T(8,128)(2,1)S(1)} %get-tuple-element.39.refs_6_) | copy-start | bytes 589828
  165.3 3.2 %copy-start.13 = (bf16[512,192]{1,0:T(8,128)(2,1)}, bf16[512,192]{1,0:T(8,128)(2,1)S(1)}, u32[]{:S(2)}) copy-start(bf16[512,192]{1,0:T(8,128)(2,1)S(1)} %get-tuple-element.40.refs_7_) | copy-start | bytes 589828
  168.4 18.3 %copy-start.15 = (bf16[256,192]{1,0:T(8,128)(2,1)}, bf16[256,192]{1,0:T(8,128)(2,1)S(1)}, u32[]{:S(2)}) copy-start(bf16[256,192]{1,0:T(8,128)(2,1)S(1)} %get-tuple-element.36.refs_3_) | copy-start | bytes 294916
  168.5 18.3 %copy-start.17 = (bf16[256,192]{1,0:T(8,128)(2,1)}, bf16[256,192]{1,0:T(8,128)(2,1)S(1)}, u32[]{:S(2)}) copy-start(bf16[256,192]{1,0:T(8,128)(2,1)S(1)} %get-tuple-element.37.refs_4_) | copy-start | bytes 294916
  168.5 18.3 %copy-start.19 = (bf16[256,192]{1,0:T(8,128)(2,1)}, bf16[256,192]{1,0:T(8,128)(2,1)S(1)}, u32[]{:S(2)}) copy-start(bf16[256,192]{1,0:T(8,128)(2,1)S(1)} %get-tuple-element.41.refs_8_) | copy-start | bytes 294916
  168.5 18.3 %copy-start.21 = (bf16[256,192]{1,0:T(8,128)(2,1)}, bf16[256,192]{1,0:T(8,128)(2,1)S(1)}, u32[]{:S(2)}) copy-start(bf16[256,192]{1,0:T(8,128)(2,1)S(1)} %get-tuple-element.42.refs_9_) | copy-start | bytes 294916
  168.5 23.1 %copy-start.24 = (f32[192,384]{1,0:T(8,128)S(1)}, f32[192,384]{1,0:T(8,128)}, u32[]{:S(2)}) copy-start(f32[192,384]{1,0:T(8,128)} %copy-done.23) | copy-start | bytes 884740
  168.5 23.1 %copy-start.26 = (f32[192,384]{1,0:T(8,128)S(1)}, f32[192,384]{1,0:T(8,128)}, u32[]{:S(2)}) copy-start(f32[192,384]{1,0:T(8,128)} %copy-done.25) | copy-start | bytes 884740
  168.5 23.1 %copy-start.28 = (f32[1,384,192]{1,2,0:T(8,128)S(1)}, f32[1,384,192]{1,2,0:T(8,128)}, u32[]{:S(2)}) copy-start(f32[1,384,192]{1,2,0:T(8,128)} %param.23) | copy-start | bytes 884740
  186.8 15.5 %copy-start.4 = (bf16[512,192]{1,0:T(8,128)(2,1)S(1)}, bf16[512,192]{1,0:T(8,128)(2,1)}, u32[]{:S(2)}) copy-start(bf16[512,192]{1,0:T(8,128)(2,1)} %copy-done.3) | copy-start | bytes 589828
  186.8 15.5 %copy-start.6 = (bf16[512,192]{1,0:T(8,128)(2,1)S(1)}, bf16[512,192]{1,0:T(8,128)(2,1)}, u32[]{:S(2)}) copy-start(bf16[512,192]{1,0:T(8,128)(2,1)} %copy-done.5) | copy-start | bytes 589828
  186.8 15.4 %copy-start.8 = (bf16[512,192]{1,0:T(8,128)(2,1)S(1)}, bf16[512,192]{1,0:T(8,128)(2,1)}, u32[]{:S(2)}) copy-start(bf16[512,192]{1,0:T(8,128)(2,1)} %copy-done.7) | copy-start | bytes 589828
  186.8 15.4 %copy-start.10 = (bf16[512,192]{1,0:T(8,128)(2,1)S(1)}, bf16[512,192]{1,0:T(8,128)(2,1)}, u32[]{:S(2)}) copy-start(bf16[512,192]{1,0:T(8,128)(2,1)} %copy-done.9) | copy-start | bytes 589828
  187.7 14.6 %all-to-all-start.3 = ((bf16[32,7,8,128]{3,2,1,0:T(8,128)(2,1)}), bf16[32,7,8,128]{3,2,1,0:T(8,128)(2,1)S(1)}, u32[]{:S(2)}, u32[]{:S(2)}) async-start(bf16[32,7,8,128]{3,2,1,0:T(8,128)(2,1)} %sum_pieces.1), calls=%async_computation.3 | async-start | bytes 917504 | tf_op jit(solution)/shard_map/all_to_all | solution.py:305
  202.3 1.0 copy-start.12
  203.2 0.9 copy-start.14
  204.2 0.9 copy-start.16
  205.1 0.9 copy-start.18
  206.0 0.9 copy-start.20
  206.9 0.9 copy-start.22
Sparse Core Ops, SparseCore 0:
  9.1 32.9 all-gather.4
  70.2 25.2 all-gather.6
where the time goes:
time: 219 us; the launch traced here: 218 us
  Pallas kernels  82.1 us (37%)
  waiting for transfers between devices  56.3 us (26%)
  starting transfers between devices  22.6 us (10%)
  local copies, waits for them, and re-layouts  20.1 us (9%)
  blocking collectives  18.2 us (8%)
  between operations  14 us (6%)
  other arithmetic  4.68 us (2%)
    pallas_call x1, Pallas kernels, spread(): pl.pallas_call(spread_body, out_shape=jax.ShapeDtypeStruct((SEQ, PAIRS *...  49.3 us
    all_to_all x3, waiting for transfers between devices, exchange(): return lax.all_to_all(x, axes, split_axis=0, concat_axis=0, tiled=True)  41.3 us
    all_to_all x3, starting transfers between devices, exchange(): return lax.all_to_all(x, axes, split_axis=0, concat_axis=0, tiled=True)  19.4 us
    all_to_all x1, blocking collectives, exchange(): return lax.all_to_all(x, axes, split_axis=0, concat_axis=0, tiled=True)  18.2 us
    ppermute x4, waiting for transfers between devices, shifted(): lax.ppermute(x, 'head', [(i, (i + by) % HEADS) for i in range(HEADS)])  14.9 us
    pallas_call x1, Pallas kernels, encode(): pl.pallas_call(encode_body, out_shape=jax.ShapeDtypeStruct((SPAN, D), BF)...  14.7 us
    pallas_call x3, Pallas kernels, fast(): pl.pallas_call(make_fast_body(chunks, first, last), out_shape=(*sizes, *s...  10.6 us
    unnamed x71, local copies, waits for them, and re-layouts  8.42 us
  transfers between devices with their start and end apart: 9, of which 5 were waited for; matrix products, arithmetic and copies ran while one was open for 7% of the time, Pallas kernels for 28%

commit v1 on v0

v1 whole, which is shorter than its diff:
```python
import jax
import jax.numpy as jnp
from jax import lax
from jax.experimental import pallas as pl
from jax.experimental.pallas import tpu as pltpu
from jax.sharding import Mesh, PartitionSpec as P

D = 768
HDIM = 64
BLK = 256
SPAN = 512
FW = 192
FH = 384
SEQ = 32
HEADS = 4
PAIRS = 8
LT = 3
GT = 224
EPSILON = 1e-06
LOG2E = 1.4426950408889634
RATE_SCALE = 0.1
VTOKENS = 65536
BF = jnp.bfloat16
F32 = jnp.float32
SEQ_AXES = ("x", "z", "core")
ALL_AXES = ("x", "z", "core", "head")
PARAMS = pltpu.CompilerParams(vmem_limit_bytes=48 << 20)

ANY = pl.BlockSpec(memory_space=pl.ANY)
SMEM = pl.BlockSpec(memory_space=pltpu.SMEM)
VMEM = pl.BlockSpec(memory_space=pltpu.VMEM)


def mm(a, b):
    return jnp.dot(a, b, preferred_element_type=F32)


def mm_nt(a, b):
    return lax.dot_general(a, b, (((1,), (1,)), ((), ())), preferred_element_type=F32)


def mm_tn(a, b):
    return lax.dot_general(a, b, (((0,), (0,)), ((), ())), preferred_element_type=F32)


def norm(rows, gain):
    factor = lax.rsqrt(jnp.mean(rows * rows, axis=-1, keepdims=True) + EPSILON)
    return (rows * factor * gain).astype(BF)


def spread_body(where_ref, x_ref, meta_ref, o_ref, buf, sems):
    parity = where_ref[0]
    half = where_ref[1]
    copies = []
    for p in range(PAIRS):
        copies.append(
            pltpu.make_async_copy(
                x_ref.at[
                    pl.ds(p * 64 + parity * 32, SEQ), :, pl.ds(pl.multiple_of(half * FH, 128), FH)
                ],
                buf.at[p],
                sems.at[p],
            )
        )
        copies[p].start()
    o_ref[:, PAIRS * LT] = jnp.broadcast_to(meta_ref[...][None], (SEQ, 8, 128))
    for p in range(PAIRS):
        copies[p].wait()
        for t in range(LT):
            o_ref[:, p * LT + t] = buf[p, :, :, t * 128 : (t + 1) * 128]


def spread(where, x, meta):
    return pl.pallas_call(
        spread_body,
        out_shape=jax.ShapeDtypeStruct((SEQ, PAIRS * LT + 1, 8, 128), BF),
        in_specs=[SMEM, ANY, VMEM],
        out_specs=VMEM,
        scratch_shapes=[
            pltpu.VMEM((PAIRS, SEQ, 8, FH), BF),
            pltpu.SemaphoreType.DMA((PAIRS,)),
        ],
        compiler_params=PARAMS,
        name="spread",
    )(where, x, meta)


def pick_body(dest_ref, x_ref, o_ref, sem):
    def step(q, carry):
        first = dest_ref[q]

        @pl.when(first >= 0)
        def _():
            pltpu.make_async_copy(
                x_ref.at[q // PAIRS, pl.ds((q % PAIRS) * LT, LT)],
                o_ref.at[jnp.minimum(first // 2, SEQ * HEADS - 1)],
                sem,
            ).start()

        return carry

    lax.fori_loop(0, SEQ * PAIRS, step, 0, unroll=8)
    pltpu.make_async_copy(o_ref, o_ref, sem).wait()


def pick(dest, x):
    return pl.pallas_call(
        pick_body,
        out_shape=jax.ShapeDtypeStruct((SEQ * HEADS, LT, 8, 128), BF),
        in_specs=[SMEM, ANY],
        out_specs=ANY,
        scratch_shapes=[pltpu.SemaphoreType.DMA(())],
        compiler_params=PARAMS,
        name="pick",
    )(dest, x)


def attend(block, bias, q_ref, k_ref, v_ref, att):
    own = slice(block * BLK, (block + 1) * BLK)
    row = lax.broadcasted_iota(jnp.int32, (FW, BLK), 0)
    ones = jnp.ones((16, SPAN), BF)
    for g in range(HEADS):
        k = k_ref[g]
        q = q_ref[g]
        for j in range(FW // HDIM):
            mine = (row >= j * HDIM) & (row < (j + 1) * HDIM)
            s = mm(k, jnp.where(mine, q, jnp.zeros_like(q)))
            parts = [s[:BLK], s[BLK:]]
            parts[1 - block] = parts[1 - block] + bias
            top = jnp.max(jnp.maximum(parts[0], parts[1]), axis=0, keepdims=True)
            p = jnp.concatenate([jnp.exp2(x - top).astype(BF) for x in parts], axis=0)
            v = jnp.concatenate([v_ref[g, j * HDIM : (j + 1) * HDIM], ones], axis=0)
            o = mm(v, p)
            o = (o[:HDIM] * (1.0 / o[HDIM : HDIM + 1])).astype(BF)
            for at in range(0, HDIM, 32):
                half, rest = divmod(j * HDIM + at, 96)
                att[pl.ds(half * FH + g * 96 + rest, 32), :] = o[at : at + 32]


def encode_first_body(
    flag_ref, x_ref, gain_ref, w_ref, o_ref, q_ref, k_ref, v_ref, rest_ref, xs, ns, att, q0, ws, sems
):
    copies = [
        pltpu.make_async_copy(w_ref.at[:, g], ws.at[g], sems.at[g]) for g in range(HEADS)
    ]
    for c in copies:
        c.start()
    flip = flag_ref[0]
    bias = jnp.where(flag_ref[1] != 0, 0.0, -1e30).astype(F32)
    for b in range(2):
        base = pl.multiple_of(jnp.bitwise_xor(flip, b) * BLK, BLK)
        for c in range(2):
            for t in range(LT):
                xs[pl.ds(base, BLK), pl.ds(c * FH + t * 128, 128)] = (
                    x_ref[:, 2 * b + c, t].astype(F32).reshape(BLK, 128)
                )
    gain = gain_ref[...]
    for r in range(8):
        ns[pl.ds(r * 64, 64), :] = norm(xs[pl.ds(r * 64, 64), :], gain)
    rest_ref[...] = xs[BLK:, :].astype(BF)
    n = ns[...]
    scale = HDIM**-0.5 * LOG2E
    for g in range(HEADS):
        copies[g].wait()
        w = ws[g, :, : 3 * 96].reshape(3 * FW, D)
        q = (mm_nt(w[:FW], n) * scale).astype(BF)
        q0[g] = q[:, :BLK]
        q_ref[g] = q[:, BLK:]
        k_ref[g] = mm_nt(n, w[FW : 2 * FW]).astype(BF)
        v_ref[g] = mm_nt(w[2 * FW :], n).astype(BF)
    attend(0, bias, q0, k_ref, v_ref, att)
    out = xs[:BLK, :]
    for c in range(2):
        for g in range(HEADS):
            out = out + mm_tn(att[pl.ds(c * FH + g * 96, 96), :], ws[g, c, 3 * 96 :])
    o_ref[...] = out.astype(BF)


def encode_first(flags, x, gain, w):
    return pl.pallas_call(
        encode_first_body,
        out_shape=(
            jax.ShapeDtypeStruct((BLK, D), BF),
            jax.ShapeDtypeStruct((HEADS, FW, BLK), BF),
            jax.ShapeDtypeStruct((HEADS, SPAN, FW), BF),
            jax.ShapeDtypeStruct((HEADS, FW, SPAN), BF),
            jax.ShapeDtypeStruct((BLK, D), BF),
        ),
        in_specs=[SMEM, VMEM, VMEM, ANY],
        out_specs=[VMEM] * 5,
        scratch_shapes=[
            pltpu.VMEM((SPAN, D), F32),
            pltpu.VMEM((SPAN, D), BF),
            pltpu.VMEM((D, BLK), BF),
            pltpu.VMEM((HEADS, FW, BLK), BF),
            pltpu.VMEM((HEADS, 2, FH, D), BF),
            pltpu.SemaphoreType.DMA((HEADS,)),
        ],
        compiler_params=PARAMS,
        name="encode_first",
    )(flags, x, gain, w)


def encode_second_body(flag_ref, q_ref, k_ref, v_ref, rest_ref, w_ref, o_ref, att, ws, sem):
    copy = pltpu.make_async_copy(w_ref.at[:, :, pl.ds(3 * 96, 96)], ws, sem)
    copy.start()
    bias = jnp.where(flag_ref[1] != 0, 0.0, -1e30).astype(F32)
    attend(1, bias, q_ref, k_ref, v_ref, att)
    copy.wait()
    mixed = mm_tn(att[...], ws[...].reshape(D, D))
    o_ref[...] = (rest_ref[...].astype(F32) + mixed).astype(BF)


def encode_second(flags, q, k, v, rest, w):
    return pl.pallas_call(
        encode_second_body,
        out_shape=jax.ShapeDtypeStruct((BLK, D), BF),
        in_specs=[SMEM, VMEM, VMEM, VMEM, VMEM, ANY],
        out_specs=VMEM,
        scratch_shapes=[
            pltpu.VMEM((D, BLK), BF),
            pltpu.VMEM((2, HEADS, 96, D), BF),
            pltpu.SemaphoreType.DMA(()),
        ],
        compiler_params=PARAMS,
        name="encode_second",
    )(flags, q, k, v, rest, w)


def make_fast_body(chunks, first, last):
    def body(*refs):
        rows_in = refs[:chunks]
        gain_ref, w_ref, rate_ref, gu_ref, down_ref = refs[chunks : chunks + 5]
        sum_ref = None if first else refs[chunks + 5]
        g_ref = refs[-1]
        gain = gain_ref[...]
        gate_up = [gu_ref[i].astype(BF) for i in range(2)]
        down = down_ref[...].astype(BF)
        sums = None
        for x_ref in rows_in:
            n = norm(x_ref[...].astype(F32), gain)
            key = mm_nt(n, w_ref[1]).astype(BF)
            value = mm_nt(n, w_ref[2]).astype(BF).astype(F32)
            z = mm_nt(n, rate_ref[...])
            soft = jnp.maximum(z, 0.0) + jnp.log1p(jnp.exp(-jnp.abs(z)))
            out_grad = (-(RATE_SCALE * VTOKENS**-0.5) * soft * value).astype(BF)
            gate = mm(key, gate_up[0])
            up = mm(key, gate_up[1])
            hidden_grad = mm(out_grad, down)
            s = jax.nn.sigmoid(gate)
            silu = gate * s
            hidden = (silu * up).astype(BF)
            gate_grad = (hidden_grad * up * s * (1.0 + gate * (1.0 - s))).astype(BF)
            up_grad = (hidden_grad * silu).astype(BF)
            parts = [mm_tn(key, gate_grad), mm_tn(key, up_grad), mm_tn(out_grad, hidden)]
            sums = parts if sums is None else [a + b for a, b in zip(sums, parts)]
        for i, total in enumerate(sums):
            if not first:
                total = total + sum_ref[i]
            if last:
                for t in range(LT):
                    g_ref[pl.ds((i * LT + t) * 24, 24)] = (
                        total[:, t * 128 : (t + 1) * 128].astype(BF).reshape(24, 8, 128)
                    )
            else:
                g_ref[i] = total
        if last:
            g_ref[pl.ds(216, 8)] = jnp.zeros((8, 8, 128), BF)

    return body


def fast(rows_in, shared, sums, last):
    first = sums is None
    operands = (*rows_in, *shared) + (() if first else (sums,))
    return pl.pallas_call(
        make_fast_body(len(rows_in), first, last),
        out_shape=(
            jax.ShapeDtypeStruct((GT, 8, 128), BF)
            if last
            else jax.ShapeDtypeStruct((3, FW, FH), F32)
        ),
        in_specs=[VMEM] * len(operands),
        out_specs=VMEM,
        compiler_params=PARAMS,
        name="fast_grad",
    )(*operands)


def make_query_body(starts):
    def body(head_ref, gain_ref, w_ref, pick_ref, *refs):
        rows_in, (q_ref, e_ref) = refs[: len(starts)], refs[len(starts) :]
        gain = gain_ref[...]
        for (shift, offset), x_ref in zip(starts, rows_in):
            x = x_ref[...]
            base = pl.multiple_of(lax.rem(head_ref[0] + shift, HEADS) * SPAN + offset, BLK)
            n = norm(x.astype(F32), gain)
            q_ref[pl.ds(base, BLK), :] = mm_nt(n, w_ref[0]).astype(BF)
            e_ref[:, pl.ds(base, BLK)] = mm_nt(pick_ref[...], x).astype(BF)

    return body


def queries(head, gain, w, pick_cols, rows_in, starts):
    return pl.pallas_call(
        make_query_body(starts),
        out_shape=(
            jax.ShapeDtypeStruct((HEADS * SPAN, FW), BF),
            jax.ShapeDtypeStruct((FW, HEADS * SPAN), BF),
        ),
        in_specs=[SMEM] + [VMEM] * (3 + len(rows_in)),
        out_specs=[VMEM] * 2,
        compiler_params=PARAMS,
        name="fast_query",
    )(head, gain, w, pick_cols, *rows_in)


def sum_body(x_ref, o_ref):
    total = x_ref[0].astype(F32)
    for i in range(1, SEQ):
        total = total + x_ref[i].astype(F32)
    total = total.astype(BF)
    for i in range(SEQ):
        o_ref[i] = total


def sum_pieces(x):
    return pl.pallas_call(
        sum_body,
        out_shape=jax.ShapeDtypeStruct(x.shape, BF),
        in_specs=[VMEM],
        out_specs=VMEM,
        compiler_params=PARAMS,
        name="sum_pieces",
    )(x)


def renorm(updated, initial, axis):
    target = jnp.sqrt(jnp.sum(initial * initial, axis=axis, keepdims=True))
    return updated * target * lax.rsqrt(jnp.sum(updated * updated, axis=axis, keepdims=True) + EPSILON)


def apply_body(g_ref, gu_ref, down_ref, q_ref, e_ref, o_ref, gs, ws):
    for i in range(3):
        for t in range(LT):
            gs[i, :, pl.ds(t * 128, 128)] = (
                g_ref[pl.ds((i * LT + t) * 24, 24)].astype(F32).reshape(FW, 128)
            )
        init = down_ref[...] if i == 2 else gu_ref[i]
        ws[i] = renorm(init - gs[i], init, 0 if i == 2 else 1).astype(BF)
    for c in range(HEADS):
        rows = slice(c * SPAN, (c + 1) * SPAN)
        q = q_ref[rows, :]
        gate = mm(q, ws[0])
        hidden = (gate * jax.nn.sigmoid(gate) * mm(q, ws[1])).astype(BF)
        o_ref[:, rows] = (e_ref[:, rows].astype(F32) + mm_nt(ws[2], hidden)).astype(BF)


def apply(grads, gate_up, down, q, e):
    return pl.pallas_call(
        apply_body,
        out_shape=jax.ShapeDtypeStruct((FW, HEADS * SPAN), BF),
        in_specs=[VMEM] * 5,
        out_specs=VMEM,
        scratch_shapes=[pltpu.VMEM((3, FW, FH), F32), pltpu.VMEM((3, FW, FH), BF)],
        compiler_params=PARAMS,
        name="apply_fast",
    )(grads, gate_up, down, q, e)


def exchange(x, axes):
    return lax.all_to_all(x, axes, split_axis=0, concat_axis=0, tiled=True)


def shifted(x, by):
    return lax.ppermute(x, "head", [(i, (i + by) % HEADS) for i in range(HEADS)])


def on_device(
    patches,
    slot_image,
    slot_dest,
    enc_gain,
    w_qkv,
    w_out,
    fast_gain,
    w_fast,
    w_rate,
    fast_gate_up,
    fast_down,
):
    head = lax.axis_index("head")
    core = lax.axis_index("core")
    seq = lax.axis_index(SEQ_AXES)

    qkv_rows = jnp.transpose(w_qkv, (0, 2, 1)).reshape(3 * FW, D)
    half = jnp.concatenate(
        [
            lax.dynamic_slice_in_dim(qkv_rows, core * 3 * 96, 3 * 96, 0),
            lax.dynamic_slice_in_dim(w_out, core * 96, 96, 0),
        ],
        axis=0,
    )
    weights = lax.all_gather(half, ("core", "head"), axis=0, tiled=False)
    weights = weights.reshape(2, HEADS, FH, D)

    where = jnp.stack([head // 2, head % 2]).astype(jnp.int32)
    ids = jnp.stack([slot_dest, slot_image]).astype(BF)
    tile = jnp.zeros((8, 128), BF).at[:2, :16].set(ids)
    pieces = exchange(spread(where, patches.reshape(-1, 8, D), tile), SEQ_AXES)

    ids_all = pieces[:, PAIRS * LT, :2, :16].astype(jnp.int32)
    first = ids_all[:, 0, 0::2].reshape(-1)
    mine = exchange(pick(first, pieces), ALL_AXES)

    same = (ids_all[:, 1, 0::2] == ids_all[:, 1, 1::2]).reshape(-1)
    here = (first // 2 == seq * HEADS + head) & (first >= 0)
    flags = jnp.stack(
        [jnp.sum(jnp.where(here, first % 2, 0)), jnp.sum(jnp.where(here & same, 1, 0))]
    ).astype(jnp.int32)

    own_0, q1, k, v, rest = encode_first(
        flags, mine.reshape(SEQ, 4, LT, 8, 128), enc_gain.reshape(1, D), weights
    )
    before_0, after_0 = shifted(own_0, 1), shifted(own_0, -1)
    own_1 = encode_second(flags, q1, k, v, rest, weights)
    before_1, after_1 = shifted(own_1, 1), shifted(own_1, -1)
    far_0 = shifted(before_0, 1)
    far_1 = shifted(after_1, -1)

    gain = fast_gain.reshape(1, D)
    w = jnp.transpose(w_fast, (0, 2, 1))
    gate_up = fast_gate_up[0]
    down = fast_down[0].T
    shared = (gain, w, jnp.broadcast_to(w_rate.T, (FW, D)), gate_up, down)
    sums = fast((own_0, own_1), shared, None, False)
    sums = fast((before_0, after_0), shared, sums, False)
    sums = fast((before_1, after_1), shared, sums, False)
    grads = fast((far_0, far_1), shared, sums, True)

    pick_cols = (head * FW + jnp.arange(FW)[:, None] == jnp.arange(D)[None, :]).astype(BF)
    starts = ((0, 0), (0, BLK), (3, 0), (3, BLK), (1, 0), (1, BLK), (2, 0), (2, BLK))
    chunks = (own_0, own_1, before_0, before_1, after_0, after_1, far_0, far_1)
    q, e = queries(head.astype(jnp.int32).reshape(1), gain, w, pick_cols, chunks, starts)

    summed = sum_pieces(exchange(grads, SEQ_AXES).reshape(SEQ, GT // SEQ, 8, 128))
    whole = exchange(summed, SEQ_AXES).reshape(GT, 8, 128)
    return apply(whole, gate_up, down, q, e).T


def solution(mesh):
    fine = Mesh(mesh.devices.reshape(4, 4, 2, HEADS), ALL_AXES)
    in_specs = (
        P(SEQ_AXES, None),
        P(SEQ_AXES),
        P(SEQ_AXES),
        P(),
        P(None, None, "head"),
        P("head", None),
        P(),
        P(None, None, "head"),
        P(None, "head"),
        P("head", None, None, None),
        P("head", None, None),
    )
    return jax.shard_map(
        on_device, mesh=fine, in_specs=in_specs, out_specs=P(SEQ_AXES, "head"), check_vma=False
    )
```

time: 219 us -> 169 us (0.77)
  Pallas kernels: 82.1 us -> 46.1 us
  blocking collectives: 18.2 us -> 48.8 us
  waiting for transfers between devices: 56.3 us -> 32.1 us
  local copies, waits for them, and re-layouts: 20.1 us -> 8.75 us
  starting transfers between devices: 22.6 us -> 14.4 us
    pallas_call x1, Pallas kernels: 49.3 us -> 2.09 us  [spread(): pl.pallas_call(spread_body, out_shape=jax.ShapeDtypeStruct((SEQ, PAIRS *...]
    all_to_all x1 -> x2, blocking collectives: 18.2 us -> 48.8 us  [exchange(): return lax.all_to_all(x, axes, split_axis=0, concat_axis=0, tiled=True)]
    all_to_all x3 -> x2, waiting for transfers between devices: 41.3 us -> 18.2 us  [exchange(): return lax.all_to_all(x, axes, split_axis=0, concat_axis=0, tiled=True)]
    pallas_call x5 -> x8, Pallas kernels: 27.4 us -> 38.6 us  [the longest x4 13 us: fast(): pl.pallas_call(make_fast_body(len(rows_in), first, last), out_shape=jax.S...]
    all_to_all x3 -> x2, starting transfers between devices: 19.4 us -> 9.63 us  [exchange(): return lax.all_to_all(x, axes, split_axis=0, concat_axis=0, tiled=True)]
    all_gather x1 -> x0, local copies, waits for them, and re-layouts: 6.09 us -> none  [on_device(): wqkv = lax.all_gather(qkv_half, ('core', 'head'), axis=0, tiled=False)]
    squeeze x2 -> x0, local copies, waits for them, and re-layouts: 2.72 us -> none  [the longest x1 1.5 us: on_device(): fast_gate_up[0, 0]]
    unnamed x71 -> x30, local copies, waits for them, and re-layouts: 8.42 us -> 6.4 us
  transfers between devices with their start and end apart: 9 -> 9, of which waited for: 5 -> 6; matrix products, arithmetic and copies ran while one was open for 7% -> 3% of each run, Pallas kernels for 28% -> 12%
where the time goes in v1:
time: 169 us; the launch traced here: 168 us
  blocking collectives  48.8 us (29%)
  Pallas kernels  46.1 us (27%)
  waiting for transfers between devices  32.1 us (19%)
  starting transfers between devices  14.4 us (9%)
  between operations  13.7 us (8%)
  local copies, waits for them, and re-layouts  8.75 us (5%)
  other arithmetic  3.91 us (2%)
    all_to_all x2, blocking collectives, exchange(): return lax.all_to_all(x, axes, split_axis=0, concat_axis=0, tiled=True)  48.8 us
    all_to_all x2, waiting for transfers between devices, exchange(): return lax.all_to_all(x, axes, split_axis=0, concat_axis=0, tiled=True)  18.2 us
    ppermute x6, waiting for transfers between devices, shifted(): lax.ppermute(x, 'head', [(i, (i + by) % HEADS) for i in range(HEADS)])  13.8 us
    pallas_call x4, Pallas kernels, fast(): pl.pallas_call(make_fast_body(len(rows_in), first, last), out_shape=jax.S...  13 us
    pallas_call x1, Pallas kernels, encode_first(): pl.pallas_call(encode_first_body, out_shape=(jax.ShapeDtypeStruct((BLK, D...  12.1 us
    all_to_all x2, starting transfers between devices, exchange(): return lax.all_to_all(x, axes, split_axis=0, concat_axis=0, tiled=True)  9.63 us
    pallas_call x1, Pallas kernels, encode_second(): pl.pallas_call(encode_second_body, out_shape=jax.ShapeDtypeStruct((BLK, D...  6.76 us
    unnamed x30, local copies, waits for them, and re-layouts  6.4 us
  transfers between devices with their start and end apart: 9, of which 6 were waited for; matrix products, arithmetic and copies ran while one was open for 3% of the time, Pallas kernels for 12%

profile of v1, /device:TPU:1, one launch (start us, length us, event | category | flops | bytes accessed | tf_op | source)
XLA Modules:
  0.0 167.8 jit_solution(9295283879480278988)
XLA Ops:
  6.5 0.0 copy-start
  6.5 0.0 all-gather.3.cloned.1.call-start
  6.6 1.1 copy-done
  7.7 0.9 constant_dynamic-slice_fusion
  8.7 0.9 pad_maximum_fusion
  9.5 0.0 all-gather.3.cloned.1.call-update
  9.6 0.1 pad_add_fusion.where_ref
  9.7 0.0 copy-done.13
  9.7 0.0 copy-done.14
  9.7 2.1 %spread.1 = bf16[32,25,8,128]{3,2,1,0:T(8,128)(2,1)S(1)} custom-call(s32[2]{0:T(128)S(1)} %pad_add_fusion.where_ref, bf16[512,8,768]{2,1,0:T(8,128)(2,1)} %bitcast.49, bf16[8,128]{1,0:T(8,128)(2,1)S(1)} %fusion.10.meta_ref), custom_call_target="tpu_custom_call" | custom-call | tf_op jit(solution)/shard_map/spread/pallas_call | solution.py:74
  11.8 32.7 %all_to_all.20.x_ref = bf16[32,25,8,128]{3,2,1,0:T(8,128)(2,1)S(1)} all-to-all(bf16[32,25,8,128]{3,2,1,0:T(8,128)(2,1)S(1)} %spread.1), channel_id=1, replica_groups=mesh['x'=4,'z'=4,'core'=2,'head'=4] {'x','z','core'}, dimensions={0} | all-to-all | bytes 3276800 | tf_op jit(solution)/shard_map/all_to_all | solution.py:372
  44.6 0.3 slice.33
  44.8 0.5 broadcast.101
  45.3 0.7 reduce.8
  46.0 0.1 reshape_squeeze.3.dest_ref
  46.1 0.0 copy-start.10
  46.1 4.5 %pick.1 = bf16[128,3,8,128]{3,2,1,0:T(8,128)(2,1)} custom-call(s32[256]{0:T(256)S(1)} %reshape_squeeze.3.dest_ref, bf16[32,25,8,128]{3,2,1,0:T(8,128)(2,1)S(1)} %all_to_all.20.x_ref), custom_call_target="tpu_custom_call" | custom-call | tf_op jit(solution)/shard_map/pick/pallas_call | solution.py:107
  50.7 5.7 %all-to-all-start.1 = ((bf16[128,3,8,128]{3,2,1,0:T(8,128)(2,1)}), bf16[128,3,8,128]{3,2,1,0:T(8,128)(2,1)S(1)}, u32[]{:S(2)}, u32[]{:S(2)}) async-start(bf16[128,3,8,128]{3,2,1,0:T(8,128)(2,1)} %pick.1), calls=%async_computation.1 | async-start | bytes 1572864 | tf_op jit(solution)/shard_map/all_to_all | solution.py:372
  56.4 0.0 copy-done.10
  56.4 0.3 slice.34
  56.7 0.3 slice.35
  57.0 0.1 compare_and_fusion
  57.1 0.7 fusion.4
  57.8 1.3 pad_add_fusion.1.flag_ref
  59.1 14.3 %all-to-all-done.1 = bf16[128,3,8,128]{3,2,1,0:T(8,128)(2,1)S(1)} async-done(((bf16[128,3,8,128]{3,2,1,0:T(8,128)(2,1)}), bf16[128,3,8,128]{3,2,1,0:T(8,128)(2,1)S(1)}, u32[]{:S(2)}, u32[]{:S(2)}) %all-to-all-start.1) | async-done | bytes 786464 | tf_op jit(solution)/shard_map/all_to_all | solution.py:372
  73.4 12.1 %encode_first.1 = (bf16[256,768]{1,0:T(8,128)(2,1)}, bf16[4,192,256]{2,1,0:T(8,128)(2,1)S(1)}, bf16[4,512,192]{2,1,0:T(8,128)(2,1)S(1)}, bf16[4,192,512]{2,1,0:T(8,128)(2,1)S(1)}, bf16[256,768]{1,0:T(8,128)(2,1)S(1)}) custom-call(s32[2]{0:T(128)S(1)} %pad_add_fusion.1.flag_ref, bf16[32,4,3,8,128]{4,3,2,1,0:T(8,128)(2,1)S(1)} %bitcast.44, ...), custom_call_target="tpu_custom_call" | custom-call | tf_op jit(solution)/shard_map/encode_first/pallas_call | solution.py:180
  85.4 0.0 copy-start.11
  85.4 0.0 copy-start.12
  85.4 0.0 copy-start.1
  85.4 0.0 copy-start.2
  85.5 0.0 copy-start.3
  85.5 6.8 %encode_second.1.refs_1_ = bf16[256,768]{1,0:T(8,128)(2,1)S(1)} custom-call(s32[2]{0:T(128)S(1)} %pad_add_fusion.1.flag_ref, bf16[4,192,256]{2,1,0:T(8,128)(2,1)S(1)} %get-tuple-element.25.q_ref, bf16[4,512,192]{2,1,0:T(8,128)(2,1)S(1)} %get-tuple-element.26.k_ref, bf16[4,192,512]{2,1,0:T(8,128)(2,1)S(1)} %get-tuple-element.27.v_ref, ...), custom_call_target="tpu_custom_call" | custom-call | tf_op jit(solution)/shard_map/encode_second/pallas_call | solution.py:215
  92.2 0.7 collective-permute-start.2
  92.9 0.9 collective-permute-start
  93.8 1.8 %collective-permute-start.5 = (bf16[256,768]{1,0:T(8,128)(2,1)}, bf16[256,768]{1,0:T(8,128)(2,1)}, u32[]{:S(2)}, u32[]{:S(2)}) collective-permute-start(bf16[256,768]{1,0:T(8,128)(2,1)} %get-tuple-element.24.refs_0_), channel_id=1, source_target_pairs={{0,3},{1,0},{2,1},{3,2},{4,7},{5,4},{6,5},{7,6},{8,11},{9,8},{10,9... | collective-permute-start | bytes 1179656 | tf_op jit(solution)/shard_map/ppermute | solution.py:376
  95.6 0.0 collective-permute-start.4
  95.6 7.3 %collective-permute-done.2.refs_1_.refs_5_ = bf16[256,768]{1,0:T(8,128)(2,1)S(1)} collective-permute-done((bf16[256,768]{1,0:T(8,128)(2,1)S(1)}, bf16[256,768]{1,0:T(8,128)(2,1)S(1)}, u32[]{:S(2)}, u32[]{:S(2)}) %collective-permute-start.2) | collective-permute-done | bytes 393248 | tf_op jit(solution)/shard_map/ppermute | solution.py:376
  102.9 0.9 collective-permute-start.3
  103.8 0.0 collective-permute-done.refs_0_.refs_2_
  103.8 0.5 collective-permute-start.1
  104.4 0.0 copy-done.11
  104.4 0.0 copy-done.12
  104.4 0.0 copy-done.1
  104.5 3.2 %fast_grad.4.refs_7_ = f32[3,192,384]{2,1,0:T(8,128)S(1)} custom-call(bf16[256,768]{1,0:T(8,128)(2,1)} %get-tuple-element.24.refs_0_, bf16[256,768]{1,0:T(8,128)(2,1)S(1)} %encode_second.1.refs_1_, f32[1,768]{1,0:T(1,128)S(1)} %reshape.74.refs_2_.gain_ref, bf16[3,192,768]{2,1,0:T(8,128)(2,1)S(1)} %bitcast.29, bf16[192,768]{1,0:T(8,128)(2,1)S(1)} %broadcast_in_dim.11.refs_4_, ...), custom_call_target="tpu_custom_call" | custom-call | tf_op jit(solution)/shard_map/fast_grad/pallas_call | solution.py:276
  107.7 3.7 %collective-permute-done.5.refs_1_.refs_4_ = bf16[256,768]{1,0:T(8,128)(2,1)} collective-permute-done((bf16[256,768]{1,0:T(8,128)(2,1)}, bf16[256,768]{1,0:T(8,128)(2,1)}, u32[]{:S(2)}, u32[]{:S(2)}) %collective-permute-start.5) | collective-permute-done | bytes 393248 | tf_op jit(solution)/shard_map/ppermute | solution.py:376
  111.3 3.3 %fast_grad.5.refs_7_ = f32[3,192,384]{2,1,0:T(8,128)S(1)} custom-call(bf16[256,768]{1,0:T(8,128)(2,1)} %collective-permute-done.refs_0_.refs_2_, bf16[256,768]{1,0:T(8,128)(2,1)} %collective-permute-done.5.refs_1_.refs_4_, f32[1,768]{1,0:T(1,128)S(1)} %reshape.74.refs_2_.gain_ref, bf16[3,192,768]{2,1,0:T(8,128)(2,1)S(1)} %bitcast.30, ...), custom_call_target="tpu_custom_call" | custom-call | tf_op jit(solution)/shard_map/fast_grad/pallas_call | solution.py:276
  114.6 0.0 collective-permute-done.4.refs_0_.refs_3_
  114.6 3.2 %fast_grad.6.refs_7_ = f32[3,192,384]{2,1,0:T(8,128)S(1)} custom-call(bf16[256,768]{1,0:T(8,128)(2,1)} %collective-permute-done.4.refs_0_.refs_3_, bf16[256,768]{1,0:T(8,128)(2,1)S(1)} %collective-permute-done.2.refs_1_.refs_5_, f32[1,768]{1,0:T(1,128)S(1)} %reshape.74.refs_2_.gain_ref, bf16[3,192,768]{2,1,0:T(8,128)(2,1)S(1)} %bitcast.31, ...), custom_call_target="tpu_custom_call" | custom-call | tf_op jit(solution)/shard_map/fast_grad/pallas_call | solution.py:276
  117.9 1.9 %collective-permute-done.3.refs_1_.refs_7_ = bf16[256,768]{1,0:T(8,128)(2,1)} collective-permute-done((bf16[256,768]{1,0:T(8,128)(2,1)S(1)}, bf16[256,768]{1,0:T(8,128)(2,1)}, u32[]{:S(2)}, u32[]{:S(2)}) %collective-permute-start.3) | collective-permute-done | bytes 393248 | tf_op jit(solution)/shard_map/ppermute | solution.py:376
  119.7 0.9 collective-permute-done.1.refs_0_.refs_6_
  120.7 3.3 %fast_grad.7 = bf16[224,8,128]{2,1,0:T(8,128)(2,1)S(1)} custom-call(bf16[256,768]{1,0:T(8,128)(2,1)} %collective-permute-done.1.refs_0_.refs_6_, bf16[256,768]{1,0:T(8,128)(2,1)} %collective-permute-done.3.refs_1_.refs_7_, f32[1,768]{1,0:T(1,128)S(1)} %reshape.74.refs_2_.gain_ref, bf16[3,192,768]{2,1,0:T(8,128)(2,1)S(1)} %bitcast.32, ...), custom_call_target="tpu_custom_call" | custom-call | tf_op jit(solution)/shard_map/fast_grad/pallas_call | solution.py:276
  124.0 16.0 %all_to_all.21 = bf16[224,8,128]{2,1,0:T(8,128)(2,1)S(1)} all-to-all(bf16[224,8,128]{2,1,0:T(8,128)(2,1)S(1)} %fast_grad.7), channel_id=1, replica_groups=mesh['x'=4,'z'=4,'core'=2,'head'=4] {'x','z','core'}, dimensions={0} | all-to-all | bytes 917504 | tf_op jit(solution)/shard_map/all_to_all | solution.py:372
  140.1 0.9 sum_pieces.1
  140.9 3.9 %all-to-all-start.3 = ((bf16[32,7,8,128]{3,2,1,0:T(8,128)(2,1)}), bf16[32,7,8,128]{3,2,1,0:T(8,128)(2,1)S(1)}, u32[]{:S(2)}, u32[]{:S(2)}) async-start(bf16[32,7,8,128]{3,2,1,0:T(8,128)(2,1)} %sum_pieces.1), calls=%async_computation.3 | async-start | bytes 917504 | tf_op jit(solution)/shard_map/all_to_all | solution.py:372
  144.8 0.1 fusion.pick_ref
  145.0 0.0 copy-start.5
  145.0 1.0 copy-done.5
  146.0 3.7 %fast_query.1 = (bf16[2048,192]{1,0:T(8,128)(2,1)S(1)}, bf16[192,2048]{1,0:T(8,128)(2,1)S(1)}) custom-call(s32[1]{0:T(128)} %bitcast.20.head_ref, f32[1,768]{1,0:T(1,128)S(1)} %reshape.74.refs_2_.gain_ref, bf16[3,192,768]{2,1,0:T(8,128)(2,1)S(1)} %bitcast.33, bf16[192,768]{1,0:T(8,128)(2,1)S(1)} %fusion.pick_ref, ...), custom_call_target="tpu_custom_call" | custom-call | tf_op jit(solution)/shard_map/fast_query/pallas_call | solution.py:305
  149.7 1.0 copy-done.6
  150.6 0.9 copy-done.8
  151.5 4.0 %all-to-all-done.3 = bf16[32,7,8,128]{3,2,1,0:T(8,128)(2,1)S(1)} async-done(((bf16[32,7,8,128]{3,2,1,0:T(8,128)(2,1)}), bf16[32,7,8,128]{3,2,1,0:T(8,128)(2,1)S(1)}, u32[]{:S(2)}, u32[]{:S(2)}) %all-to-all-start.3) | async-done | bytes 458784 | tf_op jit(solution)/shard_map/all_to_all | solution.py:372
  155.5 1.2 copy-done.7
  156.7 1.1 copy-done.9
  157.8 3.1 %apply_fast.1 = bf16[192,2048]{1,0:T(8,128)(2,1)} custom-call(bf16[224,8,128]{2,1,0:T(8,128)(2,1)S(1)} %bitcast.46, f32[2,192,384]{2,1,0:T(8,128)S(1)} %bitcast.38, f32[192,384]{1,0:T(8,128)S(1)} %bitcast.43, bf16[2048,192]{1,0:T(8,128)(2,1)S(1)} %copy-done.7, bf16[192,2048]{1,0:T(8,128)(2,1)S(1)} %copy-done.9), custom_call_target="tpu_custom_call" | custom-call | tf_op jit(solution)/shard_map/apply_fast/pallas_call | solution.py:360
  (20 shorter events, 0.1 us)
Async XLA Ops:
  6.5 1.2 copy-start
  6.5 3.1 %copy-start.13 = (s32[16]{0:T(128)S(1)}, s32[16]{0:T(128)}, u32[]{:S(2)}) copy-start(s32[16]{0:T(128)} %param.14) | copy-start | bytes 196
  6.5 3.1 %copy-start.14 = (s32[16]{0:T(128)S(1)}, s32[16]{0:T(128)}, u32[]{:S(2)}) copy-start(s32[16]{0:T(128)} %param.15) | copy-start | bytes 196
  6.5 66.8 %all-gather.3.cloned.1.call-start = ((), (), s32[]{:S(2)}) async-start(), calls=%async_computation.4 | async-start | bytes 5308416 | tf_op jit(solution)/shard_map/all_gather | solution.py:404
  46.1 10.3 %copy-start.10 = (f32[768]{0:T(1024)S(1)}, f32[768]{0:T(1024)}, u32[]{:S(2)}) copy-start(f32[768]{0:T(1024)} %param.16) | copy-start | bytes 9220
  50.7 22.7 %all-to-all-start.1 = ((bf16[128,3,8,128]{3,2,1,0:T(8,128)(2,1)}), bf16[128,3,8,128]{3,2,1,0:T(8,128)(2,1)S(1)}, u32[]{:S(2)}, u32[]{:S(2)}) async-start(bf16[128,3,8,128]{3,2,1,0:T(8,128)(2,1)} %pick.1), calls=%async_computation.1 | async-start | bytes 1572864 | tf_op jit(solution)/shard_map/all_to_all | solution.py:372
  85.4 19.0 %copy-start.11 = (f32[768]{0:T(1024)S(1)}, f32[768]{0:T(1024)}, u32[]{:S(2)}) copy-start(f32[768]{0:T(1024)} %param.19) | copy-start | bytes 9220
  85.4 18.9 %copy-start.12 = (bf16[768,1]{0,1:T(2,128)(2,1)S(1)}, bf16[768,1]{0,1:T(2,128)(2,1)}, u32[]{:S(2)}) copy-start(bf16[768,1]{0,1:T(2,128)(2,1)} %param.21) | copy-start | bytes 4612
  85.4 19.0 %copy-start.1 = (bf16[3,768,192]{1,2,0:T(8,128)(2,1)S(1)}, bf16[3,768,192]{1,2,0:T(8,128)(2,1)}, u32[]{:S(2)}) copy-start(bf16[3,768,192]{1,2,0:T(8,128)(2,1)} %param.20) | copy-start | bytes 2654212
  85.4 19.0 %copy-start.2 = (f32[1,2,192,384]{3,2,1,0:T(8,128)S(1)}, f32[1,2,192,384]{3,2,1,0:T(8,128)}, u32[]{:S(2)}) copy-start(f32[1,2,192,384]{3,2,1,0:T(8,128)} %param.22) | copy-start | bytes 1769476
  85.5 19.0 %copy-start.3 = (f32[1,384,192]{1,2,0:T(8,128)S(1)}, f32[1,384,192]{1,2,0:T(8,128)}, u32[]{:S(2)}) copy-start(f32[1,384,192]{1,2,0:T(8,128)} %param.23) | copy-start | bytes 884740
  92.2 10.6 %collective-permute-start.2 = (bf16[256,768]{1,0:T(8,128)(2,1)S(1)}, bf16[256,768]{1,0:T(8,128)(2,1)S(1)}, u32[]{:S(2)}, u32[]{:S(2)}) collective-permute-start(bf16[256,768]{1,0:T(8,128)(2,1)S(1)} %encode_second.1.refs_1_), channel_id=1, source_target_pairs={{0,3},{1,0},{2,1},{3,2},{4,7},{5,4},{6,5},{7,6},{8,11},{9,8},{10,9... | collective-permute-start | bytes 1179656 | tf_op jit(solution)/shard_map/ppermute | solution.py:376
  92.9 10.9 %collective-permute-start = (bf16[256,768]{1,0:T(8,128)(2,1)}, bf16[256,768]{1,0:T(8,128)(2,1)}, u32[]{:S(2)}, u32[]{:S(2)}) collective-permute-start(bf16[256,768]{1,0:T(8,128)(2,1)} %get-tuple-element.24.refs_0_), channel_id=1, source_target_pairs={{0,1},{1,2},{2,3},{3,0},{4,5},{5,6},{6,7},{7,4},{8,9},{9,10},{10,1... | collective-permute-start | bytes 1179656 | tf_op jit(solution)/shard_map/ppermute | solution.py:376
  93.8 17.5 %collective-permute-start.5 = (bf16[256,768]{1,0:T(8,128)(2,1)}, bf16[256,768]{1,0:T(8,128)(2,1)}, u32[]{:S(2)}, u32[]{:S(2)}) collective-permute-start(bf16[256,768]{1,0:T(8,128)(2,1)} %get-tuple-element.24.refs_0_), channel_id=1, source_target_pairs={{0,3},{1,0},{2,1},{3,2},{4,7},{5,4},{6,5},{7,6},{8,11},{9,8},{10,9... | collective-permute-start | bytes 1179656 | tf_op jit(solution)/shard_map/ppermute | solution.py:376
  95.6 19.1 %collective-permute-start.4 = (bf16[256,768]{1,0:T(8,128)(2,1)S(1)}, bf16[256,768]{1,0:T(8,128)(2,1)}, u32[]{:S(2)}, u32[]{:S(2)}) collective-permute-start(bf16[256,768]{1,0:T(8,128)(2,1)S(1)} %encode_second.1.refs_1_), channel_id=1, source_target_pairs={{0,1},{1,2},{2,3},{3,0},{4,5},{5,6},{6,7},{7,4},{8,9},{9,10},{10,1... | collective-permute-start | bytes 1179656 | tf_op jit(solution)/shard_map/ppermute | solution.py:376
  102.9 11.8 %copy-start.4 = (bf16[256,768]{1,0:T(8,128)(2,1)}, bf16[256,768]{1,0:T(8,128)(2,1)S(1)}, u32[]{:S(2)}) copy-start(bf16[256,768]{1,0:T(8,128)(2,1)S(1)} %collective-permute-done.2.refs_1_.refs_5_) | copy-start | bytes 1179652
  102.9 16.9 %collective-permute-start.3 = (bf16[256,768]{1,0:T(8,128)(2,1)S(1)}, bf16[256,768]{1,0:T(8,128)(2,1)}, u32[]{:S(2)}, u32[]{:S(2)}) collective-permute-start(bf16[256,768]{1,0:T(8,128)(2,1)S(1)} %collective-permute-done.2.refs_1_.refs_5_), channel_id=1, source_target_pairs={{0,3},{1,0},{2,1},{3,2},{4,7},{5,4},{6,5},{7,6},{8,11},{9,8},{10,9... | collective-permute-start | bytes 1179656 | tf_op jit(solution)/shard_map/ppermute | solution.py:376
  103.8 16.9 %collective-permute-start.1 = (bf16[256,768]{1,0:T(8,128)(2,1)}, bf16[256,768]{1,0:T(8,128)(2,1)}, u32[]{:S(2)}, u32[]{:S(2)}) collective-permute-start(bf16[256,768]{1,0:T(8,128)(2,1)} %collective-permute-done.refs_0_.refs_2_), channel_id=1, source_target_pairs={{0,1},{1,2},{2,3},{3,0},{4,5},{5,6},{6,7},{7,4},{8,9},{9,10},{10,1... | collective-permute-start | bytes 1179656 | tf_op jit(solution)/shard_map/ppermute | solution.py:376
  140.9 14.6 %all-to-all-start.3 = ((bf16[32,7,8,128]{3,2,1,0:T(8,128)(2,1)}), bf16[32,7,8,128]{3,2,1,0:T(8,128)(2,1)S(1)}, u32[]{:S(2)}, u32[]{:S(2)}) async-start(bf16[32,7,8,128]{3,2,1,0:T(8,128)(2,1)} %sum_pieces.1), calls=%async_computation.3 | async-start | bytes 917504 | tf_op jit(solution)/shard_map/all_to_all | solution.py:372
  145.0 1.0 copy-start.5
  149.6 1.0 copy-start.6
  150.6 0.9 copy-start.8
  155.5 1.2 copy-start.7
  156.7 1.1 copy-start.9
Sparse Core Ops, SparseCore 0:
  9.7 37.9 all-gather.2

commit v2 on v1

v2 whole, which is shorter than its diff:
```python
import jax
import jax.numpy as jnp
from jax import lax
from jax.experimental import pallas as pl
from jax.experimental.pallas import tpu as pltpu
from jax.sharding import Mesh, PartitionSpec as P

D = 768
HDIM = 64
BLK = 256
SPAN = 512
FW = 192
FH = 384
SEQ = 32
HEADS = 4
PAIRS = 8
LT = 3
GT = 224
WROWS = 688
KV_AT = 384
RATE_AT = 576
Q_AT = 592
EPSILON = 1e-06
LOG2E = 1.4426950408889634
RATE_SCALE = 0.1
VTOKENS = 65536
BF = jnp.bfloat16
F32 = jnp.float32
SEQ_AXES = ("x", "z", "core")
ALL_AXES = ("x", "z", "core", "head")


def params(mib):
    return pltpu.CompilerParams(vmem_limit_bytes=mib << 20)


def cost(us):
    return pl.CostEstimate(flops=0, bytes_accessed=int(us * 3.6e6), transcendentals=0)


ANY = pl.BlockSpec(memory_space=pltpu.HBM)
SMEM = pl.BlockSpec(memory_space=pltpu.SMEM)
VMEM = pl.BlockSpec(memory_space=pltpu.VMEM)


def in_hbm(x):
    return pltpu.with_memory_space_constraint(x, pltpu.HBM)


def mm(a, b):
    return jnp.dot(a, b, preferred_element_type=F32)


def mm_nt(a, b):
    return lax.dot_general(a, b, (((1,), (1,)), ((), ())), preferred_element_type=F32)


def mm_tn(a, b):
    return lax.dot_general(a, b, (((0,), (0,)), ((), ())), preferred_element_type=F32)


def norm(rows, gain):
    factor = lax.rsqrt(jnp.mean(rows * rows, axis=-1, keepdims=True) + EPSILON)
    return (rows * factor * gain).astype(BF)


def spread_body(
    at_ref, x_ref, meta_ref, qkv_ref, out_ref, fast_ref, rate_ref,
    o_ref, w_ref, buf, sems, wsems,
):
    head = at_ref[1]
    core = at_ref[2]
    parity = head // 2
    half = head % 2
    copies = []
    for p in range(PAIRS):
        copies.append(
            pltpu.make_async_copy(
                x_ref.at[
                    pl.ds(p * 64 + parity * 32, SEQ), :, pl.ds(pl.multiple_of(half * FH, 128), FH)
                ],
                buf.at[p],
                sems.at[p],
            )
        )
        copies[p].start()

    def rows(ref, start, count):
        return ref.at[pl.ds(pl.multiple_of(start, 32), count)]

    moves = [
        (rows(qkv_ref, core * 288, 288), w_ref.at[pl.ds(0, 288)]),
        (rows(out_ref, core * 96, 96), w_ref.at[pl.ds(288, 96)]),
        (rows(fast_ref, FW + core * FW, FW), w_ref.at[pl.ds(KV_AT, FW)]),
        (rate_ref, w_ref.at[pl.ds(RATE_AT, 16)]),
        (rows(fast_ref, core * 96, 96), w_ref.at[pl.ds(Q_AT, 96)]),
    ]
    moves = [pltpu.make_async_copy(*m, wsems.at[i]) for i, m in enumerate(moves)]
    for m in moves:
        m.start()
    o_ref[:, PAIRS * LT] = jnp.broadcast_to(meta_ref[...][None], (SEQ, 8, 128))
    for p in range(PAIRS):
        copies[p].wait()
        for t in range(LT):
            o_ref[:, p * LT + t] = buf[p, :, :, t * 128 : (t + 1) * 128]
    for m in moves:
        m.wait()


def spread(at, x, meta, *weights):
    return pl.pallas_call(
        spread_body,
        out_shape=(
            jax.ShapeDtypeStruct((SEQ, PAIRS * LT + 1, 8, 128), BF),
            jax.ShapeDtypeStruct((WROWS, D), BF),
        ),
        in_specs=[SMEM, ANY, VMEM] + [ANY] * 4,
        out_specs=[VMEM] * 2,
        scratch_shapes=[
            pltpu.VMEM((PAIRS, SEQ, 8, FH), BF),
            pltpu.SemaphoreType.DMA((PAIRS,)),
            pltpu.SemaphoreType.DMA((5,)),
        ],
        compiler_params=params(12),
        cost_estimate=cost(3),
        name="spread",
    )(at, in_hbm(x), meta, *[in_hbm(w) for w in weights])


def pick_body(at_ref, x_ref, o_ref, flag_ref, ids, table, source, sem):
    ids[...] = x_ref[:, PAIRS * LT, 0, :].astype(F32).astype(jnp.int32)
    copy = pltpu.make_async_copy(ids, table, sem)
    copy.start()
    copy.wait()

    def note(q, carry):
        first = table[q // PAIRS, (q % PAIRS) * 2]
        pair = jnp.minimum(first // 2, SEQ * HEADS - 1)
        source[jnp.where(first >= 0, pair, SEQ * HEADS)] = q
        return carry

    lax.fori_loop(0, SEQ * PAIRS, note, 0, unroll=8)

    def move(m, carry):
        q = source[m]
        o_ref[m] = x_ref[q // PAIRS, pl.ds((q % PAIRS) * LT, LT)]
        return carry

    lax.fori_loop(0, SEQ * HEADS, move, 0, unroll=8)
    q = source[at_ref[0]]
    slot = (q % PAIRS) * 2
    flag_ref[0] = table[q // PAIRS, slot] % 2
    flag_ref[1] = jnp.where(
        table[q // PAIRS, 16 + slot] == table[q // PAIRS, 17 + slot], 1, 0
    )
    flag_ref[2] = at_ref[1]


def pick(at, x):
    return pl.pallas_call(
        pick_body,
        out_shape=(
            jax.ShapeDtypeStruct((SEQ * HEADS, LT, 8, 128), BF),
            jax.ShapeDtypeStruct((3,), jnp.int32),
        ),
        in_specs=[SMEM, VMEM],
        out_specs=[VMEM, SMEM],
        scratch_shapes=[
            pltpu.VMEM((SEQ, 128), jnp.int32),
            pltpu.SMEM((SEQ, 128), jnp.int32),
            pltpu.SMEM((SEQ * HEADS + 8,), jnp.int32),
            pltpu.SemaphoreType.DMA(()),
        ],
        compiler_params=params(8),
        cost_estimate=cost(3),
        name="pick",
    )(at, x)


def attend(block, bias, q, k, v):
    lane = lax.broadcasted_iota(jnp.int32, (BLK, FW), 1)
    out = None
    for j in range(FW // HDIM):
        mine = (lane >= j * HDIM) & (lane < (j + 1) * HDIM)
        s = mm_nt(jnp.where(mine, q, jnp.zeros_like(q)), k)
        parts = [s[:, :BLK], s[:, BLK:]]
        parts[1 - block] = parts[1 - block] + bias
        top = jnp.max(jnp.maximum(parts[0], parts[1]), axis=-1, keepdims=True)
        p = jnp.concatenate([jnp.exp2(x - top).astype(BF) for x in parts], axis=1)
        o = mm(p, v)
        o = o[:, :FW] * (1.0 / o[:, FW : FW + 1])
        out = o if out is None else jnp.where(mine, o, out)
    return out.astype(BF)


def key_copies(head, w_ref, fs, sems):
    return [
        pltpu.make_async_copy(
            w_ref.at[:, lax.rem(head + d, HEADS), pl.ds(KV_AT, FW + 16)], fs.at[d], sems.at[d]
        )
        for d in range(HEADS)
    ]


def project(block, gain, copies, fs, kv_refs):
    n = norm(block.astype(F32), gain)
    lane = lax.broadcasted_iota(jnp.int32, (BLK, 2 * FW), 1)
    for c in copies:
        c.wait()
    z = mm_nt(n, jnp.concatenate([fs[d, 0, FW:] for d in range(HEADS)], axis=0))
    soft = jnp.maximum(z, 0.0) + jnp.log1p(jnp.exp(-jnp.abs(z)))
    rates = -(RATE_SCALE * VTOKENS**-0.5) * soft
    for d, kv_ref in enumerate(kv_refs):
        kv = mm_nt(n, fs[d, :, :FW].reshape(2 * FW, D)).astype(BF).astype(F32)
        kv_ref[...] = jnp.where(lane < FW, kv, kv * rates[:, d * 16 : d * 16 + 1]).astype(BF)


def encode_first_body(
    flag_ref, x_ref, gain_ref, fgain_ref, w_ref,
    o_ref, kv0, kv1, kv2, kv3, q_ref, k_ref, v_ref, rest_ref,
    xs, ns, ws, fs, sems, fsems,
):
    copies = [
        pltpu.make_async_copy(w_ref.at[:, g, pl.ds(0, FH)], ws.at[g], sems.at[g])
        for g in range(HEADS)
    ]
    later = key_copies(flag_ref[2], w_ref, fs, fsems)
    for c in copies + later:
        c.start()
    flip = flag_ref[0]
    bias = jnp.where(flag_ref[1] != 0, 0.0, -1e30).astype(F32)
    for b in range(2):
        base = pl.multiple_of(jnp.bitwise_xor(flip, b) * BLK, BLK)
        for c in range(2):
            for t in range(LT):
                xs[pl.ds(base, BLK), pl.ds(c * FH + t * 128, 128)] = (
                    x_ref[:, 2 * b + c, t].astype(F32).reshape(BLK, 128)
                )
    gain = gain_ref[...]
    for r in range(8):
        ns[pl.ds(r * 64, 64), :] = norm(xs[pl.ds(r * 64, 64), :], gain)
    rest_ref[...] = xs[BLK:, :].astype(BF)
    n = ns[...]
    scale = HDIM**-0.5 * LOG2E
    out = xs[:BLK, :]
    for g in range(HEADS):
        copies[g].wait()
        w = ws[g, :, : 3 * 96].reshape(3 * FW, D)
        q = (mm_nt(n, w[:FW]) * scale).astype(BF)
        k = mm_nt(n, w[FW : 2 * FW]).astype(BF)
        v = jnp.concatenate(
            [mm_nt(n, w[2 * FW :]).astype(BF), jnp.ones((SPAN, HDIM), BF)], axis=1
        )
        q_ref[g] = q[BLK:]
        k_ref[g] = k
        v_ref[g] = v
        att = attend(0, bias, q[:BLK], k, v)
        out = out + mm(att, ws[g, :, 3 * 96 :].reshape(FW, D))
    out = out.astype(BF)
    o_ref[...] = out
    project(out, fgain_ref[...], later, fs, (kv0, kv1, kv2, kv3))


def encode_first(flags, x, gain, fgain, w):
    return pl.pallas_call(
        encode_first_body,
        out_shape=(
            jax.ShapeDtypeStruct((BLK, D), BF),
            *[jax.ShapeDtypeStruct((BLK, 2 * FW), BF)] * HEADS,
            jax.ShapeDtypeStruct((HEADS, BLK, FW), BF),
            jax.ShapeDtypeStruct((HEADS, SPAN, FW), BF),
            jax.ShapeDtypeStruct((HEADS, SPAN, FW + HDIM), BF),
            jax.ShapeDtypeStruct((BLK, D), BF),
        ),
        in_specs=[SMEM, VMEM, VMEM, VMEM, ANY],
        out_specs=[VMEM] * 9,
        scratch_shapes=[
            pltpu.VMEM((SPAN, D), F32),
            pltpu.VMEM((SPAN, D), BF),
            pltpu.VMEM((HEADS, 2, FH, D), BF),
            pltpu.VMEM((HEADS, 2, FW + 16, D), BF),
            pltpu.SemaphoreType.DMA((HEADS,)),
            pltpu.SemaphoreType.DMA((HEADS,)),
        ],
        compiler_params=params(24),
        cost_estimate=cost(9),
        name="encode_first",
    )(flags, x, gain, fgain, w)


def encode_second_body(
    flag_ref, fgain_ref, q_ref, k_ref, v_ref, rest_ref, w_ref,
    o_ref, kv0, kv1, kv2, kv3, ws, fs, sem, fsems,
):
    copy = pltpu.make_async_copy(w_ref.at[:, :, pl.ds(3 * 96, 96)], ws, sem)
    copy.start()
    later = key_copies(flag_ref[2], w_ref, fs, fsems)
    for c in later:
        c.start()
    bias = jnp.where(flag_ref[1] != 0, 0.0, -1e30).astype(F32)
    out = rest_ref[...].astype(F32)
    for g in range(HEADS):
        att = attend(1, bias, q_ref[g], k_ref[g], v_ref[g])
        if g == 0:
            copy.wait()
        out = out + mm(att, ws[:, g].reshape(FW, D))
    out = out.astype(BF)
    o_ref[...] = out
    project(out, fgain_ref[...], later, fs, (kv0, kv1, kv2, kv3))


def encode_second(flags, fgain, q, k, v, rest, w):
    return pl.pallas_call(
        encode_second_body,
        out_shape=(
            jax.ShapeDtypeStruct((BLK, D), BF),
            *[jax.ShapeDtypeStruct((BLK, 2 * FW), BF)] * HEADS,
        ),
        in_specs=[SMEM, VMEM, VMEM, VMEM, VMEM, VMEM, ANY],
        out_specs=[VMEM] * 5,
        scratch_shapes=[
            pltpu.VMEM((2, HEADS, 96, D), BF),
            pltpu.VMEM((HEADS, 2, FW + 16, D), BF),
            pltpu.SemaphoreType.DMA(()),
            pltpu.SemaphoreType.DMA((HEADS,)),
        ],
        compiler_params=params(16),
        cost_estimate=cost(20),
        name="encode_second",
    )(flags, fgain, q, k, v, rest, w)


def query_body(flag_ref, x0_ref, x1_ref, gain_ref, w_ref, *refs):
    own_ref, up_ref, down_ref, ws, sems = refs
    whole = {0: own_ref, 1: up_ref, 3: down_ref}
    head = flag_ref[2]
    copies = [
        pltpu.make_async_copy(
            w_ref.at[:, lax.rem(head + d, HEADS), pl.ds(Q_AT, 96)], ws.at[d], sems.at[d]
        )
        for d in range(HEADS)
    ]
    for c in copies:
        c.start()
    xs = (x0_ref[...], x1_ref[...])
    ns = [norm(x.astype(F32), gain_ref[...]) for x in xs]
    cols = [[x[:, g * FW : (g + 1) * FW] for g in range(HEADS)] for x in xs]
    for d in range(HEADS):
        there = lax.rem(head + d, HEADS)
        copies[d].wait()
        w = ws[d].reshape(FW, D)
        for i in range(2):
            q = mm_nt(ns[i], w).astype(BF)
            c = cols[i]
            e = jnp.where(
                there < 2, jnp.where(there == 0, c[0], c[1]), jnp.where(there == 2, c[2], c[3])
            )
            qe = jnp.concatenate([q, e], axis=1)
            if d == 2:
                (up_ref, down_ref)[i][SPAN:, :] = qe
            else:
                whole[d][pl.ds(i * BLK, BLK), :] = qe


def query(flags, x0, x1, gain, w):
    return pl.pallas_call(
        query_body,
        out_shape=(
            jax.ShapeDtypeStruct((SPAN, 2 * FW), BF),
            jax.ShapeDtypeStruct((SPAN + BLK, 2 * FW), BF),
            jax.ShapeDtypeStruct((SPAN + BLK, 2 * FW), BF),
        ),
        in_specs=[SMEM, VMEM, VMEM, VMEM, ANY],
        out_specs=[VMEM] * 3,
        scratch_shapes=[
            pltpu.VMEM((HEADS, 2, 96, D), BF),
            pltpu.SemaphoreType.DMA((HEADS,)),
        ],
        compiler_params=params(12),
        cost_estimate=cost(4),
        name="fast_query",
    )(flags, x0, x1, gain, w)


def make_fast_body(blocks, first, last):
    def body(*refs):
        kv_refs = refs[:blocks]
        gu_ref, down_ref = refs[blocks : blocks + 2]
        sum_ref = None if first else refs[blocks + 2]
        g_ref = refs[-1]
        gate_up = [gu_ref[i].astype(BF) for i in range(2)]
        down = down_ref[...].astype(BF)
        sums = None
        for kv_ref in kv_refs:
            key = kv_ref[:, :FW]
            out_grad = kv_ref[:, FW:]
            gate = mm(key, gate_up[0])
            up = mm(key, gate_up[1])
            hidden_grad = mm(out_grad, down)
            s = jax.nn.sigmoid(gate)
            silu = gate * s
            hidden = (silu * up).astype(BF)
            gate_grad = (hidden_grad * up * s * (1.0 + gate * (1.0 - s))).astype(BF)
            up_grad = (hidden_grad * silu).astype(BF)
            parts = [mm_tn(key, gate_grad), mm_tn(key, up_grad), mm_tn(out_grad, hidden)]
            sums = parts if sums is None else [a + b for a, b in zip(sums, parts)]
        for i, total in enumerate(sums):
            if not first:
                total = total + sum_ref[i]
            if last:
                for t in range(LT):
                    g_ref[pl.ds((i * LT + t) * 24, 24)] = (
                        total[:, t * 128 : (t + 1) * 128].astype(BF).reshape(24, 8, 128)
                    )
            else:
                g_ref[i] = total
        if last:
            g_ref[pl.ds(216, 8)] = jnp.zeros((8, 8, 128), BF)

    return body


def fast(blocks, shared, sums, last):
    first = sums is None
    operands = (*blocks, *shared) + (() if first else (sums,))
    return pl.pallas_call(
        make_fast_body(len(blocks), first, last),
        out_shape=(
            jax.ShapeDtypeStruct((GT, 8, 128), BF)
            if last
            else jax.ShapeDtypeStruct((3, FW, FH), F32)
        ),
        in_specs=[VMEM] * len(operands),
        out_specs=VMEM,
        compiler_params=params(16),
        cost_estimate=cost(3),
        name="fast_grad",
    )(*operands)


def sum_body(x_ref, o_ref):
    total = x_ref[0].astype(F32)
    for i in range(1, SEQ):
        total = total + x_ref[i].astype(F32)
    total = total.astype(BF)
    for i in range(SEQ):
        o_ref[i] = total


def sum_pieces(x):
    return pl.pallas_call(
        sum_body,
        out_shape=jax.ShapeDtypeStruct(x.shape, BF),
        in_specs=[VMEM],
        out_specs=VMEM,
        compiler_params=params(4),
        cost_estimate=cost(1),
        name="sum_pieces",
    )(x)


def renorm(updated, initial, axis):
    target = jnp.sqrt(jnp.sum(initial * initial, axis=axis, keepdims=True))
    return updated * target * lax.rsqrt(jnp.sum(updated * updated, axis=axis, keepdims=True) + EPSILON)


def apply_body(head_ref, g_ref, gu_ref, down_ref, *refs):
    qe_refs, (o_ref, gs, ws) = refs[:5], refs[5:]
    for i in range(3):
        for t in range(LT):
            gs[i, :, pl.ds(t * 128, 128)] = (
                g_ref[pl.ds((i * LT + t) * 24, 24)].astype(F32).reshape(FW, 128)
            )
        init = down_ref[...] if i == 2 else gu_ref[i]
        ws[i] = renorm(init - gs[i], init, 0 if i == 2 else 1).astype(BF)
    row = lax.broadcasted_iota(jnp.int32, (FW, 2 * FW), 0)
    col = lax.broadcasted_iota(jnp.int32, (FW, 2 * FW), 1)
    columns = jnp.where(row + FW == col, 1.0, 0.0).astype(BF)
    own_ref, up_ref, down_side_ref, far0_ref, far1_ref = qe_refs
    for d in range(HEADS):
        if d == 2:
            qe = jnp.concatenate([far0_ref[...], far1_ref[...]], axis=0)
        else:
            qe = {0: own_ref, 1: up_ref, 3: down_side_ref}[d][:SPAN, :]
        q = qe[:, :FW]
        gate = mm(q, ws[0])
        hidden = (gate * jax.nn.sigmoid(gate) * mm(q, ws[1])).astype(BF)
        base = pl.multiple_of(lax.rem(head_ref[2] + HEADS - d, HEADS) * SPAN, SPAN)
        o_ref[:, pl.ds(base, SPAN)] = (mm_nt(columns, qe) + mm_nt(ws[2], hidden)).astype(BF)


def apply(flags, grads, gate_up, down, qes):
    return pl.pallas_call(
        apply_body,
        out_shape=jax.ShapeDtypeStruct((FW, HEADS * SPAN), BF),
        in_specs=[SMEM] + [VMEM] * 8,
        out_specs=VMEM,
        scratch_shapes=[pltpu.VMEM((3, FW, FH), F32), pltpu.VMEM((3, FW, FH), BF)],
        compiler_params=params(16),
        cost_estimate=cost(3),
        name="apply_fast",
    )(flags, grads, gate_up, down, *qes)


def exchange(x, axes):
    return lax.all_to_all(x, axes, split_axis=0, concat_axis=0, tiled=True)


def shifted(x, by):
    return lax.ppermute(x, "head", [(i, (i + by) % HEADS) for i in range(HEADS)])


def on_device(
    patches,
    slot_image,
    slot_dest,
    enc_gain,
    w_qkv,
    w_out,
    fast_gain,
    w_fast,
    w_rate,
    fast_gate_up,
    fast_down,
):
    head = lax.axis_index("head")
    core = lax.axis_index("core")
    seq = lax.axis_index(SEQ_AXES)
    at = jnp.stack([seq * HEADS + head, head, core]).astype(jnp.int32)

    ids = jnp.concatenate([slot_dest, slot_image]).astype(BF)
    tile = jnp.pad(ids[None, :], ((0, 7), (0, 96)))
    pieces, rows = spread(
        at,
        patches.reshape(-1, 8, D),
        tile,
        jnp.transpose(w_qkv, (0, 2, 1)).reshape(3 * FW, D),
        w_out,
        jnp.transpose(w_fast, (0, 2, 1)).reshape(3 * FW, D),
        jnp.broadcast_to(w_rate.T, (16, D)),
    )
    weights = lax.all_gather(rows, ("core", "head"), axis=0, tiled=False)
    weights = in_hbm(weights.reshape(2, HEADS, WROWS, D))
    picked, flags = pick(at, exchange(pieces, SEQ_AXES))
    mine = exchange(picked, ALL_AXES)

    fgain = fast_gain.reshape(1, D)
    own_0, *outs = encode_first(
        flags, mine.reshape(SEQ, 4, LT, 8, 128), enc_gain.reshape(1, D), fgain, weights
    )
    kv_0, carried = tuple(outs[:HEADS]), outs[HEADS:]
    got_0 = tuple(shifted(kv_0[d], d) for d in range(1, HEADS))
    own_1, *kv_1 = encode_second(flags, fgain, *carried, weights)
    kv_1 = tuple(kv_1)
    kv_1, got_0 = lax.optimization_barrier((kv_1, got_0))
    got_1 = tuple(shifted(kv_1[d], d) for d in range(1, HEADS))

    gate_up = fast_gate_up[0]
    down = fast_down[0].T
    sums = fast((kv_0[0], kv_1[0]), (gate_up, down), None, False)
    sums = fast(got_0, (gate_up, down), sums, False)
    qe = query(flags, own_0, own_1, fgain, weights)
    got_1, qe = lax.optimization_barrier((got_1, tuple(qe)))
    grads = fast(got_1, (gate_up, down), sums, True)

    own_qe, up_qe, down_qe = qe
    up_qe, down_qe = shifted(up_qe, 1), shifted(down_qe, -1)
    far_qe = (shifted(up_qe[SPAN:], 1), shifted(down_qe[SPAN:], -1))
    arrived = exchange(grads, SEQ_AXES)
    whole = exchange(sum_pieces(arrived.reshape(SEQ, GT // SEQ, 8, 128)), SEQ_AXES)
    return apply(
        flags,
        whole.reshape(GT, 8, 128),
        gate_up,
        down,
        (own_qe, up_qe, down_qe, *far_qe),
    ).T


def solution(mesh):
    fine = Mesh(mesh.devices.reshape(4, 4, 2, HEADS), ALL_AXES)
    in_specs = (
        P(SEQ_AXES, None),
        P(SEQ_AXES),
        P(SEQ_AXES),
        P(),
        P(None, None, "head"),
        P("head", None),
        P(),
        P(None, None, "head"),
        P(None, "head"),
        P("head", None, None, None),
        P("head", None, None),
    )
    return jax.shard_map(
        on_device, mesh=fine, in_specs=in_specs, out_specs=P(SEQ_AXES, "head"), check_vma=False
    )
```

time: 169 us -> 159 us (0.941)
  starting transfers between devices: 14.4 us -> 31.5 us
  blocking collectives: 48.8 us -> 32.7 us
  local copies, waits for them, and re-layouts: 8.75 us -> 0.68 us
  waiting for transfers between devices: 32.1 us -> 36.2 us
  Pallas kernels: 46.1 us -> 42.7 us
  other arithmetic: 3.91 us -> 1.54 us
    all_to_all x2 -> x1, blocking collectives: 48.8 us -> 32.7 us  [exchange(): return lax.all_to_all(x, axes, split_axis=0, concat_axis=0, tiled=True)]
    all_to_all x2 -> x3, waiting for transfers between devices: 18.2 us -> 28.9 us  [exchange(): return lax.all_to_all(x, axes, split_axis=0, concat_axis=0, tiled=True)]
    ppermute x6 -> x10, starting transfers between devices: 4.79 us -> 13.7 us  [shifted(): lax.ppermute(x, 'head', [(i, (i + by) % HEADS) for i in range(HEADS)])]
    all_to_all x2 -> x3, starting transfers between devices: 9.63 us -> 17.8 us  [exchange(): return lax.all_to_all(x, axes, split_axis=0, concat_axis=0, tiled=True)]
    ppermute x6 -> x10, waiting for transfers between devices: 13.8 us -> 7.23 us  [shifted(): lax.ppermute(x, 'head', [(i, (i + by) % HEADS) for i in range(HEADS)])]
    unnamed x30 -> x8, local copies, waits for them, and re-layouts: 6.4 us -> 0.01 us
    pallas_call x8 -> x7, Pallas kernels: 30.1 us -> 26.6 us  [the longest x1 7.02 us: encode_second(): pl.pallas_call(encode_second_body, out_shape=(jax.ShapeDtypeStruct((BLK,...]
  transfers between devices with their start and end apart: 9 -> 14, of which waited for: 6 -> 9; matrix products, arithmetic and copies ran while one was open for 3% -> 0% of each run, Pallas kernels for 12% -> 14%
where the time goes in v2:
time: 159 us
  Pallas kernels  42.7 us (27%)
  waiting for transfers between devices  36.2 us (23%)
  blocking collectives  32.7 us (21%)
  starting transfers between devices  31.5 us (20%)
  between operations  13.6 us (9%)
    all_to_all x1, blocking collectives, exchange(): return lax.all_to_all(x, axes, split_axis=0, concat_axis=0, tiled=True)  32.7 us
    all_to_all x3, waiting for transfers between devices, exchange(): return lax.all_to_all(x, axes, split_axis=0, concat_axis=0, tiled=True)  28.9 us
    all_to_all x3, starting transfers between devices, exchange(): return lax.all_to_all(x, axes, split_axis=0, concat_axis=0, tiled=True)  17.8 us
    ppermute x10, starting transfers between devices, shifted(): lax.ppermute(x, 'head', [(i, (i + by) % HEADS) for i in range(HEADS)])  13.7 us
    pallas_call x1, Pallas kernels, encode_first(): pl.pallas_call(encode_first_body, out_shape=(jax.ShapeDtypeStruct((BLK, D...  11 us
    ppermute x10, waiting for transfers between devices, shifted(): lax.ppermute(x, 'head', [(i, (i + by) % HEADS) for i in range(HEADS)])  7.23 us
    pallas_call x1, Pallas kernels, encode_second(): pl.pallas_call(encode_second_body, out_shape=(jax.ShapeDtypeStruct((BLK,...  7.02 us
    pallas_call x1, Pallas kernels, pick(): pl.pallas_call(pick_body, out_shape=(jax.ShapeDtypeStruct((SEQ * HEADS, L...  6.67 us
  transfers between devices with their start and end apart: 14, of which 9 were waited for; matrix products, arithmetic and copies ran while one was open for 0% of the time, Pallas kernels for 14%

profile of v2, /device:TPU:1, one launch (start us, length us, event | category | flops | bytes accessed | tf_op | source)
XLA Modules:
  0.0 159.0 jit_solution(16689797053179667679)
XLA Ops:
  6.5 0.0 all-gather.3.cloned.1.call-start
  6.5 0.7 convert_bitcast_fusion
  7.2 0.1 fusion.5.meta_ref
  7.3 0.7 reduce
  8.0 0.1 pad_add_fusion.at_ref
  8.1 0.6 broadcast_in_dim.9.rate_ref
  8.7 3.5 %spread.1 = (bf16[32,25,8,128]{3,2,1,0:T(8,128)(2,1)S(1)}, bf16[688,768]{1,0:T(8,128)(2,1)}) custom-call(s32[3]{0:T(128)S(1)} %pad_add_fusion.at_ref, bf16[512,8,768]{2,1,0:T(8,128)(2,1)} %bitcast.37, bf16[8,128]{1,0:T(8,128)(2,1)S(1)} %fusion.5.meta_ref, bf16[576,768]{1,0:T(8,128)(2,1)} %bitcast.38, bf16[192,768]{1,0:T(8,128)(2,1)} %out_ref.1, ...), custom_call_target="tpu_custom_call" | custom-call | bytes 10800000 | tf_op jit(solution)/shard_map/spread/pallas_call | solution.py:111
  12.2 0.0 all-gather.3.cloned.1.call-update
  12.2 32.7 %all_to_all.20.x_ref = bf16[32,25,8,128]{3,2,1,0:T(8,128)(2,1)S(1)} all-to-all(bf16[32,25,8,128]{3,2,1,0:T(8,128)(2,1)S(1)} %get-tuple-element.39), channel_id=1, replica_groups=mesh['x'=4,'z'=4,'core'=2,'head'=4] {'x','z','core'}, dimensions={0} | all-to-all | bytes 3276800 | tf_op jit(solution)/shard_map/all_to_all | solution.py:506
  45.0 0.0 copy-start.2
  45.0 0.0 copy-start.3
  45.0 6.7 %pick.1 = (bf16[128,3,8,128]{3,2,1,0:T(8,128)(2,1)}, s32[3]{0:T(128)S(1)}) custom-call(s32[3]{0:T(128)S(1)} %pad_add_fusion.at_ref, bf16[32,25,8,128]{3,2,1,0:T(8,128)(2,1)S(1)} %all_to_all.20.x_ref), custom_call_target="tpu_custom_call" | custom-call | bytes 10800000 | tf_op jit(solution)/shard_map/pick/pallas_call | solution.py:160
  51.6 5.7 %all-to-all-start.1 = ((bf16[128,3,8,128]{3,2,1,0:T(8,128)(2,1)}), bf16[128,3,8,128]{3,2,1,0:T(8,128)(2,1)S(1)}, u32[]{:S(2)}, u32[]{:S(2)}) async-start(bf16[128,3,8,128]{3,2,1,0:T(8,128)(2,1)} %get-tuple-element.41), calls=%async_computation.1 | async-start | bytes 1572864 | tf_op jit(solution)/shard_map/all_to_all | solution.py:506
  57.4 0.0 copy-done.2
  57.4 0.0 copy-done.3
  57.4 16.9 %all-to-all-done.1 = bf16[128,3,8,128]{3,2,1,0:T(8,128)(2,1)S(1)} async-done(((bf16[128,3,8,128]{3,2,1,0:T(8,128)(2,1)}), bf16[128,3,8,128]{3,2,1,0:T(8,128)(2,1)S(1)}, u32[]{:S(2)}, u32[]{:S(2)}) %all-to-all-start.1) | async-done | bytes 786464 | tf_op jit(solution)/shard_map/all_to_all | solution.py:506
  74.3 0.1 all-gather.3.cloned.1.call-done
  74.4 11.0 %encode_first.1 = (bf16[256,768]{1,0:T(8,128)(2,1)S(1)}, bf16[256,384]{1,0:T(8,128)(2,1)S(1)}, bf16[256,384]{1,0:T(8,128)(2,1)S(1)}, bf16[256,384]{1,0:T(8,128)(...) custom-call(s32[3]{0:T(128)S(1)} %get-tuple-element.40.flag_ref.head, ...), custom_call_target="tpu_custom_call" | custom-call | bytes 32400000 | tf_op jit(solution)/shard_map/encode_first/pallas_call | solution.py:265
  85.4 0.5 collective-permute-start
  85.9 1.8 %collective-permute-start.1 = (bf16[256,384]{1,0:T(8,128)(2,1)S(1)}, bf16[256,384]{1,0:T(8,128)(2,1)S(1)}, u32[]{:S(2)}, u32[]{:S(2)}) collective-permute-start(bf16[256,384]{1,0:T(8,128)(2,1)S(1)} %get-tuple-element.52), channel_id=1, source_target_pairs={{0,2},{1,3},{2,0},{3,1},{4,6},{5,7},{6,4},{7,5},{8,10},{9,11},{10,... | collective-permute-start | bytes 589832 | tf_op jit(solution)/shard_map/ppermute | solution.py:510
  87.7 1.5 collective-permute-start.2
  89.2 7.0 %encode_second.1 = (bf16[256,768]{1,0:T(8,128)(2,1)S(1)}, bf16[256,384]{1,0:T(8,128)(2,1)S(1)}, bf16[256,384]{1,0:T(8,128)(2,1)S(1)}, bf16[256,384]{1,0:T(8,128)(2,1)S(1)}, bf16[256,384]{1,0:T(8,128)(2,1)S(1)}) custom-call(s32[3]{0:T(128)S(1)} %get-tuple-element.40.flag_ref.head_ref, f32[1,768]{1,0:T(1,128)S(1)} %reshape.62.fgain_ref.gain_ref, ...), custom_call_target="tpu_custom_call" | custom-call | bytes 72000000 | tf_op jit(solution)/shard_map/encode_second/pallas_call | solution.py:313
  96.2 0.0 collective-permute-done.refs_0_
  96.2 0.3 collective-permute-done.1.refs_1_
  96.6 0.9 collective-permute-done.2.refs_2_
  97.5 1.9 %collective-permute-start.3 = (bf16[256,384]{1,0:T(8,128)(2,1)S(1)}, bf16[256,384]{1,0:T(8,128)(2,1)S(1)}, u32[]{:S(2)}, u32[]{:S(2)}) collective-permute-start(bf16[256,384]{1,0:T(8,128)(2,1)S(1)} %get-tuple-element.54), channel_id=1, source_target_pairs={{0,1},{1,2},{2,3},{3,0},{4,5},{5,6},{6,7},{7,4},{8,9},{9,10},{10,1... | collective-permute-start | bytes 589832 | tf_op jit(solution)/shard_map/ppermute | solution.py:510
  99.4 2.6 %collective-permute-start.4 = (bf16[256,384]{1,0:T(8,128)(2,1)S(1)}, bf16[256,384]{1,0:T(8,128)(2,1)S(1)}, u32[]{:S(2)}, u32[]{:S(2)}) collective-permute-start(bf16[256,384]{1,0:T(8,128)(2,1)S(1)} %get-tuple-element.55), channel_id=1, source_target_pairs={{0,2},{1,3},{2,0},{3,1},{4,6},{5,7},{6,4},{7,5},{8,10},{9,11},{10,... | collective-permute-start | bytes 589832 | tf_op jit(solution)/shard_map/ppermute | solution.py:510
  101.9 0.0 collective-permute-start.5
  101.9 0.0 copy-start
  101.9 0.0 copy-start.1
  101.9 4.0 %fast_query.1 = (bf16[512,384]{1,0:T(8,128)(2,1)S(1)}, bf16[768,384]{1,0:T(8,128)(2,1)S(1)}, bf16[768,384]{1,0:T(8,128)(2,1)}) custom-call(s32[3]{0:T(128)S(1)} %get-tuple-element.40.flag_ref.head_ref, bf16[256,768]{1,0:T(8,128)(2,1)S(1)} %get-tuple-element.57.x0_ref, bf16[256,768]{1,0:T(8,128)(2,1)S(1)} %get-tuple-element.58.x1_ref, ...), custom_call_target="tpu_custom_call" | custom-call | bytes 14400000 | tf_op jit(solution)/shard_map/fast_query/pallas_call | solution.py:366
  106.0 0.0 copy-done
  106.0 0.0 copy-done.1
  106.0 1.2 fast_grad.3.refs_5_
  107.2 1.7 %fast_grad.4.refs_5_ = f32[3,192,384]{2,1,0:T(8,128)S(1)} custom-call(bf16[256,384]{1,0:T(8,128)(2,1)S(1)} %collective-permute-done.refs_0_, bf16[256,384]{1,0:T(8,128)(2,1)S(1)} %collective-permute-done.1.refs_1_, bf16[256,384]{1,0:T(8,128)(2,1)S(1)} %collective-permute-done.2.refs_2_, f32[2,192,384]{2,1,0:T(8,128)S(1)} %bitcast.24, ...), custom_call_target="tpu_custom_call" | custom-call | bytes 10800000 | tf_op jit(solution)/shard_map/fast_grad/pallas_call | solution.py:426
  108.9 0.0 collective-permute-done.3.refs_0_
  108.9 1.7 %collective-permute-done.4.refs_1_ = bf16[256,384]{1,0:T(8,128)(2,1)S(1)} collective-permute-done((bf16[256,384]{1,0:T(8,128)(2,1)S(1)}, bf16[256,384]{1,0:T(8,128)(2,1)S(1)}, u32[]{:S(2)}, u32[]{:S(2)}) %collective-permute-start.4) | collective-permute-done | bytes 196640 | tf_op jit(solution)/shard_map/ppermute | solution.py:510
  110.6 0.0 collective-permute-done.5.refs_2_
  110.6 2.5 %fast_grad.5 = bf16[224,8,128]{2,1,0:T(8,128)(2,1)} custom-call(bf16[256,384]{1,0:T(8,128)(2,1)S(1)} %collective-permute-done.3.refs_0_, bf16[256,384]{1,0:T(8,128)(2,1)S(1)} %collective-permute-done.4.refs_1_, bf16[256,384]{1,0:T(8,128)(2,1)S(1)} %collective-permute-done.5.refs_2_, f32[2,192,384]{2,1,0:T(8,128)S(1)} %bitcast.25, f32[192,384]{1,0:T(8,128)S(1)} %bitcast.29, ...), custom_call_target="tpu_custom_call" | custom-call | bytes 10800000 | tf_op jit(solution)/shard_map/fast_grad/pallas_call | solution.py:426
  113.2 8.3 %all-to-all-start.2 = ((bf16[224,8,128]{2,1,0:T(8,128)(2,1)}), bf16[224,8,128]{2,1,0:T(8,128)(2,1)S(1)}, u32[]{:S(2)}, u32[]{:S(2)}) async-start(bf16[224,8,128]{2,1,0:T(8,128)(2,1)} %fast_grad.5), calls=%async_computation.2 | async-start | bytes 917504 | tf_op jit(solution)/shard_map/all_to_all | solution.py:506
  121.5 0.5 collective-permute-start.6
  122.0 2.3 %collective-permute-start.7 = (bf16[768,384]{1,0:T(8,128)(2,1)}, bf16[768,384]{1,0:T(8,128)(2,1)S(1)}, u32[]{:S(2)}, u32[]{:S(2)}) collective-permute-start(bf16[768,384]{1,0:T(8,128)(2,1)} %get-tuple-element.72), channel_id=1, source_target_pairs={{0,3},{1,0},{2,1},{3,2},{4,7},{5,4},{6,5},{7,6},{8,11},{9,8},{10,9... | collective-permute-start | bytes 1769480 | tf_op jit(solution)/shard_map/ppermute | solution.py:510
  124.3 8.2 %all-to-all-done.2 = bf16[224,8,128]{2,1,0:T(8,128)(2,1)S(1)} async-done(((bf16[224,8,128]{2,1,0:T(8,128)(2,1)}), bf16[224,8,128]{2,1,0:T(8,128)(2,1)S(1)}, u32[]{:S(2)}, u32[]{:S(2)}) %all-to-all-start.2) | async-done | bytes 458784 | tf_op jit(solution)/shard_map/all_to_all | solution.py:506
  132.5 0.9 sum_pieces.1
  133.4 3.7 %all-to-all-start.3 = ((bf16[32,7,8,128]{3,2,1,0:T(8,128)(2,1)}), bf16[32,7,8,128]{3,2,1,0:T(8,128)(2,1)S(1)}, u32[]{:S(2)}, u32[]{:S(2)}) async-start(bf16[32,7,8,128]{3,2,1,0:T(8,128)(2,1)} %sum_pieces.1), calls=%async_computation.3 | async-start | bytes 917504 | tf_op jit(solution)/shard_map/all_to_all | solution.py:506
  137.1 0.5 collective-permute-done.6.refs_1_
  137.5 0.1 collective-permute-start.8
  137.6 0.0 collective-permute-done.7.refs_2_
  137.7 2.7 %collective-permute-start.9 = (bf16[256,384]{1,0:T(8,128)(2,1)S(1)}, bf16[256,384]{1,0:T(8,128)(2,1)S(1)}, u32[]{:S(2)}, u32[]{:S(2)}) collective-permute-start(bf16[256,384]{1,0:T(8,128)(2,1)S(1)} %slice.9), channel_id=1, source_target_pairs={{0,3},{1,0},{2,1},{3,2},{4,7},{5,4},{6,5},{7,6},{8,11},{9,8},{10,9... | collective-permute-start | bytes 589832 | tf_op jit(solution)/shard_map/ppermute | solution.py:510
  140.4 3.8 %collective-permute-done.8.refs_3_ = bf16[256,384]{1,0:T(8,128)(2,1)S(1)} collective-permute-done((bf16[256,384]{1,0:T(8,128)(2,1)S(1)}, bf16[256,384]{1,0:T(8,128)(2,1)S(1)}, u32[]{:S(2)}, u32[]{:S(2)}) %collective-permute-start.8) | collective-permute-done | bytes 196640 | tf_op jit(solution)/shard_map/ppermute | solution.py:510
  144.2 0.0 collective-permute-done.9.refs_4_
  144.2 3.8 %all-to-all-done.3 = bf16[32,7,8,128]{3,2,1,0:T(8,128)(2,1)S(1)} async-done(((bf16[32,7,8,128]{3,2,1,0:T(8,128)(2,1)}), bf16[32,7,8,128]{3,2,1,0:T(8,128)(2,1)S(1)}, u32[]{:S(2)}, u32[]{:S(2)}) %all-to-all-start.3) | async-done | bytes 458784 | tf_op jit(solution)/shard_map/all_to_all | solution.py:506
  147.9 4.2 %apply_fast.1 = bf16[192,2048]{1,0:T(8,128)(2,1)} custom-call(s32[3]{0:T(128)S(1)} %get-tuple-element.40.flag_ref.head_ref, bf16[224,8,128]{2,1,0:T(8,128)(2,1)S(1)} %bitcast.32, f32[2,192,384]{2,1,0:T(8,128)S(1)} %bitcast.26, f32[192,384]{1,0:T(8,128)S(1)} %bitcast.30, bf16[512,384]{1,0:T(8,128)(2,1)S(1)} %get-tuple-element.70.refs_0_, ...), custom_call_target="tpu_custom_call" | custom-call | bytes 10800000 | tf_op jit(solution)/shard_map/apply_fast/pallas_call | solution.py:493
  (4 shorter events, 0.1 us)
Async XLA Ops:
  6.5 67.9 %all-gather.3.cloned.1.call-start = ((), (), s32[]{:S(2)}) async-start(), calls=%async_computation.4 | async-start | bytes 9510912 | tf_op jit(solution)/shard_map/all_gather | solution.py:542
  45.0 12.4 %copy-start.2 = (f32[768]{0:T(1024)S(1)}, f32[768]{0:T(1024)}, u32[]{:S(2)}) copy-start(f32[768]{0:T(1024)} %param.17) | copy-start | bytes 9220
  45.0 12.4 %copy-start.3 = (f32[768]{0:T(1024)S(1)}, f32[768]{0:T(1024)}, u32[]{:S(2)}) copy-start(f32[768]{0:T(1024)} %param.14) | copy-start | bytes 9220
  51.6 22.7 %all-to-all-start.1 = ((bf16[128,3,8,128]{3,2,1,0:T(8,128)(2,1)}), bf16[128,3,8,128]{3,2,1,0:T(8,128)(2,1)S(1)}, u32[]{:S(2)}, u32[]{:S(2)}) async-start(bf16[128,3,8,128]{3,2,1,0:T(8,128)(2,1)} %get-tuple-element.41), calls=%async_computation.1 | async-start | bytes 1572864 | tf_op jit(solution)/shard_map/all_to_all | solution.py:506
  85.4 10.8 %collective-permute-start = (bf16[256,384]{1,0:T(8,128)(2,1)S(1)}, bf16[256,384]{1,0:T(8,128)(2,1)S(1)}, u32[]{:S(2)}, u32[]{:S(2)}) collective-permute-start(bf16[256,384]{1,0:T(8,128)(2,1)S(1)} %get-tuple-element.51), channel_id=1, source_target_pairs={{0,1},{1,2},{2,3},{3,0},{4,5},{5,6},{6,7},{7,4},{8,9},{9,10},{10,1... | collective-permute-start | bytes 589832 | tf_op jit(solution)/shard_map/ppermute | solution.py:510
  85.9 10.7 %collective-permute-start.1 = (bf16[256,384]{1,0:T(8,128)(2,1)S(1)}, bf16[256,384]{1,0:T(8,128)(2,1)S(1)}, u32[]{:S(2)}, u32[]{:S(2)}) collective-permute-start(bf16[256,384]{1,0:T(8,128)(2,1)S(1)} %get-tuple-element.52), channel_id=1, source_target_pairs={{0,2},{1,3},{2,0},{3,1},{4,6},{5,7},{6,4},{7,5},{8,10},{9,11},{10,... | collective-permute-start | bytes 589832 | tf_op jit(solution)/shard_map/ppermute | solution.py:510
  87.7 9.8 %collective-permute-start.2 = (bf16[256,384]{1,0:T(8,128)(2,1)S(1)}, bf16[256,384]{1,0:T(8,128)(2,1)S(1)}, u32[]{:S(2)}, u32[]{:S(2)}) collective-permute-start(bf16[256,384]{1,0:T(8,128)(2,1)S(1)} %get-tuple-element.53), channel_id=1, source_target_pairs={{0,3},{1,0},{2,1},{3,2},{4,7},{5,4},{6,5},{7,6},{8,11},{9,8},{10,9... | collective-permute-start | bytes 589832 | tf_op jit(solution)/shard_map/ppermute | solution.py:510
  97.5 11.4 %collective-permute-start.3 = (bf16[256,384]{1,0:T(8,128)(2,1)S(1)}, bf16[256,384]{1,0:T(8,128)(2,1)S(1)}, u32[]{:S(2)}, u32[]{:S(2)}) collective-permute-start(bf16[256,384]{1,0:T(8,128)(2,1)S(1)} %get-tuple-element.54), channel_id=1, source_target_pairs={{0,1},{1,2},{2,3},{3,0},{4,5},{5,6},{6,7},{7,4},{8,9},{9,10},{10,1... | collective-permute-start | bytes 589832 | tf_op jit(solution)/shard_map/ppermute | solution.py:510
  99.4 11.3 %collective-permute-start.4 = (bf16[256,384]{1,0:T(8,128)(2,1)S(1)}, bf16[256,384]{1,0:T(8,128)(2,1)S(1)}, u32[]{:S(2)}, u32[]{:S(2)}) collective-permute-start(bf16[256,384]{1,0:T(8,128)(2,1)S(1)} %get-tuple-element.55), channel_id=1, source_target_pairs={{0,2},{1,3},{2,0},{3,1},{4,6},{5,7},{6,4},{7,5},{8,10},{9,11},{10,... | collective-permute-start | bytes 589832 | tf_op jit(solution)/shard_map/ppermute | solution.py:510
  101.9 8.7 %collective-permute-start.5 = (bf16[256,384]{1,0:T(8,128)(2,1)S(1)}, bf16[256,384]{1,0:T(8,128)(2,1)S(1)}, u32[]{:S(2)}, u32[]{:S(2)}) collective-permute-start(bf16[256,384]{1,0:T(8,128)(2,1)S(1)} %get-tuple-element.56), channel_id=1, source_target_pairs={{0,3},{1,0},{2,1},{3,2},{4,7},{5,4},{6,5},{7,6},{8,11},{9,8},{10,9... | collective-permute-start | bytes 589832 | tf_op jit(solution)/shard_map/ppermute | solution.py:510
  101.9 4.0 %copy-start = (f32[1,2,192,384]{3,2,1,0:T(8,128)S(1)}, f32[1,2,192,384]{3,2,1,0:T(8,128)}, u32[]{:S(2)}) copy-start(f32[1,2,192,384]{3,2,1,0:T(8,128)} %param.20) | copy-start | bytes 1769476
  101.9 4.1 %copy-start.1 = (f32[1,384,192]{1,2,0:T(8,128)S(1)}, f32[1,384,192]{1,2,0:T(8,128)}, u32[]{:S(2)}) copy-start(f32[1,384,192]{1,2,0:T(8,128)} %param.21) | copy-start | bytes 884740
  113.2 19.3 %all-to-all-start.2 = ((bf16[224,8,128]{2,1,0:T(8,128)(2,1)}), bf16[224,8,128]{2,1,0:T(8,128)(2,1)S(1)}, u32[]{:S(2)}, u32[]{:S(2)}) async-start(bf16[224,8,128]{2,1,0:T(8,128)(2,1)} %fast_grad.5), calls=%async_computation.2 | async-start | bytes 917504 | tf_op jit(solution)/shard_map/all_to_all | solution.py:506
  121.5 16.0 %collective-permute-start.6 = (bf16[768,384]{1,0:T(8,128)(2,1)S(1)}, bf16[768,384]{1,0:T(8,128)(2,1)S(1)}, u32[]{:S(2)}, u32[]{:S(2)}) collective-permute-start(bf16[768,384]{1,0:T(8,128)(2,1)S(1)} %get-tuple-element.71), channel_id=1, source_target_pairs={{0,1},{1,2},{2,3},{3,0},{4,5},{5,6},{6,7},{7,4},{8,9},{9,10},{10,1... | collective-permute-start | bytes 1769480 | tf_op jit(solution)/shard_map/ppermute | solution.py:510
  122.0 15.6 %collective-permute-start.7 = (bf16[768,384]{1,0:T(8,128)(2,1)}, bf16[768,384]{1,0:T(8,128)(2,1)S(1)}, u32[]{:S(2)}, u32[]{:S(2)}) collective-permute-start(bf16[768,384]{1,0:T(8,128)(2,1)} %get-tuple-element.72), channel_id=1, source_target_pairs={{0,3},{1,0},{2,1},{3,2},{4,7},{5,4},{6,5},{7,6},{8,11},{9,8},{10,9... | collective-permute-start | bytes 1769480 | tf_op jit(solution)/shard_map/ppermute | solution.py:510
  133.4 14.6 %all-to-all-start.3 = ((bf16[32,7,8,128]{3,2,1,0:T(8,128)(2,1)}), bf16[32,7,8,128]{3,2,1,0:T(8,128)(2,1)S(1)}, u32[]{:S(2)}, u32[]{:S(2)}) async-start(bf16[32,7,8,128]{3,2,1,0:T(8,128)(2,1)} %sum_pieces.1), calls=%async_computation.3 | async-start | bytes 917504 | tf_op jit(solution)/shard_map/all_to_all | solution.py:506
  137.5 6.6 %collective-permute-start.8 = (bf16[256,384]{1,0:T(8,128)(2,1)S(1)}, bf16[256,384]{1,0:T(8,128)(2,1)S(1)}, u32[]{:S(2)}, u32[]{:S(2)}) collective-permute-start(bf16[256,384]{1,0:T(8,128)(2,1)S(1)} %slice.8), channel_id=1, source_target_pairs={{0,1},{1,2},{2,3},{3,0},{4,5},{5,6},{6,7},{7,4},{8,9},{9,10},{10,1... | collective-permute-start | bytes 589832 | tf_op jit(solution)/shard_map/ppermute | solution.py:510
  137.7 6.5 %collective-permute-start.9 = (bf16[256,384]{1,0:T(8,128)(2,1)S(1)}, bf16[256,384]{1,0:T(8,128)(2,1)S(1)}, u32[]{:S(2)}, u32[]{:S(2)}) collective-permute-start(bf16[256,384]{1,0:T(8,128)(2,1)S(1)} %slice.9), channel_id=1, source_target_pairs={{0,3},{1,0},{2,1},{3,2},{4,7},{5,4},{6,5},{7,6},{8,11},{9,8},{10,9... | collective-permute-start | bytes 589832 | tf_op jit(solution)/shard_map/ppermute | solution.py:510
Sparse Core Ops, SparseCore 0:
  12.3 62.0 all-gather.2

commit v3 on v2

--- a/solution.py
+++ b/solution.py
@@ -20,6 +20,7 @@
 KV_AT = 384
 RATE_AT = 576
 Q_AT = 592
+CUT = 352
 EPSILON = 1e-06
 LOG2E = 1.4426950408889634
 RATE_SCALE = 0.1
@@ -66,7 +67,7 @@
 
 def spread_body(
     at_ref, x_ref, meta_ref, qkv_ref, out_ref, fast_ref, rate_ref,
-    o_ref, w_ref, buf, sems, wsems,
+    o_ref, low_ref, high_ref, buf, w_ref, sems, wsems, osem,
 ):
     head = at_ref[1]
     core = at_ref[2]
@@ -99,12 +100,20 @@
     for m in moves:
         m.start()
     o_ref[:, PAIRS * LT] = jnp.broadcast_to(meta_ref[...][None], (SEQ, 8, 128))
+    for m in moves:
+        m.wait()
+    outs = [
+        pltpu.make_async_copy(w_ref.at[pl.ds(0, CUT)], low_ref, osem.at[0]),
+        pltpu.make_async_copy(w_ref.at[pl.ds(CUT, WROWS - CUT)], high_ref, osem.at[1]),
+    ]
+    for c in outs:
+        c.start()
     for p in range(PAIRS):
         copies[p].wait()
         for t in range(LT):
             o_ref[:, p * LT + t] = buf[p, :, :, t * 128 : (t + 1) * 128]
-    for m in moves:
-        m.wait()
+    for c in outs:
+        c.wait()
 
 
 def spread(at, x, meta, *weights):
@@ -112,14 +121,17 @@
         spread_body,
         out_shape=(
             jax.ShapeDtypeStruct((SEQ, PAIRS * LT + 1, 8, 128), BF),
-            jax.ShapeDtypeStruct((WROWS, D), BF),
+            pltpu.HBM((CUT, D), BF),
+            pltpu.HBM((WROWS - CUT, D), BF),
         ),
         in_specs=[SMEM, ANY, VMEM] + [ANY] * 4,
-        out_specs=[VMEM] * 2,
+        out_specs=[VMEM, ANY, ANY],
         scratch_shapes=[
             pltpu.VMEM((PAIRS, SEQ, 8, FH), BF),
+            pltpu.VMEM((WROWS, D), BF),
             pltpu.SemaphoreType.DMA((PAIRS,)),
             pltpu.SemaphoreType.DMA((5,)),
+            pltpu.SemaphoreType.DMA((2,)),
         ],
         compiler_params=params(12),
         cost_estimate=cost(3),
@@ -154,6 +166,7 @@
         table[q // PAIRS, 16 + slot] == table[q // PAIRS, 17 + slot], 1, 0
     )
     flag_ref[2] = at_ref[1]
+    flag_ref[3] = at_ref[2]
 
 
 def pick(at, x):
@@ -161,7 +174,7 @@
         pick_body,
         out_shape=(
             jax.ShapeDtypeStruct((SEQ * HEADS, LT, 8, 128), BF),
-            jax.ShapeDtypeStruct((3,), jnp.int32),
+            jax.ShapeDtypeStruct((4,), jnp.int32),
         ),
         in_specs=[SMEM, VMEM],
         out_specs=[VMEM, SMEM],
@@ -175,6 +188,25 @@
         cost_estimate=cost(3),
         name="pick",
     )(at, x)
+
+
+def weight_copies(core, w_refs, d, start, count, dst, sem):
+    copies = []
+    low = max(0, min(count, CUT - start))
+    for side in range(2):
+        to = dst.at[core if side == 0 else 1 - core]
+        low_ref, high_ref = w_refs[side * 8 + d * 2 : side * 8 + d * 2 + 2]
+        pieces = [(low_ref, start, 0, low), (high_ref, start + low - CUT, low, count - low)]
+        for ref, at, put, n in pieces:
+            if n:
+                copies.append(
+                    pltpu.make_async_copy(ref.at[pl.ds(at, n)], to.at[pl.ds(put, n)], sem)
+                )
+    return copies
+
+
+def wait_all(dst, sem):
+    pltpu.make_async_copy(dst, dst, sem).wait()
 
 
 def attend(block, bias, q, k, v):
@@ -193,20 +225,11 @@
     return out.astype(BF)
 
 
-def key_copies(head, w_ref, fs, sems):
-    return [
-        pltpu.make_async_copy(
-            w_ref.at[:, lax.rem(head + d, HEADS), pl.ds(KV_AT, FW + 16)], fs.at[d], sems.at[d]
-        )
-        for d in range(HEADS)
-    ]
-
-
-def project(block, gain, copies, fs, kv_refs):
+def project(block, gain, fs, fsems, kv_refs):
     n = norm(block.astype(F32), gain)
     lane = lax.broadcasted_iota(jnp.int32, (BLK, 2 * FW), 1)
-    for c in copies:
-        c.wait()
+    for d in range(HEADS):
+        wait_all(fs.at[d], fsems.at[d])
     z = mm_nt(n, jnp.concatenate([fs[d, 0, FW:] for d in range(HEADS)], axis=0))
     soft = jnp.maximum(z, 0.0) + jnp.log1p(jnp.exp(-jnp.abs(z)))
     rates = -(RATE_SCALE * VTOKENS**-0.5) * soft
@@ -216,17 +239,18 @@
 
 
 def encode_first_body(
-    flag_ref, x_ref, gain_ref, fgain_ref, w_ref,
-    o_ref, kv0, kv1, kv2, kv3, q_ref, k_ref, v_ref, rest_ref,
-    xs, ns, ws, fs, sems, fsems,
+    flag_ref, x_ref, gain_ref, fgain_ref, *refs
 ):
-    copies = [
-        pltpu.make_async_copy(w_ref.at[:, g, pl.ds(0, FH)], ws.at[g], sems.at[g])
-        for g in range(HEADS)
-    ]
-    later = key_copies(flag_ref[2], w_ref, fs, fsems)
-    for c in copies + later:
-        c.start()
+    w_refs = refs[:16]
+    o_ref, kv0, kv1, kv2, kv3, q_ref, k_ref, v_ref, rest_ref = refs[16:25]
+    xs, ns, ws, fs, sems, fsems = refs[25:]
+    core = flag_ref[3]
+    for d in range(HEADS):
+        for c in weight_copies(core, w_refs, d, 0, FH, ws.at[d], sems.at[d]):
+            c.start()
+    for d in range(HEADS):
+        for c in weight_copies(core, w_refs, d, KV_AT, FW + 16, fs.at[d], fsems.at[d]):
+            c.start()
     flip = flag_ref[0]
     bias = jnp.where(flag_ref[1] != 0, 0.0, -1e30).astype(F32)
     for b in range(2):
@@ -244,7 +268,7 @@
     scale = HDIM**-0.5 * LOG2E
     out = xs[:BLK, :]
     for g in range(HEADS):
-        copies[g].wait()
+        wait_all(ws.at[g], sems.at[g])
         w = ws[g, :, : 3 * 96].reshape(3 * FW, D)
         q = (mm_nt(n, w[:FW]) * scale).astype(BF)
         k = mm_nt(n, w[FW : 2 * FW]).astype(BF)
@@ -258,10 +282,10 @@
         out = out + mm(att, ws[g, :, 3 * 96 :].reshape(FW, D))
     out = out.astype(BF)
     o_ref[...] = out
-    project(out, fgain_ref[...], later, fs, (kv0, kv1, kv2, kv3))
-
-
-def encode_first(flags, x, gain, fgain, w):
+    project(out, fgain_ref[...], fs, fsems, (kv0, kv1, kv2, kv3))
+
+
+def encode_first(flags, x, gain, fgain, weights):
     return pl.pallas_call(
         encode_first_body,
         out_shape=(
@@ -272,7 +296,7 @@
             jax.ShapeDtypeStruct((HEADS, SPAN, FW + HDIM), BF),
             jax.ShapeDtypeStruct((BLK, D), BF),
         ),
-        in_specs=[SMEM, VMEM, VMEM, VMEM, ANY],
+        in_specs=[SMEM, VMEM, VMEM, VMEM] + [ANY] * 16,
         out_specs=[VMEM] * 9,
         scratch_shapes=[
             pltpu.VMEM((SPAN, D), F32),
@@ -285,41 +309,44 @@
         compiler_params=params(24),
         cost_estimate=cost(9),
         name="encode_first",
-    )(flags, x, gain, fgain, w)
+    )(flags, x, gain, fgain, *weights)
 
 
 def encode_second_body(
-    flag_ref, fgain_ref, q_ref, k_ref, v_ref, rest_ref, w_ref,
-    o_ref, kv0, kv1, kv2, kv3, ws, fs, sem, fsems,
+    flag_ref, fgain_ref, q_ref, k_ref, v_ref, rest_ref, *refs
 ):
-    copy = pltpu.make_async_copy(w_ref.at[:, :, pl.ds(3 * 96, 96)], ws, sem)
-    copy.start()
-    later = key_copies(flag_ref[2], w_ref, fs, fsems)
-    for c in later:
-        c.start()
+    w_refs = refs[:16]
+    o_ref, kv0, kv1, kv2, kv3, ws, fs, sem, fsems = refs[16:]
+    core = flag_ref[3]
+    for d in range(HEADS):
+        for c in weight_copies(core, w_refs, d, 3 * 96, 96, ws.at[d], sem):
+            c.start()
+    for d in range(HEADS):
+        for c in weight_copies(core, w_refs, d, KV_AT, FW + 16, fs.at[d], fsems.at[d]):
+            c.start()
     bias = jnp.where(flag_ref[1] != 0, 0.0, -1e30).astype(F32)
     out = rest_ref[...].astype(F32)
     for g in range(HEADS):
         att = attend(1, bias, q_ref[g], k_ref[g], v_ref[g])
         if g == 0:
-            copy.wait()
-        out = out + mm(att, ws[:, g].reshape(FW, D))
+            wait_all(ws, sem)
+        out = out + mm(att, ws[g].reshape(FW, D))
     out = out.astype(BF)
     o_ref[...] = out
-    project(out, fgain_ref[...], later, fs, (kv0, kv1, kv2, kv3))
-
-
-def encode_second(flags, fgain, q, k, v, rest, w):
+    project(out, fgain_ref[...], fs, fsems, (kv0, kv1, kv2, kv3))
+
+
+def encode_second(flags, fgain, q, k, v, rest, weights):
     return pl.pallas_call(
         encode_second_body,
         out_shape=(
             jax.ShapeDtypeStruct((BLK, D), BF),
             *[jax.ShapeDtypeStruct((BLK, 2 * FW), BF)] * HEADS,
         ),
-        in_specs=[SMEM, VMEM, VMEM, VMEM, VMEM, VMEM, ANY],
+        in_specs=[SMEM] + [VMEM] * 5 + [ANY] * 16,
         out_specs=[VMEM] * 5,
         scratch_shapes=[
-            pltpu.VMEM((2, HEADS, 96, D), BF),
+            pltpu.VMEM((HEADS, 2, 96, D), BF),
             pltpu.VMEM((HEADS, 2, FW + 16, D), BF),
             pltpu.SemaphoreType.DMA(()),
             pltpu.SemaphoreType.DMA((HEADS,)),
@@ -327,27 +354,23 @@
         compiler_params=params(16),
         cost_estimate=cost(20),
         name="encode_second",
-    )(flags, fgain, q, k, v, rest, w)
-
-
-def query_body(flag_ref, x0_ref, x1_ref, gain_ref, w_ref, *refs):
-    own_ref, up_ref, down_ref, ws, sems = refs
+    )(flags, fgain, q, k, v, rest, *weights)
+
+
+def query_body(flag_ref, x0_ref, x1_ref, gain_ref, *refs):
+    w_refs = refs[:16]
+    own_ref, up_ref, down_ref, ws, sems = refs[16:]
     whole = {0: own_ref, 1: up_ref, 3: down_ref}
     head = flag_ref[2]
-    copies = [
-        pltpu.make_async_copy(
-            w_ref.at[:, lax.rem(head + d, HEADS), pl.ds(Q_AT, 96)], ws.at[d], sems.at[d]
-        )
-        for d in range(HEADS)
-    ]
-    for c in copies:
-        c.start()
+    for d in range(HEADS):
+        for c in weight_copies(flag_ref[3], w_refs, d, Q_AT, 96, ws.at[d], sems.at[d]):
+            c.start()
     xs = (x0_ref[...], x1_ref[...])
     ns = [norm(x.astype(F32), gain_ref[...]) for x in xs]
     cols = [[x[:, g * FW : (g + 1) * FW] for g in range(HEADS)] for x in xs]
     for d in range(HEADS):
         there = lax.rem(head + d, HEADS)
-        copies[d].wait()
+        wait_all(ws.at[d], sems.at[d])
         w = ws[d].reshape(FW, D)
         for i in range(2):
             q = mm_nt(ns[i], w).astype(BF)
@@ -362,7 +385,7 @@
                 whole[d][pl.ds(i * BLK, BLK), :] = qe
 
 
-def query(flags, x0, x1, gain, w):
+def query(flags, x0, x1, gain, weights):
     return pl.pallas_call(
         query_body,
         out_shape=(
@@ -370,7 +393,7 @@
             jax.ShapeDtypeStruct((SPAN + BLK, 2 * FW), BF),
             jax.ShapeDtypeStruct((SPAN + BLK, 2 * FW), BF),
         ),
-        in_specs=[SMEM, VMEM, VMEM, VMEM, ANY],
+        in_specs=[SMEM, VMEM, VMEM, VMEM] + [ANY] * 16,
         out_specs=[VMEM] * 3,
         scratch_shapes=[
             pltpu.VMEM((HEADS, 2, 96, D), BF),
@@ -379,7 +402,7 @@
         compiler_params=params(12),
         cost_estimate=cost(4),
         name="fast_query",
-    )(flags, x0, x1, gain, w)
+    )(flags, x0, x1, gain, *weights)
 
 
 def make_fast_body(blocks, first, last):
@@ -510,6 +533,10 @@
     return lax.ppermute(x, "head", [(i, (i + by) % HEADS) for i in range(HEADS)])
 
 
+def swapped(x):
+    return lax.ppermute(x, "core", [(0, 1), (1, 0)])
+
+
 def on_device(
     patches,
     slot_image,
@@ -530,7 +557,7 @@
 
     ids = jnp.concatenate([slot_dest, slot_image]).astype(BF)
     tile = jnp.pad(ids[None, :], ((0, 7), (0, 96)))
-    pieces, rows = spread(
+    pieces, low, high = spread(
         at,
         patches.reshape(-1, 8, D),
         tile,
@@ -539,10 +566,14 @@
         jnp.transpose(w_fast, (0, 2, 1)).reshape(3 * FW, D),
         jnp.broadcast_to(w_rate.T, (16, D)),
     )
-    weights = lax.all_gather(rows, ("core", "head"), axis=0, tiled=False)
-    weights = in_hbm(weights.reshape(2, HEADS, WROWS, D))
+    before = (shifted(low, 1), shifted(high, 1))
+    after = (shifted(low, -1), shifted(high, -1))
     picked, flags = pick(at, exchange(pieces, SEQ_AXES))
+    picked, before, after = lax.optimization_barrier((picked, before, after))
     mine = exchange(picked, ALL_AXES)
+    far = (shifted(before[0], 1), shifted(after[1], -1))
+    weights = (low, high, *after, *far, *before)
+    weights = [in_hbm(w) for w in weights + tuple(swapped(w) for w in weights)]
 
     fgain = fast_gain.reshape(1, D)
     own_0, *outs = encode_first(

time: 159 us -> 151 us (0.950)
  blocking collectives: 32.7 us -> 0 us
  starting transfers between devices: 31.5 us -> 62.9 us
  between operations: 13.6 us -> 0.33 us
  waiting for transfers between devices: 36.2 us -> 39.7 us
  local copies, waits for them, and re-layouts: 0.68 us -> 2.28 us
    all_to_all x1 -> x0, blocking collectives: 32.7 us -> none  [exchange(): return lax.all_to_all(x, axes, split_axis=0, concat_axis=0, tiled=True)]
    ppermute x0 -> x8, starting transfers between devices: none -> 12.8 us  [swapped(): return lax.ppermute(x, 'core', [(0, 1), (1, 0)])]
    all_to_all x3 -> x4, starting transfers between devices: 17.8 us -> 27.1 us  [exchange(): return lax.all_to_all(x, axes, split_axis=0, concat_axis=0, tiled=True)]
    ppermute x10 -> x16, starting transfers between devices: 13.7 us -> 23 us  [shifted(): lax.ppermute(x, 'head', [(i, (i + by) % HEADS) for i in range(HEADS)])]
    ppermute x10 -> x16, waiting for transfers between devices: 7.23 us -> 9.67 us  [shifted(): lax.ppermute(x, 'head', [(i, (i + by) % HEADS) for i in range(HEADS)])]
    unnamed x8 -> x22, local copies, waits for them, and re-layouts: 0.01 us -> 1.61 us
    all_to_all x3 -> x4, waiting for transfers between devices: 28.9 us -> 30 us  [exchange(): return lax.all_to_all(x, axes, split_axis=0, concat_axis=0, tiled=True)]
  transfers between devices with their start and end apart: 14 -> 28, of which waited for: 9 -> 9; matrix products, arithmetic and copies ran while one was open for 0% -> 0% of each run, Pallas kernels for 14% -> 14%
where the time goes in v3:
time: 151 us; the launch traced here: 150 us
  starting transfers between devices  62.9 us (42%)
  Pallas kernels  43.6 us (29%)
  waiting for transfers between devices  39.7 us (26%)
  local copies, waits for them, and re-layouts  2.28 us (2%)
  other arithmetic  1.54 us (1%)
    all_to_all x4, waiting for transfers between devices, exchange(): return lax.all_to_all(x, axes, split_axis=0, concat_axis=0, tiled=True)  30 us
    all_to_all x4, starting transfers between devices, exchange(): return lax.all_to_all(x, axes, split_axis=0, concat_axis=0, tiled=True)  27.1 us
    ppermute x16, starting transfers between devices, shifted(): lax.ppermute(x, 'head', [(i, (i + by) % HEADS) for i in range(HEADS)])  23 us
    ppermute x8, starting transfers between devices, swapped(): return lax.ppermute(x, 'core', [(0, 1), (1, 0)])  12.8 us
    pallas_call x1, Pallas kernels, encode_first(): pl.pallas_call(encode_first_body, out_shape=(jax.ShapeDtypeStruct((BLK, D...  10.9 us
    ppermute x16, waiting for transfers between devices, shifted(): lax.ppermute(x, 'head', [(i, (i + by) % HEADS) for i in range(HEADS)])  9.67 us
    pallas_call x1, Pallas kernels, encode_second(): pl.pallas_call(encode_second_body, out_shape=(jax.ShapeDtypeStruct((BLK,...  6.99 us
    pallas_call x1, Pallas kernels, pick(): pl.pallas_call(pick_body, out_shape=(jax.ShapeDtypeStruct((SEQ * HEADS, L...  6.67 us
  transfers between devices with their start and end apart: 28, of which 9 were waited for; matrix products, arithmetic and copies ran while one was open for 0% of the time, Pallas kernels for 14%

profile of v3, /device:TPU:1, one launch (start us, length us, event | category | flops | bytes accessed | tf_op | source)
XLA Modules:
  0.0 150.3 jit_solution(11146893917060034937)
XLA Ops:
  0.0 0.7 convert_bitcast_fusion
  0.7 0.1 fusion.5.meta_ref
  0.8 0.7 reduce
  1.5 0.1 pad_add_fusion.at_ref
  1.5 0.6 broadcast_in_dim.9.rate_ref
  2.2 4.6 %spread.1 = (bf16[32,25,8,128]{3,2,1,0:T(8,128)(2,1)}, bf16[352,768]{1,0:T(8,128)(2,1)}, bf16[336,768]{1,0:T(8,128)(2,1)}) custom-call(s32[3]{0:T(128)S(1)} %pad_add_fusion.at_ref, bf16[512,8,768]{2,1,0:T(8,128)(2,1)} %bitcast.33, bf16[8,128]{1,0:T(8,128)(2,1)S(1)} %fusion.5.meta_ref, bf16[576,768]{1,0:T(8,128)(2,1)} %bitcast.34, bf16[192,768]{1,0:T(8,128)(2,1)} %out_ref.1, ...), custom_call_target="tpu_custom_call" | custom-call | bytes 10800000 | tf_op jit(solution)/shard_map/spread/pallas_call | solution.py:120
  6.8 9.6 %all-to-all-start = ((bf16[32,25,8,128]{3,2,1,0:T(8,128)(2,1)}), bf16[32,25,8,128]{3,2,1,0:T(8,128)(2,1)S(1)}, u32[]{:S(2)}, u32[]{:S(2)}) async-start(bf16[32,25,8,128]{3,2,1,0:T(8,128)(2,1)} %get-tuple-element.45), calls=%async_computation | async-start | bytes 3276800 | tf_op jit(solution)/shard_map/all_to_all | solution.py:529
  16.4 0.0 copy-start.9
  16.4 0.0 copy-start.10
  16.4 2.8 %collective-permute-start.2 = (bf16[352,768]{1,0:T(8,128)(2,1)S(1)}, bf16[352,768]{1,0:T(8,128)(2,1)S(1)}, u32[]{:S(2)}, u32[]{:S(2)}) collective-permute-start(bf16[352,768]{1,0:T(8,128)(2,1)S(1)} %copy-done.2), channel_id=1, source_target_pairs={{0,3},{1,0},{2,1},{3,2},{4,7},{5,4},{6,5},{7,6},{8,11},{9,8},{10,9... | collective-permute-start | bytes 1622024 | tf_op jit(solution)/shard_map/ppermute | solution.py:533
  19.2 0.0 collective-permute-start
  19.2 2.7 %collective-permute-start.3 = (bf16[336,768]{1,0:T(8,128)(2,1)}, bf16[336,768]{1,0:T(8,128)(2,1)}, u32[]{:S(2)}, u32[]{:S(2)}) collective-permute-start(bf16[336,768]{1,0:T(8,128)(2,1)} %get-tuple-element.49.refs_1_), channel_id=1, source_target_pairs={{0,3},{1,0},{2,1},{3,2},{4,7},{5,4},{6,5},{7,6},{8,11},{9,8},{10,9... | collective-permute-start | bytes 1548296 | tf_op jit(solution)/shard_map/ppermute | solution.py:533
  21.9 1.1 collective-permute-start.6
  23.0 16.8 %all-to-all-done.x_ref = bf16[32,25,8,128]{3,2,1,0:T(8,128)(2,1)S(1)} async-done(((bf16[32,25,8,128]{3,2,1,0:T(8,128)(2,1)}), bf16[32,25,8,128]{3,2,1,0:T(8,128)(2,1)S(1)}, u32[]{:S(2)}, u32[]{:S(2)}) %all-to-all-start) | async-done | bytes 1638432 | tf_op jit(solution)/shard_map/all_to_all | solution.py:529
  39.8 6.7 %pick.1 = (bf16[128,3,8,128]{3,2,1,0:T(8,128)(2,1)}, s32[4]{0:T(128)S(1)}) custom-call(s32[3]{0:T(128)S(1)} %pad_add_fusion.at_ref, bf16[32,25,8,128]{3,2,1,0:T(8,128)(2,1)S(1)} %all-to-all-done.x_ref), custom_call_target="tpu_custom_call" | custom-call | bytes 10800000 | tf_op jit(solution)/shard_map/pick/pallas_call | solution.py:173
  46.4 0.0 collective-permute-done.3.refs_3_
  46.5 0.0 collective-permute-done.refs_6_
  46.5 1.4 collective-permute-start.4
  47.9 1.0 collective-permute-start.7
  48.8 0.0 collective-permute-start.13
  48.8 1.4 collective-permute-start.5
  50.2 6.3 %all-to-all-start.1 = ((bf16[128,3,8,128]{3,2,1,0:T(8,128)(2,1)}), bf16[128,3,8,128]{3,2,1,0:T(8,128)(2,1)S(1)}, u32[]{:S(2)}, u32[]{:S(2)}) async-start(bf16[128,3,8,128]{3,2,1,0:T(8,128)(2,1)} %get-tuple-element.50), calls=%async_computation.1 | async-start | bytes 1572864 | tf_op jit(solution)/shard_map/all_to_all | solution.py:529
  56.6 0.0 collective-permute-done.7.refs_9_
  56.6 1.1 collective-permute-start.8
  57.7 0.0 collective-permute-done.6.refs_8_
  57.7 0.1 collective-permute-start.12
  57.8 3.2 %collective-permute-done.4.refs_4_ = bf16[352,768]{1,0:T(8,128)(2,1)S(1)} collective-permute-done((bf16[352,768]{1,0:T(8,128)(2,1)S(1)}, bf16[352,768]{1,0:T(8,128)(2,1)S(1)}, u32[]{:S(2)}, u32[]{:S(2)}) %collective-permute-start.4) | collective-permute-done | bytes 540704 | tf_op jit(solution)/shard_map/ppermute | solution.py:533
  61.1 6.6 %collective-permute-start.10 = (bf16[352,768]{1,0:T(8,128)(2,1)S(1)}, bf16[352,768]{1,0:T(8,128)(2,1)}, u32[]{:S(2)}, u32[]{:S(2)}) collective-permute-start(bf16[352,768]{1,0:T(8,128)(2,1)S(1)} %collective-permute-done.4.refs_4_), channel_id=1, source_target_pairs={{0,4},{4,0},{1,5},{5,1},{2,6},{6,2},{3,7},{7,3},{8,12},{12,8},{9,1... | collective-permute-start | bytes 1622024 | tf_op jit(solution)/shard_map/ppermute | solution.py:537
  67.7 0.0 collective-permute-done.13.refs_15_
  67.7 0.1 collective-permute-start.9
  67.8 0.0 collective-permute-done.5.refs_5_
  67.8 2.8 %collective-permute-start.11 = (bf16[336,768]{1,0:T(8,128)(2,1)}, bf16[336,768]{1,0:T(8,128)(2,1)}, u32[]{:S(2)}, u32[]{:S(2)}) collective-permute-start(bf16[336,768]{1,0:T(8,128)(2,1)} %collective-permute-done.5.refs_5_), channel_id=1, source_target_pairs={{0,4},{4,0},{1,5},{5,1},{2,6},{6,2},{3,7},{7,3},{8,12},{12,8},{9,1... | collective-permute-start | bytes 1548296 | tf_op jit(solution)/shard_map/ppermute | solution.py:537
  70.6 0.0 collective-permute-done.9.refs_11_
  70.7 0.8 copy-done.8
  71.4 0.8 copy-done.6
  72.2 0.0 collective-permute-done.12.refs_14_
  72.2 1.3 all-to-all-done.1
  73.5 0.0 collective-permute-done.11.refs_13_
  73.6 10.9 %encode_first.1 = (bf16[256,768]{1,0:T(8,128)(2,1)S(1)}, bf16[256,384]{1,0:T(8,128)(2,1)S(1)}, bf16[256,384]{1,0:T(8,128)(2,1)S(1)}, bf16[256,384]{1,0:T(8,128)(...) custom-call(s32[4]{0:T(128)S(1)} %get-tuple-element.46.flag_ref.head, ...), custom_call_target="tpu_custom_call" | custom-call | bytes 32400000 | tf_op jit(solution)/shard_map/encode_first/pallas_call | solution.py:289
  84.5 1.3 collective-permute-start.14
  85.8 2.6 %collective-permute-start.15 = (bf16[256,384]{1,0:T(8,128)(2,1)S(1)}, bf16[256,384]{1,0:T(8,128)(2,1)S(1)}, u32[]{:S(2)}, u32[]{:S(2)}) collective-permute-start(bf16[256,384]{1,0:T(8,128)(2,1)S(1)} %get-tuple-element.64), channel_id=1, source_target_pairs={{0,2},{1,3},{2,0},{3,1},{4,6},{5,7},{6,4},{7,5},{8,10},{9,11},{10,... | collective-permute-start | bytes 589832 | tf_op jit(solution)/shard_map/ppermute | solution.py:533
  88.4 1.1 collective-permute-start.16
  89.6 7.0 %encode_second.1 = (bf16[256,768]{1,0:T(8,128)(2,1)S(1)}, bf16[256,384]{1,0:T(8,128)(2,1)S(1)}, bf16[256,384]{1,0:T(8,128)(2,1)S(1)}, bf16[256,384]{1,0:T(8,128)(2,1)S(1)}, bf16[256,384]{1,0:T(8,128)(2,1)S(1)}) custom-call(s32[4]{0:T(128)S(1)} %get-tuple-element.46.flag_ref.head_ref, f32[1,768]{1,0:T(1,128)S(1)} %reshape.59.fgain_ref.gain_ref, ...), custom_call_target="tpu_custom_call" | custom-call | bytes 72000000 | tf_op jit(solution)/shard_map/encode_second/pallas_call | solution.py:340
  96.6 0.7 collective-permute-done.15.refs_1_
  97.3 0.9 collective-permute-start.17
  98.2 2.9 %collective-permute-start.18 = (bf16[256,384]{1,0:T(8,128)(2,1)S(1)}, bf16[256,384]{1,0:T(8,128)(2,1)S(1)}, u32[]{:S(2)}, u32[]{:S(2)}) collective-permute-start(bf16[256,384]{1,0:T(8,128)(2,1)S(1)} %get-tuple-element.67), channel_id=1, source_target_pairs={{0,2},{1,3},{2,0},{3,1},{4,6},{5,7},{6,4},{7,5},{8,10},{9,11},{10,... | collective-permute-start | bytes 589832 | tf_op jit(solution)/shard_map/ppermute | solution.py:533
  101.1 0.4 collective-permute-start.19
  101.5 4.0 %fast_query.1 = (bf16[512,384]{1,0:T(8,128)(2,1)S(1)}, bf16[768,384]{1,0:T(8,128)(2,1)S(1)}, bf16[768,384]{1,0:T(8,128)(2,1)}) custom-call(s32[4]{0:T(128)S(1)} %get-tuple-element.46.flag_ref.head_ref, bf16[256,768]{1,0:T(8,128)(2,1)S(1)} %get-tuple-element.69.x0_ref, bf16[256,768]{1,0:T(8,128)(2,1)S(1)} %get-tuple-element.70.x1_ref, ...), custom_call_target="tpu_custom_call" | custom-call | bytes 14400000 | tf_op jit(solution)/shard_map/fast_query/pallas_call | solution.py:389
  105.5 1.2 fast_grad.3.refs_5_
  106.6 1.7 %fast_grad.4.refs_5_ = f32[3,192,384]{2,1,0:T(8,128)S(1)} custom-call(bf16[256,384]{1,0:T(8,128)(2,1)S(1)} %collective-permute-done.14.refs_0_, bf16[256,384]{1,0:T(8,128)(2,1)S(1)} %collective-permute-done.15.refs_1_, bf16[256,384]{1,0:T(8,128)(2,1)S(1)} %collective-permute-done.16.refs_2_, f32[2,192,384]{2,1,0:T(8,128)S(1)} %bitcast.23, ...), custom_call_target="tpu_custom_call" | custom-call | bytes 10800000 | tf_op jit(solution)/shard_map/fast_grad/pallas_call | solution.py:449
  108.4 1.4 collective-permute-done.18.refs_1_
  109.8 2.5 %fast_grad.5 = bf16[224,8,128]{2,1,0:T(8,128)(2,1)} custom-call(bf16[256,384]{1,0:T(8,128)(2,1)S(1)} %collective-permute-done.17.refs_0_, bf16[256,384]{1,0:T(8,128)(2,1)S(1)} %collective-permute-done.18.refs_1_, bf16[256,384]{1,0:T(8,128)(2,1)S(1)} %collective-permute-done.19.refs_2_, f32[2,192,384]{2,1,0:T(8,128)S(1)} %bitcast.24, ...), custom_call_target="tpu_custom_call" | custom-call | bytes 10800000 | tf_op jit(solution)/shard_map/fast_grad/pallas_call | solution.py:449
  112.3 7.5 %all-to-all-start.2 = ((bf16[224,8,128]{2,1,0:T(8,128)(2,1)}), bf16[224,8,128]{2,1,0:T(8,128)(2,1)S(1)}, u32[]{:S(2)}, u32[]{:S(2)}) async-start(bf16[224,8,128]{2,1,0:T(8,128)(2,1)} %fast_grad.5), calls=%async_computation.2 | async-start | bytes 917504 | tf_op jit(solution)/shard_map/all_to_all | solution.py:529
  119.8 0.1 collective-permute-start.20
  119.9 2.7 %collective-permute-start.21 = (bf16[768,384]{1,0:T(8,128)(2,1)}, bf16[768,384]{1,0:T(8,128)(2,1)S(1)}, u32[]{:S(2)}, u32[]{:S(2)}) collective-permute-start(bf16[768,384]{1,0:T(8,128)(2,1)} %get-tuple-element.84), channel_id=1, source_target_pairs={{0,3},{1,0},{2,1},{3,2},{4,7},{5,4},{6,5},{7,6},{8,11},{9,8},{10,9... | collective-permute-start | bytes 1769480 | tf_op jit(solution)/shard_map/ppermute | solution.py:533
  122.5 8.2 %all-to-all-done.2 = bf16[224,8,128]{2,1,0:T(8,128)(2,1)S(1)} async-done(((bf16[224,8,128]{2,1,0:T(8,128)(2,1)}), bf16[224,8,128]{2,1,0:T(8,128)(2,1)S(1)}, u32[]{:S(2)}, u32[]{:S(2)}) %all-to-all-start.2) | async-done | bytes 458784 | tf_op jit(solution)/shard_map/all_to_all | solution.py:529
  130.7 0.8 sum_pieces.1
  131.6 3.7 %all-to-all-start.3 = ((bf16[32,7,8,128]{3,2,1,0:T(8,128)(2,1)}), bf16[32,7,8,128]{3,2,1,0:T(8,128)(2,1)S(1)}, u32[]{:S(2)}, u32[]{:S(2)}) async-start(bf16[32,7,8,128]{3,2,1,0:T(8,128)(2,1)} %sum_pieces.1), calls=%async_computation.3 | async-start | bytes 917504 | tf_op jit(solution)/shard_map/all_to_all | solution.py:529
  135.3 0.5 collective-permute-done.20.refs_1_
  135.8 0.1 collective-permute-start.22
  135.9 2.7 %collective-permute-start.23 = (bf16[256,384]{1,0:T(8,128)(2,1)S(1)}, bf16[256,384]{1,0:T(8,128)(2,1)S(1)}, u32[]{:S(2)}, u32[]{:S(2)}) collective-permute-start(bf16[256,384]{1,0:T(8,128)(2,1)S(1)} %slice.9), channel_id=1, source_target_pairs={{0,3},{1,0},{2,1},{3,2},{4,7},{5,4},{6,5},{7,6},{8,11},{9,8},{10,9... | collective-permute-start | bytes 589832 | tf_op jit(solution)/shard_map/ppermute | solution.py:533
  138.6 3.8 %collective-permute-done.22.refs_3_ = bf16[256,384]{1,0:T(8,128)(2,1)S(1)} collective-permute-done((bf16[256,384]{1,0:T(8,128)(2,1)S(1)}, bf16[256,384]{1,0:T(8,128)(2,1)S(1)}, u32[]{:S(2)}, u32[]{:S(2)}) %collective-permute-start.22) | collective-permute-done | bytes 196640 | tf_op jit(solution)/shard_map/ppermute | solution.py:533
  142.4 3.7 %all-to-all-done.3 = bf16[32,7,8,128]{3,2,1,0:T(8,128)(2,1)S(1)} async-done(((bf16[32,7,8,128]{3,2,1,0:T(8,128)(2,1)}), bf16[32,7,8,128]{3,2,1,0:T(8,128)(2,1)S(1)}, u32[]{:S(2)}, u32[]{:S(2)}) %all-to-all-start.3) | async-done | bytes 458784 | tf_op jit(solution)/shard_map/all_to_all | solution.py:529
  146.1 4.2 %apply_fast.1 = bf16[192,2048]{1,0:T(8,128)(2,1)} custom-call(s32[4]{0:T(128)S(1)} %get-tuple-element.46.flag_ref.head_ref, bf16[224,8,128]{2,1,0:T(8,128)(2,1)S(1)} %bitcast.31, f32[2,192,384]{2,1,0:T(8,128)S(1)} %bitcast.25, f32[192,384]{1,0:T(8,128)S(1)} %bitcast.29, bf16[512,384]{1,0:T(8,128)(2,1)S(1)} %get-tuple-element.82.refs_0_, ...), custom_call_target="tpu_custom_call" | custom-call | bytes 10800000 | tf_op jit(solution)/shard_map/apply_fast/pallas_call | solution.py:516
  (33 shorter events, 0.1 us)
Async XLA Ops:
  6.8 9.6 %copy-start.2 = (bf16[352,768]{1,0:T(8,128)(2,1)S(1)}, bf16[352,768]{1,0:T(8,128)(2,1)}, u32[]{:S(2)}) copy-start(bf16[352,768]{1,0:T(8,128)(2,1)} %get-tuple-element.48.refs_0_) | copy-start | bytes 1622020
  6.8 33.0 %all-to-all-start = ((bf16[32,25,8,128]{3,2,1,0:T(8,128)(2,1)}), bf16[32,25,8,128]{3,2,1,0:T(8,128)(2,1)S(1)}, u32[]{:S(2)}, u32[]{:S(2)}) async-start(bf16[32,25,8,128]{3,2,1,0:T(8,128)(2,1)} %get-tuple-element.45), calls=%async_computation | async-start | bytes 3276800 | tf_op jit(solution)/shard_map/all_to_all | solution.py:529
  16.4 54.2 %copy-start.9 = (f32[768]{0:T(1024)S(1)}, f32[768]{0:T(1024)}, u32[]{:S(2)}) copy-start(f32[768]{0:T(1024)} %param.17) | copy-start | bytes 9220
  16.4 54.2 %copy-start.10 = (f32[768]{0:T(1024)S(1)}, f32[768]{0:T(1024)}, u32[]{:S(2)}) copy-start(f32[768]{0:T(1024)} %param.14) | copy-start | bytes 9220
  16.4 30.0 %collective-permute-start.2 = (bf16[352,768]{1,0:T(8,128)(2,1)S(1)}, bf16[352,768]{1,0:T(8,128)(2,1)S(1)}, u32[]{:S(2)}, u32[]{:S(2)}) collective-permute-start(bf16[352,768]{1,0:T(8,128)(2,1)S(1)} %copy-done.2), channel_id=1, source_target_pairs={{0,3},{1,0},{2,1},{3,2},{4,7},{5,4},{6,5},{7,6},{8,11},{9,8},{10,9... | collective-permute-start | bytes 1622024 | tf_op jit(solution)/shard_map/ppermute | solution.py:533
  19.2 27.3 %collective-permute-start = (bf16[352,768]{1,0:T(8,128)(2,1)S(1)}, bf16[352,768]{1,0:T(8,128)(2,1)S(1)}, u32[]{:S(2)}, u32[]{:S(2)}) collective-permute-start(bf16[352,768]{1,0:T(8,128)(2,1)S(1)} %copy-done.2), channel_id=1, source_target_pairs={{0,1},{1,2},{2,3},{3,0},{4,5},{5,6},{6,7},{7,4},{8,9},{9,10},{10,1... | collective-permute-start | bytes 1622024 | tf_op jit(solution)/shard_map/ppermute | solution.py:533
  19.2 27.2 %collective-permute-start.3 = (bf16[336,768]{1,0:T(8,128)(2,1)}, bf16[336,768]{1,0:T(8,128)(2,1)}, u32[]{:S(2)}, u32[]{:S(2)}) collective-permute-start(bf16[336,768]{1,0:T(8,128)(2,1)} %get-tuple-element.49.refs_1_), channel_id=1, source_target_pairs={{0,3},{1,0},{2,1},{3,2},{4,7},{5,4},{6,5},{7,6},{8,11},{9,8},{10,9... | collective-permute-start | bytes 1548296 | tf_op jit(solution)/shard_map/ppermute | solution.py:533
  21.9 24.5 %collective-permute-start.1 = (bf16[336,768]{1,0:T(8,128)(2,1)}, bf16[336,768]{1,0:T(8,128)(2,1)}, u32[]{:S(2)}, u32[]{:S(2)}) collective-permute-start(bf16[336,768]{1,0:T(8,128)(2,1)} %get-tuple-element.49.refs_1_), channel_id=1, source_target_pairs={{0,1},{1,2},{2,3},{3,0},{4,5},{5,6},{6,7},{7,4},{8,9},{9,10},{10,1... | collective-permute-start | bytes 1548296 | tf_op jit(solution)/shard_map/ppermute | solution.py:533
  21.9 35.8 %collective-permute-start.6 = (bf16[352,768]{1,0:T(8,128)(2,1)S(1)}, bf16[352,768]{1,0:T(8,128)(2,1)}, u32[]{:S(2)}, u32[]{:S(2)}) collective-permute-start(bf16[352,768]{1,0:T(8,128)(2,1)S(1)} %copy-done.2), channel_id=1, source_target_pairs={{0,4},{4,0},{1,5},{5,1},{2,6},{6,2},{3,7},{7,3},{8,12},{12,8},{9,1... | collective-permute-start | bytes 1622024 | tf_op jit(solution)/shard_map/ppermute | solution.py:537
  46.5 27.1 %copy-start.3 = (bf16[352,768]{1,0:T(8,128)(2,1)}, bf16[352,768]{1,0:T(8,128)(2,1)S(1)}, u32[]{:S(2)}) copy-start(bf16[352,768]{1,0:T(8,128)(2,1)S(1)} %collective-permute-done.2.refs_2_) | copy-start | bytes 1622020
  46.5 27.1 %copy-start.4 = (bf16[352,768]{1,0:T(8,128)(2,1)}, bf16[352,768]{1,0:T(8,128)(2,1)S(1)}, u32[]{:S(2)}) copy-start(bf16[352,768]{1,0:T(8,128)(2,1)S(1)} %collective-permute-done.refs_6_) | copy-start | bytes 1622020
  46.5 14.6 %collective-permute-start.4 = (bf16[352,768]{1,0:T(8,128)(2,1)S(1)}, bf16[352,768]{1,0:T(8,128)(2,1)S(1)}, u32[]{:S(2)}, u32[]{:S(2)}) collective-permute-start(bf16[352,768]{1,0:T(8,128)(2,1)S(1)} %collective-permute-done.refs_6_), channel_id=1, source_target_pairs={{0,1},{1,2},{2,3},{3,0},{4,5},{5,6},{6,7},{7,4},{8,9},{9,10},{10,1... | collective-permute-start | bytes 1622024 | tf_op jit(solution)/shard_map/ppermute | solution.py:533
  47.9 8.7 %collective-permute-start.7 = (bf16[336,768]{1,0:T(8,128)(2,1)}, bf16[336,768]{1,0:T(8,128)(2,1)}, u32[]{:S(2)}, u32[]{:S(2)}) collective-permute-start(bf16[336,768]{1,0:T(8,128)(2,1)} %get-tuple-element.49.refs_1_), channel_id=1, source_target_pairs={{0,4},{4,0},{1,5},{5,1},{2,6},{6,2},{3,7},{7,3},{8,12},{12,8},{9,1... | collective-permute-start | bytes 1548296 | tf_op jit(solution)/shard_map/ppermute | solution.py:537
  48.8 18.9 %collective-permute-start.13 = (bf16[336,768]{1,0:T(8,128)(2,1)}, bf16[336,768]{1,0:T(8,128)(2,1)}, u32[]{:S(2)}, u32[]{:S(2)}) collective-permute-start(bf16[336,768]{1,0:T(8,128)(2,1)} %collective-permute-done.1.refs_7_), channel_id=1, source_target_pairs={{0,4},{4,0},{1,5},{5,1},{2,6},{6,2},{3,7},{7,3},{8,12},{12,8},{9,1... | collective-permute-start | bytes 1548296 | tf_op jit(solution)/shard_map/ppermute | solution.py:537
  48.8 18.9 %collective-permute-start.5 = (bf16[336,768]{1,0:T(8,128)(2,1)}, bf16[336,768]{1,0:T(8,128)(2,1)}, u32[]{:S(2)}, u32[]{:S(2)}) collective-permute-start(bf16[336,768]{1,0:T(8,128)(2,1)} %collective-permute-done.3.refs_3_), channel_id=1, source_target_pairs={{0,3},{1,0},{2,1},{3,2},{4,7},{5,4},{6,5},{7,6},{8,11},{9,8},{10,9... | collective-permute-start | bytes 1548296 | tf_op jit(solution)/shard_map/ppermute | solution.py:533
  50.2 23.3 %all-to-all-start.1 = ((bf16[128,3,8,128]{3,2,1,0:T(8,128)(2,1)}), bf16[128,3,8,128]{3,2,1,0:T(8,128)(2,1)S(1)}, u32[]{:S(2)}, u32[]{:S(2)}) async-start(bf16[128,3,8,128]{3,2,1,0:T(8,128)(2,1)} %get-tuple-element.50), calls=%async_computation.1 | async-start | bytes 1572864 | tf_op jit(solution)/shard_map/all_to_all | solution.py:529
  56.6 14.1 %collective-permute-start.8 = (bf16[352,768]{1,0:T(8,128)(2,1)S(1)}, bf16[352,768]{1,0:T(8,128)(2,1)S(1)}, u32[]{:S(2)}, u32[]{:S(2)}) collective-permute-start(bf16[352,768]{1,0:T(8,128)(2,1)S(1)} %collective-permute-done.2.refs_2_), channel_id=1, source_target_pairs={{0,4},{4,0},{1,5},{5,1},{2,6},{6,2},{3,7},{7,3},{8,12},{12,8},{9,1... | collective-permute-start | bytes 1622024 | tf_op jit(solution)/shard_map/ppermute | solution.py:537
  57.7 14.5 %collective-permute-start.12 = (bf16[352,768]{1,0:T(8,128)(2,1)S(1)}, bf16[352,768]{1,0:T(8,128)(2,1)S(1)}, u32[]{:S(2)}, u32[]{:S(2)}) collective-permute-start(bf16[352,768]{1,0:T(8,128)(2,1)S(1)} %collective-permute-done.refs_6_), channel_id=1, source_target_pairs={{0,4},{4,0},{1,5},{5,1},{2,6},{6,2},{3,7},{7,3},{8,12},{12,8},{9,1... | collective-permute-start | bytes 1622024 | tf_op jit(solution)/shard_map/ppermute | solution.py:537
  61.1 12.5 %copy-start.5 = (bf16[352,768]{1,0:T(8,128)(2,1)}, bf16[352,768]{1,0:T(8,128)(2,1)S(1)}, u32[]{:S(2)}) copy-start(bf16[352,768]{1,0:T(8,128)(2,1)S(1)} %collective-permute-done.4.refs_4_) | copy-start | bytes 1622020
  61.1 12.5 %collective-permute-start.10 = (bf16[352,768]{1,0:T(8,128)(2,1)S(1)}, bf16[352,768]{1,0:T(8,128)(2,1)}, u32[]{:S(2)}, u32[]{:S(2)}) collective-permute-start(bf16[352,768]{1,0:T(8,128)(2,1)S(1)} %collective-permute-done.4.refs_4_), channel_id=1, source_target_pairs={{0,4},{4,0},{1,5},{5,1},{2,6},{6,2},{3,7},{7,3},{8,12},{12,8},{9,1... | collective-permute-start | bytes 1622024 | tf_op jit(solution)/shard_map/ppermute | solution.py:537
  67.7 2.9 %collective-permute-start.9 = (bf16[336,768]{1,0:T(8,128)(2,1)}, bf16[336,768]{1,0:T(8,128)(2,1)S(1)}, u32[]{:S(2)}, u32[]{:S(2)}) collective-permute-start(bf16[336,768]{1,0:T(8,128)(2,1)} %collective-permute-done.3.refs_3_), channel_id=1, source_target_pairs={{0,4},{4,0},{1,5},{5,1},{2,6},{6,2},{3,7},{7,3},{8,12},{12,8},{9,1... | collective-permute-start | bytes 1548296 | tf_op jit(solution)/shard_map/ppermute | solution.py:537
  67.8 5.7 %collective-permute-start.11 = (bf16[336,768]{1,0:T(8,128)(2,1)}, bf16[336,768]{1,0:T(8,128)(2,1)}, u32[]{:S(2)}, u32[]{:S(2)}) collective-permute-start(bf16[336,768]{1,0:T(8,128)(2,1)} %collective-permute-done.5.refs_5_), channel_id=1, source_target_pairs={{0,4},{4,0},{1,5},{5,1},{2,6},{6,2},{3,7},{7,3},{8,12},{12,8},{9,1... | collective-permute-start | bytes 1548296 | tf_op jit(solution)/shard_map/ppermute | solution.py:537
  70.6 0.8 copy-start.8
  71.4 0.8 copy-start.6
  72.2 1.3 copy-start.7
  84.5 12.1 %collective-permute-start.14 = (bf16[256,384]{1,0:T(8,128)(2,1)S(1)}, bf16[256,384]{1,0:T(8,128)(2,1)S(1)}, u32[]{:S(2)}, u32[]{:S(2)}) collective-permute-start(bf16[256,384]{1,0:T(8,128)(2,1)S(1)} %get-tuple-element.63), channel_id=1, source_target_pairs={{0,1},{1,2},{2,3},{3,0},{4,5},{5,6},{6,7},{7,4},{8,9},{9,10},{10,1... | collective-permute-start | bytes 589832 | tf_op jit(solution)/shard_map/ppermute | solution.py:533
  85.8 11.5 %collective-permute-start.15 = (bf16[256,384]{1,0:T(8,128)(2,1)S(1)}, bf16[256,384]{1,0:T(8,128)(2,1)S(1)}, u32[]{:S(2)}, u32[]{:S(2)}) collective-permute-start(bf16[256,384]{1,0:T(8,128)(2,1)S(1)} %get-tuple-element.64), channel_id=1, source_target_pairs={{0,2},{1,3},{2,0},{3,1},{4,6},{5,7},{6,4},{7,5},{8,10},{9,11},{10,... | collective-permute-start | bytes 589832 | tf_op jit(solution)/shard_map/ppermute | solution.py:533
  88.4 8.9 %collective-permute-start.16 = (bf16[256,384]{1,0:T(8,128)(2,1)S(1)}, bf16[256,384]{1,0:T(8,128)(2,1)S(1)}, u32[]{:S(2)}, u32[]{:S(2)}) collective-permute-start(bf16[256,384]{1,0:T(8,128)(2,1)S(1)} %get-tuple-element.65), channel_id=1, source_target_pairs={{0,3},{1,0},{2,1},{3,2},{4,7},{5,4},{6,5},{7,6},{8,11},{9,8},{10,9... | collective-permute-start | bytes 589832 | tf_op jit(solution)/shard_map/ppermute | solution.py:533
  97.3 11.1 %collective-permute-start.17 = (bf16[256,384]{1,0:T(8,128)(2,1)S(1)}, bf16[256,384]{1,0:T(8,128)(2,1)S(1)}, u32[]{:S(2)}, u32[]{:S(2)}) collective-permute-start(bf16[256,384]{1,0:T(8,128)(2,1)S(1)} %get-tuple-element.66), channel_id=1, source_target_pairs={{0,1},{1,2},{2,3},{3,0},{4,5},{5,6},{6,7},{7,4},{8,9},{9,10},{10,1... | collective-permute-start | bytes 589832 | tf_op jit(solution)/shard_map/ppermute | solution.py:533
  98.2 11.6 %collective-permute-start.18 = (bf16[256,384]{1,0:T(8,128)(2,1)S(1)}, bf16[256,384]{1,0:T(8,128)(2,1)S(1)}, u32[]{:S(2)}, u32[]{:S(2)}) collective-permute-start(bf16[256,384]{1,0:T(8,128)(2,1)S(1)} %get-tuple-element.67), channel_id=1, source_target_pairs={{0,2},{1,3},{2,0},{3,1},{4,6},{5,7},{6,4},{7,5},{8,10},{9,11},{10,... | collective-permute-start | bytes 589832 | tf_op jit(solution)/shard_map/ppermute | solution.py:533
  101.1 8.7 %collective-permute-start.19 = (bf16[256,384]{1,0:T(8,128)(2,1)S(1)}, bf16[256,384]{1,0:T(8,128)(2,1)S(1)}, u32[]{:S(2)}, u32[]{:S(2)}) collective-permute-start(bf16[256,384]{1,0:T(8,128)(2,1)S(1)} %get-tuple-element.68), channel_id=1, source_target_pairs={{0,3},{1,0},{2,1},{3,2},{4,7},{5,4},{6,5},{7,6},{8,11},{9,8},{10,9... | collective-permute-start | bytes 589832 | tf_op jit(solution)/shard_map/ppermute | solution.py:533
  101.5 4.0 %copy-start = (f32[1,2,192,384]{3,2,1,0:T(8,128)S(1)}, f32[1,2,192,384]{3,2,1,0:T(8,128)}, u32[]{:S(2)}) copy-start(f32[1,2,192,384]{3,2,1,0:T(8,128)} %param.20) | copy-start | bytes 1769476
  101.5 4.0 %copy-start.1 = (f32[1,384,192]{1,2,0:T(8,128)S(1)}, f32[1,384,192]{1,2,0:T(8,128)}, u32[]{:S(2)}) copy-start(f32[1,384,192]{1,2,0:T(8,128)} %param.21) | copy-start | bytes 884740
  112.3 18.4 %all-to-all-start.2 = ((bf16[224,8,128]{2,1,0:T(8,128)(2,1)}), bf16[224,8,128]{2,1,0:T(8,128)(2,1)S(1)}, u32[]{:S(2)}, u32[]{:S(2)}) async-start(bf16[224,8,128]{2,1,0:T(8,128)(2,1)} %fast_grad.5), calls=%async_computation.2 | async-start | bytes 917504 | tf_op jit(solution)/shard_map/all_to_all | solution.py:529
  119.8 16.0 %collective-permute-start.20 = (bf16[768,384]{1,0:T(8,128)(2,1)S(1)}, bf16[768,384]{1,0:T(8,128)(2,1)S(1)}, u32[]{:S(2)}, u32[]{:S(2)}) collective-permute-start(bf16[768,384]{1,0:T(8,128)(2,1)S(1)} %get-tuple-element.83), channel_id=1, source_target_pairs={{0,1},{1,2},{2,3},{3,0},{4,5},{5,6},{6,7},{7,4},{8,9},{9,10},{10,1... | collective-permute-start | bytes 1769480 | tf_op jit(solution)/shard_map/ppermute | solution.py:533
  119.9 16.0 %collective-permute-start.21 = (bf16[768,384]{1,0:T(8,128)(2,1)}, bf16[768,384]{1,0:T(8,128)(2,1)S(1)}, u32[]{:S(2)}, u32[]{:S(2)}) collective-permute-start(bf16[768,384]{1,0:T(8,128)(2,1)} %get-tuple-element.84), channel_id=1, source_target_pairs={{0,3},{1,0},{2,1},{3,2},{4,7},{5,4},{6,5},{7,6},{8,11},{9,8},{10,9... | collective-permute-start | bytes 1769480 | tf_op jit(solution)/shard_map/ppermute | solution.py:533
  131.6 14.6 %all-to-all-start.3 = ((bf16[32,7,8,128]{3,2,1,0:T(8,128)(2,1)}), bf16[32,7,8,128]{3,2,1,0:T(8,128)(2,1)S(1)}, u32[]{:S(2)}, u32[]{:S(2)}) async-start(bf16[32,7,8,128]{3,2,1,0:T(8,128)(2,1)} %sum_pieces.1), calls=%async_computation.3 | async-start | bytes 917504 | tf_op jit(solution)/shard_map/all_to_all | solution.py:529
  135.8 6.6 %collective-permute-start.22 = (bf16[256,384]{1,0:T(8,128)(2,1)S(1)}, bf16[256,384]{1,0:T(8,128)(2,1)S(1)}, u32[]{:S(2)}, u32[]{:S(2)}) collective-permute-start(bf16[256,384]{1,0:T(8,128)(2,1)S(1)} %slice.8), channel_id=1, source_target_pairs={{0,1},{1,2},{2,3},{3,0},{4,5},{5,6},{6,7},{7,4},{8,9},{9,10},{10,1... | collective-permute-start | bytes 589832 | tf_op jit(solution)/shard_map/ppermute | solution.py:533
  135.9 6.5 %collective-permute-start.23 = (bf16[256,384]{1,0:T(8,128)(2,1)S(1)}, bf16[256,384]{1,0:T(8,128)(2,1)S(1)}, u32[]{:S(2)}, u32[]{:S(2)}) collective-permute-start(bf16[256,384]{1,0:T(8,128)(2,1)S(1)} %slice.9), channel_id=1, source_target_pairs={{0,3},{1,0},{2,1},{3,2},{4,7},{5,4},{6,5},{7,6},{8,11},{9,8},{10,9... | collective-permute-start | bytes 589832 | tf_op jit(solution)/shard_map/ppermute | solution.py:533

commit v4 on v3

--- a/solution.py
+++ b/solution.py
@@ -66,13 +66,21 @@
 
 
 def spread_body(
-    at_ref, x_ref, meta_ref, qkv_ref, out_ref, fast_ref, rate_ref,
-    o_ref, low_ref, high_ref, buf, w_ref, sems, wsems, osem,
+    at_ref, dest_hbm, image_hbm, x_ref, rate_hbm, qkv_ref, out_ref, fast_ref,
+    o_ref, low_ref, high_ref, buf, o_buf, w_ref, dest_ref, image_ref, rate_ref,
+    sems, wsems, osem, psem, ssem,
 ):
     head = at_ref[1]
     core = at_ref[2]
-    parity = head // 2
-    half = head % 2
+    parity = lax.shift_right_logical(head, 1)
+    half = head & 1
+    small = [
+        pltpu.make_async_copy(dest_hbm, dest_ref, ssem.at[0]),
+        pltpu.make_async_copy(image_hbm, image_ref, ssem.at[1]),
+        pltpu.make_async_copy(rate_hbm, rate_ref, ssem.at[2]),
+    ]
+    for c in small:
+        c.start()
     copies = []
     for p in range(PAIRS):
         copies.append(
@@ -93,13 +101,23 @@
         (rows(qkv_ref, core * 288, 288), w_ref.at[pl.ds(0, 288)]),
         (rows(out_ref, core * 96, 96), w_ref.at[pl.ds(288, 96)]),
         (rows(fast_ref, FW + core * FW, FW), w_ref.at[pl.ds(KV_AT, FW)]),
-        (rate_ref, w_ref.at[pl.ds(RATE_AT, 16)]),
         (rows(fast_ref, core * 96, 96), w_ref.at[pl.ds(Q_AT, 96)]),
     ]
     moves = [pltpu.make_async_copy(*m, wsems.at[i]) for i, m in enumerate(moves)]
     for m in moves:
         m.start()
-    o_ref[:, PAIRS * LT] = jnp.broadcast_to(meta_ref[...][None], (SEQ, 8, 128))
+    for c in small:
+        c.wait()
+    w_ref[pl.ds(RATE_AT, 16), :] = jnp.broadcast_to(rate_ref[...], (16, D))
+    row = lax.broadcasted_iota(jnp.int32, (8, 128), 0)
+    lane = jnp.where(row == 0, lax.broadcasted_iota(jnp.int32, (8, 128), 1), 128)
+    tile = jnp.zeros((8, 128), F32)
+    for i in range(16):
+        tile = jnp.where(lane == i, dest_ref[i].astype(F32), tile)
+        tile = jnp.where(lane == 16 + i, image_ref[i].astype(F32), tile)
+    o_buf[PAIRS, :, 0] = jnp.broadcast_to(tile.astype(BF)[None], (SEQ, 8, 128))
+    puts = [pltpu.make_async_copy(o_buf.at[PAIRS, :, 0], o_ref.at[:, PAIRS * LT], psem.at[PAIRS])]
+    puts[0].start()
     for m in moves:
         m.wait()
     outs = [
@@ -111,32 +129,42 @@
     for p in range(PAIRS):
         copies[p].wait()
         for t in range(LT):
-            o_ref[:, p * LT + t] = buf[p, :, :, t * 128 : (t + 1) * 128]
-    for c in outs:
+            o_buf[p, :, t] = buf[p, :, :, t * 128 : (t + 1) * 128]
+        puts.append(
+            pltpu.make_async_copy(o_buf.at[p], o_ref.at[:, pl.ds(p * LT, LT)], psem.at[p])
+        )
+        puts[-1].start()
+    for c in outs + puts:
         c.wait()
 
 
-def spread(at, x, meta, *weights):
+def spread(at, dest, image, x, rate, *weights):
     return pl.pallas_call(
         spread_body,
         out_shape=(
-            jax.ShapeDtypeStruct((SEQ, PAIRS * LT + 1, 8, 128), BF),
+            pltpu.HBM((SEQ, PAIRS * LT + 1, 8, 128), BF),
             pltpu.HBM((CUT, D), BF),
             pltpu.HBM((WROWS - CUT, D), BF),
         ),
-        in_specs=[SMEM, ANY, VMEM] + [ANY] * 4,
-        out_specs=[VMEM, ANY, ANY],
+        in_specs=[SMEM] + [ANY] * 7,
+        out_specs=[ANY] * 3,
         scratch_shapes=[
             pltpu.VMEM((PAIRS, SEQ, 8, FH), BF),
+            pltpu.VMEM((PAIRS + 1, SEQ, LT, 8, 128), BF),
             pltpu.VMEM((WROWS, D), BF),
+            pltpu.SMEM((16,), jnp.int32),
+            pltpu.SMEM((16,), jnp.int32),
+            pltpu.VMEM((1, D), BF),
             pltpu.SemaphoreType.DMA((PAIRS,)),
-            pltpu.SemaphoreType.DMA((5,)),
+            pltpu.SemaphoreType.DMA((4,)),
             pltpu.SemaphoreType.DMA((2,)),
+            pltpu.SemaphoreType.DMA((PAIRS + 1,)),
+            pltpu.SemaphoreType.DMA((3,)),
         ],
         compiler_params=params(12),
         cost_estimate=cost(3),
         name="spread",
-    )(at, in_hbm(x), meta, *[in_hbm(w) for w in weights])
+    )(at, *[in_hbm(a) for a in (dest, image, x, rate, *weights)])
 
 
 def pick_body(at_ref, x_ref, o_ref, flag_ref, ids, table, source, sem):
@@ -145,26 +173,27 @@
     copy.start()
     copy.wait()
 
-    def note(q, carry):
-        first = table[q // PAIRS, (q % PAIRS) * 2]
-        pair = jnp.minimum(first // 2, SEQ * HEADS - 1)
-        source[jnp.where(first >= 0, pair, SEQ * HEADS)] = q
+    def note(i, carry):
+        for p in range(PAIRS):
+            first = table[i, 2 * p]
+            pair = jnp.minimum(lax.shift_right_arithmetic(first, 1), SEQ * HEADS - 1)
+            source[jnp.where(first >= 0, pair, SEQ * HEADS)] = i * PAIRS + p
         return carry
 
-    lax.fori_loop(0, SEQ * PAIRS, note, 0, unroll=8)
+    lax.fori_loop(0, SEQ, note, 0, unroll=2)
 
     def move(m, carry):
         q = source[m]
-        o_ref[m] = x_ref[q // PAIRS, pl.ds((q % PAIRS) * LT, LT)]
+        at = (q & (PAIRS - 1)) * LT
+        o_ref[m] = x_ref[lax.shift_right_logical(q, 3), pl.ds(at, LT)]
         return carry
 
-    lax.fori_loop(0, SEQ * HEADS, move, 0, unroll=8)
+    lax.fori_loop(0, SEQ * HEADS, move, 0, unroll=16)
     q = source[at_ref[0]]
-    slot = (q % PAIRS) * 2
-    flag_ref[0] = table[q // PAIRS, slot] % 2
-    flag_ref[1] = jnp.where(
-        table[q // PAIRS, 16 + slot] == table[q // PAIRS, 17 + slot], 1, 0
-    )
+    origin = lax.shift_right_logical(q, 3)
+    slot = (q & (PAIRS - 1)) * 2
+    flag_ref[0] = table[origin, slot] & 1
+    flag_ref[1] = jnp.where(table[origin, 16 + slot] == table[origin, 17 + slot], 1, 0)
     flag_ref[2] = at_ref[1]
     flag_ref[3] = at_ref[2]
 
@@ -369,7 +398,7 @@
     ns = [norm(x.astype(F32), gain_ref[...]) for x in xs]
     cols = [[x[:, g * FW : (g + 1) * FW] for g in range(HEADS)] for x in xs]
     for d in range(HEADS):
-        there = lax.rem(head + d, HEADS)
+        there = ((head + d) & (HEADS - 1))
         wait_all(ws.at[d], sems.at[d])
         w = ws[d].reshape(FW, D)
         for i in range(2):
@@ -488,7 +517,7 @@
 
 
 def apply_body(head_ref, g_ref, gu_ref, down_ref, *refs):
-    qe_refs, (o_ref, gs, ws) = refs[:5], refs[5:]
+    qe_refs, (o_ref, o_buf, gs, ws, sems) = refs[:5], refs[5:]
     for i in range(3):
         for t in range(LT):
             gs[i, :, pl.ds(t * 128, 128)] = (
@@ -500,7 +529,8 @@
     col = lax.broadcasted_iota(jnp.int32, (FW, 2 * FW), 1)
     columns = jnp.where(row + FW == col, 1.0, 0.0).astype(BF)
     own_ref, up_ref, down_side_ref, far0_ref, far1_ref = qe_refs
-    for d in range(HEADS):
+    puts = []
+    for d in (0, 1, 3, 2):
         if d == 2:
             qe = jnp.concatenate([far0_ref[...], far1_ref[...]], axis=0)
         else:
@@ -508,17 +538,28 @@
         q = qe[:, :FW]
         gate = mm(q, ws[0])
         hidden = (gate * jax.nn.sigmoid(gate) * mm(q, ws[1])).astype(BF)
-        base = pl.multiple_of(lax.rem(head_ref[2] + HEADS - d, HEADS) * SPAN, SPAN)
-        o_ref[:, pl.ds(base, SPAN)] = (mm_nt(columns, qe) + mm_nt(ws[2], hidden)).astype(BF)
+        base = pl.multiple_of(((head_ref[2] + HEADS - d) & (HEADS - 1)) * SPAN, SPAN)
+        o_buf[d] = (mm_nt(columns, qe) + mm_nt(ws[2], hidden)).astype(BF)
+        puts.append(
+            pltpu.make_async_copy(o_buf.at[d], o_ref.at[:, pl.ds(base, SPAN)], sems.at[d])
+        )
+        puts[-1].start()
+    for c in puts:
+        c.wait()
 
 
 def apply(flags, grads, gate_up, down, qes):
     return pl.pallas_call(
         apply_body,
-        out_shape=jax.ShapeDtypeStruct((FW, HEADS * SPAN), BF),
+        out_shape=pltpu.HBM((FW, HEADS * SPAN), BF),
         in_specs=[SMEM] + [VMEM] * 8,
-        out_specs=VMEM,
-        scratch_shapes=[pltpu.VMEM((3, FW, FH), F32), pltpu.VMEM((3, FW, FH), BF)],
+        out_specs=ANY,
+        scratch_shapes=[
+            pltpu.VMEM((HEADS, FW, SPAN), BF),
+            pltpu.VMEM((3, FW, FH), F32),
+            pltpu.VMEM((3, FW, FH), BF),
+            pltpu.SemaphoreType.DMA((HEADS,)),
+        ],
         compiler_params=params(16),
         cost_estimate=cost(3),
         name="apply_fast",
@@ -555,16 +596,15 @@
     seq = lax.axis_index(SEQ_AXES)
     at = jnp.stack([seq * HEADS + head, head, core]).astype(jnp.int32)
 
-    ids = jnp.concatenate([slot_dest, slot_image]).astype(BF)
-    tile = jnp.pad(ids[None, :], ((0, 7), (0, 96)))
     pieces, low, high = spread(
         at,
+        slot_dest,
+        slot_image,
         patches.reshape(-1, 8, D),
-        tile,
+        w_rate.T,
         jnp.transpose(w_qkv, (0, 2, 1)).reshape(3 * FW, D),
         w_out,
         jnp.transpose(w_fast, (0, 2, 1)).reshape(3 * FW, D),
-        jnp.broadcast_to(w_rate.T, (16, D)),
     )
     before = (shifted(low, 1), shifted(high, 1))
     after = (shifted(low, -1), shifted(high, -1))

time: 151 us -> 148 us (0.980)
  waiting for transfers between devices: 39.7 us -> 44.4 us
  Pallas kernels: 43.6 us -> 39.6 us
    ppermute x16, waiting for transfers between devices: 9.67 us -> 13.2 us  [shifted(): lax.ppermute(x, 'head', [(i, (i + by) % HEADS) for i in range(HEADS)])]
    pallas_call x1, Pallas kernels: 6.67 us -> 3.33 us  [pick(): pl.pallas_call(pick_body, out_shape=(jax.ShapeDtypeStruct((SEQ * HEADS, L...]
    ppermute x16, starting transfers between devices: 23 us -> 21.3 us  [shifted(): lax.ppermute(x, 'head', [(i, (i + by) % HEADS) for i in range(HEADS)])]
  transfers between devices with their start and end apart: 28 -> 28, of which waited for: 9 -> 12; matrix products, arithmetic and copies ran while one was open for 0% -> 0% of each run, Pallas kernels for 14% -> 12%
where the time goes in v4:
time: 148 us
  starting transfers between devices  61.5 us (42%)
  waiting for transfers between devices  44.4 us (30%)
  Pallas kernels  39.6 us (27%)
  local copies, waits for them, and re-layouts  1.66 us (1%)
    all_to_all x4, waiting for transfers between devices, exchange(): return lax.all_to_all(x, axes, split_axis=0, concat_axis=0, tiled=True)  31.1 us
    all_to_all x4, starting transfers between devices, exchange(): return lax.all_to_all(x, axes, split_axis=0, concat_axis=0, tiled=True)  28.1 us
    ppermute x16, starting transfers between devices, shifted(): lax.ppermute(x, 'head', [(i, (i + by) % HEADS) for i in range(HEADS)])  21.3 us
    ppermute x16, waiting for transfers between devices, shifted(): lax.ppermute(x, 'head', [(i, (i + by) % HEADS) for i in range(HEADS)])  13.2 us
    ppermute x8, starting transfers between devices, swapped(): return lax.ppermute(x, 'core', [(0, 1), (1, 0)])  12.2 us
    pallas_call x1, Pallas kernels, encode_first(): pl.pallas_call(encode_first_body, out_shape=(jax.ShapeDtypeStruct((BLK, D...  10.9 us
    pallas_call x1, Pallas kernels, encode_second(): pl.pallas_call(encode_second_body, out_shape=(jax.ShapeDtypeStruct((BLK,...  6.99 us
    pallas_call x3, Pallas kernels, fast(): pl.pallas_call(make_fast_body(len(blocks), first, last), out_shape=jax.Sh...  5.39 us
  transfers between devices with their start and end apart: 28, of which 12 were waited for; matrix products, arithmetic and copies ran while one was open for 0% of the time, Pallas kernels for 12%

profile of v4, /device:TPU:1, one launch (start us, length us, event | category | flops | bytes accessed | tf_op | source)
XLA Modules:
  0.0 147.7 jit_solution(17151108993619422416)
XLA Ops:
  0.0 0.1 pad_add_fusion.at_ref
  0.1 4.0 %spread.1 = (bf16[32,25,8,128]{3,2,1,0:T(8,128)(2,1)}, bf16[352,768]{1,0:T(8,128)(2,1)}, bf16[336,768]{1,0:T(8,128)(2,1)}) custom-call(s32[3]{0:T(128)S(1)} %pad_add_fusion.at_ref, s32[16]{0:T(128)} %dest_hbm.1, s32[16]{0:T(128)} %image_hbm.1, bf16[512,8,768]{2,1,0:T(8,128)(2,1)} %bitcast.30, bf16[1,768]{1,0:T(2,128)(2,1)} %bitcast.33, ...), custom_call_target="tpu_custom_call" | custom-call | bytes 10800000 | tf_op jit(solution)/shard_map/spread/pallas_call | solution.py:142
  4.1 9.6 %all-to-all-start = ((bf16[32,25,8,128]{3,2,1,0:T(8,128)(2,1)}), bf16[32,25,8,128]{3,2,1,0:T(8,128)(2,1)S(1)}, u32[]{:S(2)}, u32[]{:S(2)}) async-start(bf16[32,25,8,128]{3,2,1,0:T(8,128)(2,1)} %get-tuple-element.45), calls=%async_computation | async-start | bytes 3276800 | tf_op jit(solution)/shard_map/all_to_all | solution.py:570
  13.7 0.0 copy-start.9
  13.7 0.0 copy-start.10
  13.7 2.8 %collective-permute-start.2 = (bf16[352,768]{1,0:T(8,128)(2,1)S(1)}, bf16[352,768]{1,0:T(8,128)(2,1)S(1)}, u32[]{:S(2)}, u32[]{:S(2)}) collective-permute-start(bf16[352,768]{1,0:T(8,128)(2,1)S(1)} %copy-done.2), channel_id=1, source_target_pairs={{0,3},{1,0},{2,1},{3,2},{4,7},{5,4},{6,5},{7,6},{8,11},{9,8},{10,9... | collective-permute-start | bytes 1622024 | tf_op jit(solution)/shard_map/ppermute | solution.py:574
  16.6 0.0 collective-permute-start
  16.6 2.7 %collective-permute-start.3 = (bf16[336,768]{1,0:T(8,128)(2,1)}, bf16[336,768]{1,0:T(8,128)(2,1)}, u32[]{:S(2)}, u32[]{:S(2)}) collective-permute-start(bf16[336,768]{1,0:T(8,128)(2,1)} %get-tuple-element.49.refs_1_), channel_id=1, source_target_pairs={{0,3},{1,0},{2,1},{3,2},{4,7},{5,4},{6,5},{7,6},{8,11},{9,8},{10,9... | collective-permute-start | bytes 1548296 | tf_op jit(solution)/shard_map/ppermute | solution.py:574
  19.2 1.1 collective-permute-start.6
  20.3 16.8 %all-to-all-done.x_ref = bf16[32,25,8,128]{3,2,1,0:T(8,128)(2,1)S(1)} async-done(((bf16[32,25,8,128]{3,2,1,0:T(8,128)(2,1)}), bf16[32,25,8,128]{3,2,1,0:T(8,128)(2,1)S(1)}, u32[]{:S(2)}, u32[]{:S(2)}) %all-to-all-start) | async-done | bytes 1638432 | tf_op jit(solution)/shard_map/all_to_all | solution.py:570
  37.1 3.3 %pick.1 = (bf16[128,3,8,128]{3,2,1,0:T(8,128)(2,1)}, s32[4]{0:T(128)S(1)}) custom-call(s32[3]{0:T(128)S(1)} %pad_add_fusion.at_ref, bf16[32,25,8,128]{3,2,1,0:T(8,128)(2,1)S(1)} %all-to-all-done.x_ref), custom_call_target="tpu_custom_call" | custom-call | bytes 10800000 | tf_op jit(solution)/shard_map/pick/pallas_call | solution.py:202
  40.4 1.8 %collective-permute-done.1.refs_7_ = bf16[336,768]{1,0:T(8,128)(2,1)} collective-permute-done((bf16[336,768]{1,0:T(8,128)(2,1)}, bf16[336,768]{1,0:T(8,128)(2,1)}, u32[]{:S(2)}, u32[]{:S(2)}) %collective-permute-start.1) | collective-permute-done | bytes 516128 | tf_op jit(solution)/shard_map/ppermute | solution.py:574
  42.3 0.1 collective-permute-start.4
  42.4 1.4 collective-permute-start.7
  43.8 0.1 collective-permute-start.13
  43.9 2.8 %collective-permute-start.5 = (bf16[336,768]{1,0:T(8,128)(2,1)}, bf16[336,768]{1,0:T(8,128)(2,1)}, u32[]{:S(2)}, u32[]{:S(2)}) collective-permute-start(bf16[336,768]{1,0:T(8,128)(2,1)} %collective-permute-done.3.refs_3_), channel_id=1, source_target_pairs={{0,3},{1,0},{2,1},{3,2},{4,7},{5,4},{6,5},{7,6},{8,11},{9,8},{10,9... | collective-permute-start | bytes 1548296 | tf_op jit(solution)/shard_map/ppermute | solution.py:574
  46.7 7.2 %all-to-all-start.1 = ((bf16[128,3,8,128]{3,2,1,0:T(8,128)(2,1)}), bf16[128,3,8,128]{3,2,1,0:T(8,128)(2,1)S(1)}, u32[]{:S(2)}, u32[]{:S(2)}) async-start(bf16[128,3,8,128]{3,2,1,0:T(8,128)(2,1)} %get-tuple-element.50), calls=%async_computation.1 | async-start | bytes 1572864 | tf_op jit(solution)/shard_map/all_to_all | solution.py:570
  53.9 0.0 collective-permute-done.7.refs_9_
  53.9 1.1 collective-permute-start.8
  55.1 0.0 collective-permute-done.6.refs_8_
  55.1 0.1 collective-permute-start.12
  55.2 0.8 collective-permute-done.4.refs_4_
  56.0 4.2 %collective-permute-start.10 = (bf16[352,768]{1,0:T(8,128)(2,1)S(1)}, bf16[352,768]{1,0:T(8,128)(2,1)}, u32[]{:S(2)}, u32[]{:S(2)}) collective-permute-start(bf16[352,768]{1,0:T(8,128)(2,1)S(1)} %collective-permute-done.4.refs_4_), channel_id=1, source_target_pairs={{0,4},{4,0},{1,5},{5,1},{2,6},{6,2},{3,7},{7,3},{8,12},{12,8},{9,1... | collective-permute-start | bytes 1622024 | tf_op jit(solution)/shard_map/ppermute | solution.py:578
  60.2 0.0 collective-permute-done.13.refs_15_
  60.2 0.1 collective-permute-start.9
  60.2 2.6 %collective-permute-done.5.refs_5_ = bf16[336,768]{1,0:T(8,128)(2,1)} collective-permute-done((bf16[336,768]{1,0:T(8,128)(2,1)}, bf16[336,768]{1,0:T(8,128)(2,1)}, u32[]{:S(2)}, u32[]{:S(2)}) %collective-permute-start.5) | collective-permute-done | bytes 516128 | tf_op jit(solution)/shard_map/ppermute | solution.py:574
  62.9 4.0 %collective-permute-start.11 = (bf16[336,768]{1,0:T(8,128)(2,1)}, bf16[336,768]{1,0:T(8,128)(2,1)}, u32[]{:S(2)}, u32[]{:S(2)}) collective-permute-start(bf16[336,768]{1,0:T(8,128)(2,1)} %collective-permute-done.5.refs_5_), channel_id=1, source_target_pairs={{0,4},{4,0},{1,5},{5,1},{2,6},{6,2},{3,7},{7,3},{8,12},{12,8},{9,1... | collective-permute-start | bytes 1548296 | tf_op jit(solution)/shard_map/ppermute | solution.py:578
  66.9 0.0 collective-permute-done.8.refs_10_
  66.9 0.8 copy-done.8
  67.7 0.8 copy-done.6
  68.5 0.0 collective-permute-done.12.refs_14_
  68.5 2.4 %all-to-all-done.1 = bf16[128,3,8,128]{3,2,1,0:T(8,128)(2,1)S(1)} async-done(((bf16[128,3,8,128]{3,2,1,0:T(8,128)(2,1)}), bf16[128,3,8,128]{3,2,1,0:T(8,128)(2,1)S(1)}, u32[]{:S(2)}, u32[]{:S(2)}) %all-to-all-start.1) | async-done | bytes 786464 | tf_op jit(solution)/shard_map/all_to_all | solution.py:570
  70.9 0.0 collective-permute-done.11.refs_13_
  70.9 0.0 collective-permute-done.10.refs_12_
  70.9 10.9 %encode_first.1 = (bf16[256,768]{1,0:T(8,128)(2,1)S(1)}, bf16[256,384]{1,0:T(8,128)(2,1)S(1)}, bf16[256,384]{1,0:T(8,128)(2,1)S(1)}, bf16[256,384]{1,0:T(8,128)(...) custom-call(s32[4]{0:T(128)S(1)} %get-tuple-element.46.flag_ref.head, ...), custom_call_target="tpu_custom_call" | custom-call | bytes 32400000 | tf_op jit(solution)/shard_map/encode_first/pallas_call | solution.py:318
  81.8 0.4 collective-permute-start.14
  82.3 2.6 %collective-permute-start.15 = (bf16[256,384]{1,0:T(8,128)(2,1)S(1)}, bf16[256,384]{1,0:T(8,128)(2,1)S(1)}, u32[]{:S(2)}, u32[]{:S(2)}) collective-permute-start(bf16[256,384]{1,0:T(8,128)(2,1)S(1)} %get-tuple-element.64), channel_id=1, source_target_pairs={{0,2},{1,3},{2,0},{3,1},{4,6},{5,7},{6,4},{7,5},{8,10},{9,11},{10,... | collective-permute-start | bytes 589832 | tf_op jit(solution)/shard_map/ppermute | solution.py:574
  84.9 0.0 collective-permute-start.16
  84.9 7.0 %encode_second.1 = (bf16[256,768]{1,0:T(8,128)(2,1)S(1)}, bf16[256,384]{1,0:T(8,128)(2,1)S(1)}, bf16[256,384]{1,0:T(8,128)(2,1)S(1)}, bf16[256,384]{1,0:T(8,128)(2,1)S(1)}, bf16[256,384]{1,0:T(8,128)(2,1)S(1)}) custom-call(s32[4]{0:T(128)S(1)} %get-tuple-element.46.flag_ref.head_ref, f32[1,768]{1,0:T(1,128)S(1)} %reshape.27.fgain_ref.gain_ref, ...), custom_call_target="tpu_custom_call" | custom-call | bytes 72000000 | tf_op jit(solution)/shard_map/encode_second/pallas_call | solution.py:369
  91.9 1.7 %collective-permute-done.15.refs_1_ = bf16[256,384]{1,0:T(8,128)(2,1)S(1)} collective-permute-done((bf16[256,384]{1,0:T(8,128)(2,1)S(1)}, bf16[256,384]{1,0:T(8,128)(2,1)S(1)}, u32[]{:S(2)}, u32[]{:S(2)}) %collective-permute-start.15) | collective-permute-done | bytes 196640 | tf_op jit(solution)/shard_map/ppermute | solution.py:574
  93.6 0.3 collective-permute-done.16.refs_2_
  93.9 1.0 collective-permute-start.17
  94.9 3.4 %collective-permute-start.18 = (bf16[256,384]{1,0:T(8,128)(2,1)S(1)}, bf16[256,384]{1,0:T(8,128)(2,1)S(1)}, u32[]{:S(2)}, u32[]{:S(2)}) collective-permute-start(bf16[256,384]{1,0:T(8,128)(2,1)S(1)} %get-tuple-element.67), channel_id=1, source_target_pairs={{0,2},{1,3},{2,0},{3,1},{4,6},{5,7},{6,4},{7,5},{8,10},{9,11},{10,... | collective-permute-start | bytes 589832 | tf_op jit(solution)/shard_map/ppermute | solution.py:574
  98.3 4.0 %fast_query.1 = (bf16[512,384]{1,0:T(8,128)(2,1)S(1)}, bf16[768,384]{1,0:T(8,128)(2,1)S(1)}, bf16[768,384]{1,0:T(8,128)(2,1)}) custom-call(s32[4]{0:T(128)S(1)} %get-tuple-element.46.flag_ref.head_ref, bf16[256,768]{1,0:T(8,128)(2,1)S(1)} %get-tuple-element.69.x0_ref, bf16[256,768]{1,0:T(8,128)(2,1)S(1)} %get-tuple-element.70.x1_ref, ...), custom_call_target="tpu_custom_call" | custom-call | bytes 14400000 | tf_op jit(solution)/shard_map/fast_query/pallas_call | solution.py:418
  102.4 1.2 fast_grad.3.refs_5_
  103.6 1.7 %fast_grad.4.refs_5_ = f32[3,192,384]{2,1,0:T(8,128)S(1)} custom-call(bf16[256,384]{1,0:T(8,128)(2,1)S(1)} %collective-permute-done.14.refs_0_, bf16[256,384]{1,0:T(8,128)(2,1)S(1)} %collective-permute-done.15.refs_1_, bf16[256,384]{1,0:T(8,128)(2,1)S(1)} %collective-permute-done.16.refs_2_, f32[2,192,384]{2,1,0:T(8,128)S(1)} %bitcast.20, ...), custom_call_target="tpu_custom_call" | custom-call | bytes 10800000 | tf_op jit(solution)/shard_map/fast_grad/pallas_call | solution.py:478
  105.3 0.0 collective-permute-done.17.refs_0_
  105.3 1.7 %collective-permute-done.18.refs_1_ = bf16[256,384]{1,0:T(8,128)(2,1)S(1)} collective-permute-done((bf16[256,384]{1,0:T(8,128)(2,1)S(1)}, bf16[256,384]{1,0:T(8,128)(2,1)S(1)}, u32[]{:S(2)}, u32[]{:S(2)}) %collective-permute-start.18) | collective-permute-done | bytes 196640 | tf_op jit(solution)/shard_map/ppermute | solution.py:574
  107.0 0.0 collective-permute-done.19.refs_2_
  107.0 2.5 %fast_grad.5 = bf16[224,8,128]{2,1,0:T(8,128)(2,1)} custom-call(bf16[256,384]{1,0:T(8,128)(2,1)S(1)} %collective-permute-done.17.refs_0_, bf16[256,384]{1,0:T(8,128)(2,1)S(1)} %collective-permute-done.18.refs_1_, bf16[256,384]{1,0:T(8,128)(2,1)S(1)} %collective-permute-done.19.refs_2_, f32[2,192,384]{2,1,0:T(8,128)S(1)} %bitcast.21, ...), custom_call_target="tpu_custom_call" | custom-call | bytes 10800000 | tf_op jit(solution)/shard_map/fast_grad/pallas_call | solution.py:478
  109.5 7.6 %all-to-all-start.2 = ((bf16[224,8,128]{2,1,0:T(8,128)(2,1)}), bf16[224,8,128]{2,1,0:T(8,128)(2,1)S(1)}, u32[]{:S(2)}, u32[]{:S(2)}) async-start(bf16[224,8,128]{2,1,0:T(8,128)(2,1)} %fast_grad.5), calls=%async_computation.2 | async-start | bytes 917504 | tf_op jit(solution)/shard_map/all_to_all | solution.py:570
  117.1 0.1 collective-permute-start.20
  117.2 2.7 %collective-permute-start.21 = (bf16[768,384]{1,0:T(8,128)(2,1)}, bf16[768,384]{1,0:T(8,128)(2,1)S(1)}, u32[]{:S(2)}, u32[]{:S(2)}) collective-permute-start(bf16[768,384]{1,0:T(8,128)(2,1)} %get-tuple-element.84), channel_id=1, source_target_pairs={{0,3},{1,0},{2,1},{3,2},{4,7},{5,4},{6,5},{7,6},{8,11},{9,8},{10,9... | collective-permute-start | bytes 1769480 | tf_op jit(solution)/shard_map/ppermute | solution.py:574
  119.9 8.2 %all-to-all-done.2 = bf16[224,8,128]{2,1,0:T(8,128)(2,1)S(1)} async-done(((bf16[224,8,128]{2,1,0:T(8,128)(2,1)}), bf16[224,8,128]{2,1,0:T(8,128)(2,1)S(1)}, u32[]{:S(2)}, u32[]{:S(2)}) %all-to-all-start.2) | async-done | bytes 458784 | tf_op jit(solution)/shard_map/all_to_all | solution.py:570
  128.1 0.9 sum_pieces.1
  128.9 3.7 %all-to-all-start.3 = ((bf16[32,7,8,128]{3,2,1,0:T(8,128)(2,1)}), bf16[32,7,8,128]{3,2,1,0:T(8,128)(2,1)S(1)}, u32[]{:S(2)}, u32[]{:S(2)}) async-start(bf16[32,7,8,128]{3,2,1,0:T(8,128)(2,1)} %sum_pieces.1), calls=%async_computation.3 | async-start | bytes 917504 | tf_op jit(solution)/shard_map/all_to_all | solution.py:570
  132.6 0.5 collective-permute-done.20.refs_1_
  133.1 0.1 collective-permute-start.22
  133.2 0.0 collective-permute-done.21.refs_2_
  133.3 2.7 %collective-permute-start.23 = (bf16[256,384]{1,0:T(8,128)(2,1)S(1)}, bf16[256,384]{1,0:T(8,128)(2,1)S(1)}, u32[]{:S(2)}, u32[]{:S(2)}) collective-permute-start(bf16[256,384]{1,0:T(8,128)(2,1)S(1)} %slice.9), channel_id=1, source_target_pairs={{0,3},{1,0},{2,1},{3,2},{4,7},{5,4},{6,5},{7,6},{8,11},{9,8},{10,9... | collective-permute-start | bytes 589832 | tf_op jit(solution)/shard_map/ppermute | solution.py:574
  136.0 3.8 %collective-permute-done.22.refs_3_ = bf16[256,384]{1,0:T(8,128)(2,1)S(1)} collective-permute-done((bf16[256,384]{1,0:T(8,128)(2,1)S(1)}, bf16[256,384]{1,0:T(8,128)(2,1)S(1)}, u32[]{:S(2)}, u32[]{:S(2)}) %collective-permute-start.22) | collective-permute-done | bytes 196640 | tf_op jit(solution)/shard_map/ppermute | solution.py:574
  139.8 0.0 collective-permute-done.23.refs_4_
  139.8 3.7 %all-to-all-done.3 = bf16[32,7,8,128]{3,2,1,0:T(8,128)(2,1)S(1)} async-done(((bf16[32,7,8,128]{3,2,1,0:T(8,128)(2,1)}), bf16[32,7,8,128]{3,2,1,0:T(8,128)(2,1)S(1)}, u32[]{:S(2)}, u32[]{:S(2)}) %all-to-all-start.3) | async-done | bytes 458784 | tf_op jit(solution)/shard_map/all_to_all | solution.py:570
  143.5 4.0 %apply_fast.1 = bf16[192,2048]{1,0:T(8,128)(2,1)} custom-call(s32[4]{0:T(128)S(1)} %get-tuple-element.46.flag_ref.head_ref, bf16[224,8,128]{2,1,0:T(8,128)(2,1)S(1)} %bitcast.28, f32[2,192,384]{2,1,0:T(8,128)S(1)} %bitcast.22, f32[192,384]{1,0:T(8,128)S(1)} %bitcast.26, bf16[512,384]{1,0:T(8,128)(2,1)S(1)} %get-tuple-element.82.refs_0_, ...), custom_call_target="tpu_custom_call" | custom-call | bytes 10800000 | tf_op jit(solution)/shard_map/apply_fast/pallas_call | solution.py:552
  (29 shorter events, 0.1 us)
Async XLA Ops:
  4.1 9.6 %copy-start.2 = (bf16[352,768]{1,0:T(8,128)(2,1)S(1)}, bf16[352,768]{1,0:T(8,128)(2,1)}, u32[]{:S(2)}) copy-start(bf16[352,768]{1,0:T(8,128)(2,1)} %get-tuple-element.48.refs_0_) | copy-start | bytes 1622020
  4.1 33.0 %all-to-all-start = ((bf16[32,25,8,128]{3,2,1,0:T(8,128)(2,1)}), bf16[32,25,8,128]{3,2,1,0:T(8,128)(2,1)S(1)}, u32[]{:S(2)}, u32[]{:S(2)}) async-start(bf16[32,25,8,128]{3,2,1,0:T(8,128)(2,1)} %get-tuple-element.45), calls=%async_computation | async-start | bytes 3276800 | tf_op jit(solution)/shard_map/all_to_all | solution.py:570
  13.7 53.2 %copy-start.9 = (f32[768]{0:T(1024)S(1)}, f32[768]{0:T(1024)}, u32[]{:S(2)}) copy-start(f32[768]{0:T(1024)} %param.17) | copy-start | bytes 9220
  13.7 53.2 %copy-start.10 = (f32[768]{0:T(1024)S(1)}, f32[768]{0:T(1024)}, u32[]{:S(2)}) copy-start(f32[768]{0:T(1024)} %param.14) | copy-start | bytes 9220
  13.7 28.5 %collective-permute-start.2 = (bf16[352,768]{1,0:T(8,128)(2,1)S(1)}, bf16[352,768]{1,0:T(8,128)(2,1)S(1)}, u32[]{:S(2)}, u32[]{:S(2)}) collective-permute-start(bf16[352,768]{1,0:T(8,128)(2,1)S(1)} %copy-done.2), channel_id=1, source_target_pairs={{0,3},{1,0},{2,1},{3,2},{4,7},{5,4},{6,5},{7,6},{8,11},{9,8},{10,9... | collective-permute-start | bytes 1622024 | tf_op jit(solution)/shard_map/ppermute | solution.py:574
  16.6 25.7 %collective-permute-start = (bf16[352,768]{1,0:T(8,128)(2,1)S(1)}, bf16[352,768]{1,0:T(8,128)(2,1)S(1)}, u32[]{:S(2)}, u32[]{:S(2)}) collective-permute-start(bf16[352,768]{1,0:T(8,128)(2,1)S(1)} %copy-done.2), channel_id=1, source_target_pairs={{0,1},{1,2},{2,3},{3,0},{4,5},{5,6},{6,7},{7,4},{8,9},{9,10},{10,1... | collective-permute-start | bytes 1622024 | tf_op jit(solution)/shard_map/ppermute | solution.py:574
  16.6 23.9 %collective-permute-start.3 = (bf16[336,768]{1,0:T(8,128)(2,1)}, bf16[336,768]{1,0:T(8,128)(2,1)}, u32[]{:S(2)}, u32[]{:S(2)}) collective-permute-start(bf16[336,768]{1,0:T(8,128)(2,1)} %get-tuple-element.49.refs_1_), channel_id=1, source_target_pairs={{0,3},{1,0},{2,1},{3,2},{4,7},{5,4},{6,5},{7,6},{8,11},{9,8},{10,9... | collective-permute-start | bytes 1548296 | tf_op jit(solution)/shard_map/ppermute | solution.py:574
  19.2 23.0 %collective-permute-start.1 = (bf16[336,768]{1,0:T(8,128)(2,1)}, bf16[336,768]{1,0:T(8,128)(2,1)}, u32[]{:S(2)}, u32[]{:S(2)}) collective-permute-start(bf16[336,768]{1,0:T(8,128)(2,1)} %get-tuple-element.49.refs_1_), channel_id=1, source_target_pairs={{0,1},{1,2},{2,3},{3,0},{4,5},{5,6},{6,7},{7,4},{8,9},{9,10},{10,1... | collective-permute-start | bytes 1548296 | tf_op jit(solution)/shard_map/ppermute | solution.py:574
  19.2 35.8 %collective-permute-start.6 = (bf16[352,768]{1,0:T(8,128)(2,1)S(1)}, bf16[352,768]{1,0:T(8,128)(2,1)}, u32[]{:S(2)}, u32[]{:S(2)}) collective-permute-start(bf16[352,768]{1,0:T(8,128)(2,1)S(1)} %copy-done.2), channel_id=1, source_target_pairs={{0,4},{4,0},{1,5},{5,1},{2,6},{6,2},{3,7},{7,3},{8,12},{12,8},{9,1... | collective-permute-start | bytes 1622024 | tf_op jit(solution)/shard_map/ppermute | solution.py:578
  42.3 28.6 %copy-start.3 = (bf16[352,768]{1,0:T(8,128)(2,1)}, bf16[352,768]{1,0:T(8,128)(2,1)S(1)}, u32[]{:S(2)}) copy-start(bf16[352,768]{1,0:T(8,128)(2,1)S(1)} %collective-permute-done.2.refs_2_) | copy-start | bytes 1622020
  42.3 28.6 %copy-start.4 = (bf16[352,768]{1,0:T(8,128)(2,1)}, bf16[352,768]{1,0:T(8,128)(2,1)S(1)}, u32[]{:S(2)}) copy-start(bf16[352,768]{1,0:T(8,128)(2,1)S(1)} %collective-permute-done.refs_6_) | copy-start | bytes 1622020
  42.3 13.7 %collective-permute-start.4 = (bf16[352,768]{1,0:T(8,128)(2,1)S(1)}, bf16[352,768]{1,0:T(8,128)(2,1)S(1)}, u32[]{:S(2)}, u32[]{:S(2)}) collective-permute-start(bf16[352,768]{1,0:T(8,128)(2,1)S(1)} %collective-permute-done.refs_6_), channel_id=1, source_target_pairs={{0,1},{1,2},{2,3},{3,0},{4,5},{5,6},{6,7},{7,4},{8,9},{9,10},{10,1... | collective-permute-start | bytes 1622024 | tf_op jit(solution)/shard_map/ppermute | solution.py:574
  42.4 11.6 %collective-permute-start.7 = (bf16[336,768]{1,0:T(8,128)(2,1)}, bf16[336,768]{1,0:T(8,128)(2,1)}, u32[]{:S(2)}, u32[]{:S(2)}) collective-permute-start(bf16[336,768]{1,0:T(8,128)(2,1)} %get-tuple-element.49.refs_1_), channel_id=1, source_target_pairs={{0,4},{4,0},{1,5},{5,1},{2,6},{6,2},{3,7},{7,3},{8,12},{12,8},{9,1... | collective-permute-start | bytes 1548296 | tf_op jit(solution)/shard_map/ppermute | solution.py:578
  43.8 16.4 %collective-permute-start.13 = (bf16[336,768]{1,0:T(8,128)(2,1)}, bf16[336,768]{1,0:T(8,128)(2,1)}, u32[]{:S(2)}, u32[]{:S(2)}) collective-permute-start(bf16[336,768]{1,0:T(8,128)(2,1)} %collective-permute-done.1.refs_7_), channel_id=1, source_target_pairs={{0,4},{4,0},{1,5},{5,1},{2,6},{6,2},{3,7},{7,3},{8,12},{12,8},{9,1... | collective-permute-start | bytes 1548296 | tf_op jit(solution)/shard_map/ppermute | solution.py:578
  43.9 19.0 %collective-permute-start.5 = (bf16[336,768]{1,0:T(8,128)(2,1)}, bf16[336,768]{1,0:T(8,128)(2,1)}, u32[]{:S(2)}, u32[]{:S(2)}) collective-permute-start(bf16[336,768]{1,0:T(8,128)(2,1)} %collective-permute-done.3.refs_3_), channel_id=1, source_target_pairs={{0,3},{1,0},{2,1},{3,2},{4,7},{5,4},{6,5},{7,6},{8,11},{9,8},{10,9... | collective-permute-start | bytes 1548296 | tf_op jit(solution)/shard_map/ppermute | solution.py:574
  46.7 24.2 %all-to-all-start.1 = ((bf16[128,3,8,128]{3,2,1,0:T(8,128)(2,1)}), bf16[128,3,8,128]{3,2,1,0:T(8,128)(2,1)S(1)}, u32[]{:S(2)}, u32[]{:S(2)}) async-start(bf16[128,3,8,128]{3,2,1,0:T(8,128)(2,1)} %get-tuple-element.50), calls=%async_computation.1 | async-start | bytes 1572864 | tf_op jit(solution)/shard_map/all_to_all | solution.py:570
  53.9 13.0 %collective-permute-start.8 = (bf16[352,768]{1,0:T(8,128)(2,1)S(1)}, bf16[352,768]{1,0:T(8,128)(2,1)S(1)}, u32[]{:S(2)}, u32[]{:S(2)}) collective-permute-start(bf16[352,768]{1,0:T(8,128)(2,1)S(1)} %collective-permute-done.2.refs_2_), channel_id=1, source_target_pairs={{0,4},{4,0},{1,5},{5,1},{2,6},{6,2},{3,7},{7,3},{8,12},{12,8},{9,1... | collective-permute-start | bytes 1622024 | tf_op jit(solution)/shard_map/ppermute | solution.py:578
  55.1 13.4 %collective-permute-start.12 = (bf16[352,768]{1,0:T(8,128)(2,1)S(1)}, bf16[352,768]{1,0:T(8,128)(2,1)S(1)}, u32[]{:S(2)}, u32[]{:S(2)}) collective-permute-start(bf16[352,768]{1,0:T(8,128)(2,1)S(1)} %collective-permute-done.refs_6_), channel_id=1, source_target_pairs={{0,4},{4,0},{1,5},{5,1},{2,6},{6,2},{3,7},{7,3},{8,12},{12,8},{9,1... | collective-permute-start | bytes 1622024 | tf_op jit(solution)/shard_map/ppermute | solution.py:578
  56.0 14.9 %copy-start.5 = (bf16[352,768]{1,0:T(8,128)(2,1)}, bf16[352,768]{1,0:T(8,128)(2,1)S(1)}, u32[]{:S(2)}) copy-start(bf16[352,768]{1,0:T(8,128)(2,1)S(1)} %collective-permute-done.4.refs_4_) | copy-start | bytes 1622020
  56.0 14.9 %collective-permute-start.10 = (bf16[352,768]{1,0:T(8,128)(2,1)S(1)}, bf16[352,768]{1,0:T(8,128)(2,1)}, u32[]{:S(2)}, u32[]{:S(2)}) collective-permute-start(bf16[352,768]{1,0:T(8,128)(2,1)S(1)} %collective-permute-done.4.refs_4_), channel_id=1, source_target_pairs={{0,4},{4,0},{1,5},{5,1},{2,6},{6,2},{3,7},{7,3},{8,12},{12,8},{9,1... | collective-permute-start | bytes 1622024 | tf_op jit(solution)/shard_map/ppermute | solution.py:578
  60.2 6.7 %collective-permute-start.9 = (bf16[336,768]{1,0:T(8,128)(2,1)}, bf16[336,768]{1,0:T(8,128)(2,1)S(1)}, u32[]{:S(2)}, u32[]{:S(2)}) collective-permute-start(bf16[336,768]{1,0:T(8,128)(2,1)} %collective-permute-done.3.refs_3_), channel_id=1, source_target_pairs={{0,4},{4,0},{1,5},{5,1},{2,6},{6,2},{3,7},{7,3},{8,12},{12,8},{9,1... | collective-permute-start | bytes 1548296 | tf_op jit(solution)/shard_map/ppermute | solution.py:578
  62.9 8.0 %collective-permute-start.11 = (bf16[336,768]{1,0:T(8,128)(2,1)}, bf16[336,768]{1,0:T(8,128)(2,1)}, u32[]{:S(2)}, u32[]{:S(2)}) collective-permute-start(bf16[336,768]{1,0:T(8,128)(2,1)} %collective-permute-done.5.refs_5_), channel_id=1, source_target_pairs={{0,4},{4,0},{1,5},{5,1},{2,6},{6,2},{3,7},{7,3},{8,12},{12,8},{9,1... | collective-permute-start | bytes 1548296 | tf_op jit(solution)/shard_map/ppermute | solution.py:578
  66.9 0.8 copy-start.8
  67.7 0.8 copy-start.6
  68.5 2.4 %copy-start.7 = (bf16[352,768]{1,0:T(8,128)(2,1)}, bf16[352,768]{1,0:T(8,128)(2,1)S(1)}, u32[]{:S(2)}) copy-start(bf16[352,768]{1,0:T(8,128)(2,1)S(1)} %collective-permute-done.12.refs_14_) | copy-start | bytes 1622020
  81.8 10.0 %collective-permute-start.14 = (bf16[256,384]{1,0:T(8,128)(2,1)S(1)}, bf16[256,384]{1,0:T(8,128)(2,1)S(1)}, u32[]{:S(2)}, u32[]{:S(2)}) collective-permute-start(bf16[256,384]{1,0:T(8,128)(2,1)S(1)} %get-tuple-element.63), channel_id=1, source_target_pairs={{0,1},{1,2},{2,3},{3,0},{4,5},{5,6},{6,7},{7,4},{8,9},{9,10},{10,1... | collective-permute-start | bytes 589832 | tf_op jit(solution)/shard_map/ppermute | solution.py:574
  82.3 11.3 %collective-permute-start.15 = (bf16[256,384]{1,0:T(8,128)(2,1)S(1)}, bf16[256,384]{1,0:T(8,128)(2,1)S(1)}, u32[]{:S(2)}, u32[]{:S(2)}) collective-permute-start(bf16[256,384]{1,0:T(8,128)(2,1)S(1)} %get-tuple-element.64), channel_id=1, source_target_pairs={{0,2},{1,3},{2,0},{3,1},{4,6},{5,7},{6,4},{7,5},{8,10},{9,11},{10,... | collective-permute-start | bytes 589832 | tf_op jit(solution)/shard_map/ppermute | solution.py:574
  84.9 9.1 %collective-permute-start.16 = (bf16[256,384]{1,0:T(8,128)(2,1)S(1)}, bf16[256,384]{1,0:T(8,128)(2,1)S(1)}, u32[]{:S(2)}, u32[]{:S(2)}) collective-permute-start(bf16[256,384]{1,0:T(8,128)(2,1)S(1)} %get-tuple-element.65), channel_id=1, source_target_pairs={{0,3},{1,0},{2,1},{3,2},{4,7},{5,4},{6,5},{7,6},{8,11},{9,8},{10,9... | collective-permute-start | bytes 589832 | tf_op jit(solution)/shard_map/ppermute | solution.py:574
  93.9 11.4 %collective-permute-start.17 = (bf16[256,384]{1,0:T(8,128)(2,1)S(1)}, bf16[256,384]{1,0:T(8,128)(2,1)S(1)}, u32[]{:S(2)}, u32[]{:S(2)}) collective-permute-start(bf16[256,384]{1,0:T(8,128)(2,1)S(1)} %get-tuple-element.66), channel_id=1, source_target_pairs={{0,1},{1,2},{2,3},{3,0},{4,5},{5,6},{6,7},{7,4},{8,9},{9,10},{10,1... | collective-permute-start | bytes 589832 | tf_op jit(solution)/shard_map/ppermute | solution.py:574
  94.9 12.1 %collective-permute-start.18 = (bf16[256,384]{1,0:T(8,128)(2,1)S(1)}, bf16[256,384]{1,0:T(8,128)(2,1)S(1)}, u32[]{:S(2)}, u32[]{:S(2)}) collective-permute-start(bf16[256,384]{1,0:T(8,128)(2,1)S(1)} %get-tuple-element.67), channel_id=1, source_target_pairs={{0,2},{1,3},{2,0},{3,1},{4,6},{5,7},{6,4},{7,5},{8,10},{9,11},{10,... | collective-permute-start | bytes 589832 | tf_op jit(solution)/shard_map/ppermute | solution.py:574
  98.3 8.7 %collective-permute-start.19 = (bf16[256,384]{1,0:T(8,128)(2,1)S(1)}, bf16[256,384]{1,0:T(8,128)(2,1)S(1)}, u32[]{:S(2)}, u32[]{:S(2)}) collective-permute-start(bf16[256,384]{1,0:T(8,128)(2,1)S(1)} %get-tuple-element.68), channel_id=1, source_target_pairs={{0,3},{1,0},{2,1},{3,2},{4,7},{5,4},{6,5},{7,6},{8,11},{9,8},{10,9... | collective-permute-start | bytes 589832 | tf_op jit(solution)/shard_map/ppermute | solution.py:574
  98.3 4.1 %copy-start = (f32[1,2,192,384]{3,2,1,0:T(8,128)S(1)}, f32[1,2,192,384]{3,2,1,0:T(8,128)}, u32[]{:S(2)}) copy-start(f32[1,2,192,384]{3,2,1,0:T(8,128)} %param.20) | copy-start | bytes 1769476
  98.3 4.1 %copy-start.1 = (f32[1,384,192]{1,2,0:T(8,128)S(1)}, f32[1,384,192]{1,2,0:T(8,128)}, u32[]{:S(2)}) copy-start(f32[1,384,192]{1,2,0:T(8,128)} %param.21) | copy-start | bytes 884740
  109.5 18.6 %all-to-all-start.2 = ((bf16[224,8,128]{2,1,0:T(8,128)(2,1)}), bf16[224,8,128]{2,1,0:T(8,128)(2,1)S(1)}, u32[]{:S(2)}, u32[]{:S(2)}) async-start(bf16[224,8,128]{2,1,0:T(8,128)(2,1)} %fast_grad.5), calls=%async_computation.2 | async-start | bytes 917504 | tf_op jit(solution)/shard_map/all_to_all | solution.py:570
  117.1 16.0 %collective-permute-start.20 = (bf16[768,384]{1,0:T(8,128)(2,1)S(1)}, bf16[768,384]{1,0:T(8,128)(2,1)S(1)}, u32[]{:S(2)}, u32[]{:S(2)}) collective-permute-start(bf16[768,384]{1,0:T(8,128)(2,1)S(1)} %get-tuple-element.83), channel_id=1, source_target_pairs={{0,1},{1,2},{2,3},{3,0},{4,5},{5,6},{6,7},{7,4},{8,9},{9,10},{10,1... | collective-permute-start | bytes 1769480 | tf_op jit(solution)/shard_map/ppermute | solution.py:574
  117.2 16.0 %collective-permute-start.21 = (bf16[768,384]{1,0:T(8,128)(2,1)}, bf16[768,384]{1,0:T(8,128)(2,1)S(1)}, u32[]{:S(2)}, u32[]{:S(2)}) collective-permute-start(bf16[768,384]{1,0:T(8,128)(2,1)} %get-tuple-element.84), channel_id=1, source_target_pairs={{0,3},{1,0},{2,1},{3,2},{4,7},{5,4},{6,5},{7,6},{8,11},{9,8},{10,9... | collective-permute-start | bytes 1769480 | tf_op jit(solution)/shard_map/ppermute | solution.py:574
  128.9 14.6 %all-to-all-start.3 = ((bf16[32,7,8,128]{3,2,1,0:T(8,128)(2,1)}), bf16[32,7,8,128]{3,2,1,0:T(8,128)(2,1)S(1)}, u32[]{:S(2)}, u32[]{:S(2)}) async-start(bf16[32,7,8,128]{3,2,1,0:T(8,128)(2,1)} %sum_pieces.1), calls=%async_computation.3 | async-start | bytes 917504 | tf_op jit(solution)/shard_map/all_to_all | solution.py:570
  133.1 6.6 %collective-permute-start.22 = (bf16[256,384]{1,0:T(8,128)(2,1)S(1)}, bf16[256,384]{1,0:T(8,128)(2,1)S(1)}, u32[]{:S(2)}, u32[]{:S(2)}) collective-permute-start(bf16[256,384]{1,0:T(8,128)(2,1)S(1)} %slice.8), channel_id=1, source_target_pairs={{0,1},{1,2},{2,3},{3,0},{4,5},{5,6},{6,7},{7,4},{8,9},{9,10},{10,1... | collective-permute-start | bytes 589832 | tf_op jit(solution)/shard_map/ppermute | solution.py:574
  133.3 6.5 %collective-permute-start.23 = (bf16[256,384]{1,0:T(8,128)(2,1)S(1)}, bf16[256,384]{1,0:T(8,128)(2,1)S(1)}, u32[]{:S(2)}, u32[]{:S(2)}) collective-permute-start(bf16[256,384]{1,0:T(8,128)(2,1)S(1)} %slice.9), channel_id=1, source_target_pairs={{0,3},{1,0},{2,1},{3,2},{4,7},{5,4},{6,5},{7,6},{8,11},{9,8},{10,9... | collective-permute-start | bytes 589832 | tf_op jit(solution)/shard_map/ppermute | solution.py:574

commit v5 on v4

--- a/solution.py
+++ b/solution.py
@@ -609,7 +609,6 @@
     before = (shifted(low, 1), shifted(high, 1))
     after = (shifted(low, -1), shifted(high, -1))
     picked, flags = pick(at, exchange(pieces, SEQ_AXES))
-    picked, before, after = lax.optimization_barrier((picked, before, after))
     mine = exchange(picked, ALL_AXES)
     far = (shifted(before[0], 1), shifted(after[1], -1))
     weights = (low, high, *after, *far, *before)

time: 148 us -> 145 us (0.980)
  starting transfers between devices: 61.5 us -> 50.6 us
  waiting for transfers between devices: 44.4 us -> 52.9 us
    ppermute x16, waiting for transfers between devices: 13.2 us -> 28.3 us  [shifted(): lax.ppermute(x, 'head', [(i, (i + by) % HEADS) for i in range(HEADS)])]
    all_to_all x4, waiting for transfers between devices: 31.1 us -> 22.4 us  [exchange(): return lax.all_to_all(x, axes, split_axis=0, concat_axis=0, tiled=True)]
    ppermute x8, starting transfers between devices: 12.2 us -> 6.41 us  [swapped(): return lax.ppermute(x, 'core', [(0, 1), (1, 0)])]
    ppermute x16, starting transfers between devices: 21.3 us -> 18.5 us  [shifted(): lax.ppermute(x, 'head', [(i, (i + by) % HEADS) for i in range(HEADS)])]
    all_to_all x4, starting transfers between devices: 28.1 us -> 25.7 us  [exchange(): return lax.all_to_all(x, axes, split_axis=0, concat_axis=0, tiled=True)]
    ppermute x8, waiting for transfers between devices: 0.02 us -> 2.12 us  [swapped(): return lax.ppermute(x, 'core', [(0, 1), (1, 0)])]
  transfers between devices with their start and end apart: 28 -> 28, of which waited for: 12 -> 12; matrix products, arithmetic and copies ran while one was open for 0% -> 0% of each run, Pallas kernels for 12% -> 13%
where the time goes in v5:
time: 145 us
  waiting for transfers between devices  52.9 us (36%)
  starting transfers between devices  50.6 us (35%)
  Pallas kernels  39.7 us (27%)
    ppermute x16, waiting for transfers between devices, shifted(): lax.ppermute(x, 'head', [(i, (i + by) % HEADS) for i in range(HEADS)])  28.3 us
    all_to_all x4, starting transfers between devices, exchange(): return lax.all_to_all(x, axes, split_axis=0, concat_axis=0, tiled=True)  25.7 us
    all_to_all x4, waiting for transfers between devices, exchange(): return lax.all_to_all(x, axes, split_axis=0, concat_axis=0, tiled=True)  22.4 us
    ppermute x16, starting transfers between devices, shifted(): lax.ppermute(x, 'head', [(i, (i + by) % HEADS) for i in range(HEADS)])  18.5 us
    pallas_call x1, Pallas kernels, encode_first(): pl.pallas_call(encode_first_body, out_shape=(jax.ShapeDtypeStruct((BLK, D...  10.9 us
    pallas_call x1, Pallas kernels, encode_second(): pl.pallas_call(encode_second_body, out_shape=(jax.ShapeDtypeStruct((BLK,...  6.99 us
    ppermute x8, starting transfers between devices, swapped(): return lax.ppermute(x, 'core', [(0, 1), (1, 0)])  6.41 us
    pallas_call x3, Pallas kernels, fast(): pl.pallas_call(make_fast_body(len(blocks), first, last), out_shape=jax.Sh...  5.42 us
  transfers between devices with their start and end apart: 28, of which 12 were waited for; matrix products, arithmetic and copies ran while one was open for 0% of the time, Pallas kernels for 13%

profile of v5, /device:TPU:1, one launch (start us, length us, event | category | flops | bytes accessed | tf_op | source)
XLA Modules:
  0.0 144.8 jit_solution(6059554553653603653)
XLA Ops:
  0.0 0.1 pad_add_fusion.at_ref
  0.1 4.1 %spread.1 = (bf16[32,25,8,128]{3,2,1,0:T(8,128)(2,1)}, bf16[352,768]{1,0:T(8,128)(2,1)}, bf16[336,768]{1,0:T(8,128)(2,1)}) custom-call(s32[3]{0:T(128)S(1)} %pad_add_fusion.at_ref, s32[16]{0:T(128)} %dest_hbm.1, s32[16]{0:T(128)} %image_hbm.1, bf16[512,8,768]{2,1,0:T(8,128)(2,1)} %bitcast.30, bf16[1,768]{1,0:T(2,128)(2,1)} %bitcast.33, ...), custom_call_target="tpu_custom_call" | custom-call | bytes 10800000 | tf_op jit(solution)/shard_map/spread/pallas_call | solution.py:142
  4.2 9.6 %all-to-all-start = ((bf16[32,25,8,128]{3,2,1,0:T(8,128)(2,1)}), bf16[32,25,8,128]{3,2,1,0:T(8,128)(2,1)S(1)}, u32[]{:S(2)}, u32[]{:S(2)}) async-start(bf16[32,25,8,128]{3,2,1,0:T(8,128)(2,1)} %get-tuple-element.40), calls=%async_computation | async-start | bytes 3276800 | tf_op jit(solution)/shard_map/all_to_all | solution.py:570
  13.7 0.0 copy-start.10
  13.8 0.0 copy-start.11
  13.8 1.4 collective-permute-start.2
  15.1 0.5 collective-permute-start.7
  15.7 1.3 collective-permute-start.5
  17.0 1.4 collective-permute-start.1
  18.3 0.6 collective-permute-start.6
  18.9 0.0 collective-permute-done.7.refs_9_
  18.9 0.3 collective-permute-start
  19.2 9.6 %collective-permute-done.2.refs_6_ = bf16[352,768]{1,0:T(8,128)(2,1)S(1)} collective-permute-done((bf16[352,768]{1,0:T(8,128)(2,1)S(1)}, bf16[352,768]{1,0:T(8,128)(2,1)S(1)}, u32[]{:S(2)}, u32[]{:S(2)}) %collective-permute-start.2) | collective-permute-done | bytes 540704 | tf_op jit(solution)/shard_map/ppermute | solution.py:574
  28.8 0.1 collective-permute-start.3
  28.9 11.1 %collective-permute-done.5.refs_7_ = bf16[336,768]{1,0:T(8,128)(2,1)} collective-permute-done((bf16[336,768]{1,0:T(8,128)(2,1)}, bf16[336,768]{1,0:T(8,128)(2,1)}, u32[]{:S(2)}, u32[]{:S(2)}) %collective-permute-start.5) | collective-permute-done | bytes 516128 | tf_op jit(solution)/shard_map/ppermute | solution.py:574
  40.0 1.6 %collective-permute-start.13 = (bf16[336,768]{1,0:T(8,128)(2,1)}, bf16[336,768]{1,0:T(8,128)(2,1)}, u32[]{:S(2)}, u32[]{:S(2)}) collective-permute-start(bf16[336,768]{1,0:T(8,128)(2,1)} %collective-permute-done.5.refs_7_), channel_id=1, source_target_pairs={{0,4},{4,0},{1,5},{5,1},{2,6},{6,2},{3,7},{7,3},{8,12},{12,8},{9,1... | collective-permute-start | bytes 1548296 | tf_op jit(solution)/shard_map/ppermute | solution.py:578
  41.5 0.0 collective-permute-done.1.refs_3_
  41.6 1.5 %collective-permute-start.4 = (bf16[336,768]{1,0:T(8,128)(2,1)}, bf16[336,768]{1,0:T(8,128)(2,1)}, u32[]{:S(2)}, u32[]{:S(2)}) collective-permute-start(bf16[336,768]{1,0:T(8,128)(2,1)} %collective-permute-done.1.refs_3_), channel_id=1, source_target_pairs={{0,3},{1,0},{2,1},{3,2},{4,7},{5,4},{6,5},{7,6},{8,11},{9,8},{10,9... | collective-permute-start | bytes 1548296 | tf_op jit(solution)/shard_map/ppermute | solution.py:574
  43.1 0.0 all-to-all-done.x_ref
  43.1 3.3 %pick.1 = (bf16[128,3,8,128]{3,2,1,0:T(8,128)(2,1)}, s32[4]{0:T(128)S(1)}) custom-call(s32[3]{0:T(128)S(1)} %pad_add_fusion.at_ref, bf16[32,25,8,128]{3,2,1,0:T(8,128)(2,1)S(1)} %all-to-all-done.x_ref), custom_call_target="tpu_custom_call" | custom-call | bytes 10800000 | tf_op jit(solution)/shard_map/pick/pallas_call | solution.py:202
  46.4 7.1 %all-to-all-start.1 = ((bf16[128,3,8,128]{3,2,1,0:T(8,128)(2,1)}), bf16[128,3,8,128]{3,2,1,0:T(8,128)(2,1)S(1)}, u32[]{:S(2)}, u32[]{:S(2)}) async-start(bf16[128,3,8,128]{3,2,1,0:T(8,128)(2,1)} %get-tuple-element.42), calls=%async_computation.1 | async-start | bytes 1572864 | tf_op jit(solution)/shard_map/all_to_all | solution.py:570
  53.6 0.0 collective-permute-done.6.refs_8_
  53.6 1.1 collective-permute-start.12
  54.7 0.0 collective-permute-done.refs_2_
  54.7 0.1 collective-permute-start.8
  54.9 0.4 collective-permute-start.10
  55.3 0.1 collective-permute-start.9
  55.4 2.0 %collective-permute-start.11 = (bf16[336,768]{1,0:T(8,128)(2,1)}, bf16[336,768]{1,0:T(8,128)(2,1)S(1)}, u32[]{:S(2)}, u32[]{:S(2)}) collective-permute-start(bf16[336,768]{1,0:T(8,128)(2,1)} %collective-permute-done.4.refs_5_), channel_id=1, source_target_pairs={{0,4},{4,0},{1,5},{5,1},{2,6},{6,2},{3,7},{7,3},{8,12},{12,8},{9,1... | collective-permute-start | bytes 1548296 | tf_op jit(solution)/shard_map/ppermute | solution.py:578
  57.4 1.4 collective-permute-done.9.refs_11_
  58.8 0.7 collective-permute-done.11.refs_13_
  59.5 0.1 copy-done.8
  59.6 0.9 copy-done.9
  60.5 10.0 %all-to-all-done.1 = bf16[128,3,8,128]{3,2,1,0:T(8,128)(2,1)S(1)} async-done(((bf16[128,3,8,128]{3,2,1,0:T(8,128)(2,1)}), bf16[128,3,8,128]{3,2,1,0:T(8,128)(2,1)S(1)}, u32[]{:S(2)}, u32[]{:S(2)}) %all-to-all-start.1) | async-done | bytes 786464 | tf_op jit(solution)/shard_map/all_to_all | solution.py:570
  70.5 10.9 %encode_first.1 = (bf16[256,768]{1,0:T(8,128)(2,1)S(1)}, bf16[256,384]{1,0:T(8,128)(2,1)S(1)}, bf16[256,384]{1,0:T(8,128)(2,1)S(1)}, bf16[256,384]{1,0:T(8,128)(...) custom-call(s32[4]{0:T(128)S(1)} %get-tuple-element.41.flag_ref.head, ...), custom_call_target="tpu_custom_call" | custom-call | bytes 32400000 | tf_op jit(solution)/shard_map/encode_first/pallas_call | solution.py:318
  81.5 0.4 collective-permute-start.14
  81.9 1.4 collective-permute-start.15
  83.3 1.1 collective-permute-start.16
  84.4 7.0 %encode_second.1 = (bf16[256,768]{1,0:T(8,128)(2,1)S(1)}, bf16[256,384]{1,0:T(8,128)(2,1)S(1)}, bf16[256,384]{1,0:T(8,128)(2,1)S(1)}, bf16[256,384]{1,0:T(8,128)(2,1)S(1)}, bf16[256,384]{1,0:T(8,128)(2,1)S(1)}) custom-call(s32[4]{0:T(128)S(1)} %get-tuple-element.41.flag_ref.head_ref, f32[1,768]{1,0:T(1,128)S(1)} %reshape.27.fgain_ref.gain_ref, ...), custom_call_target="tpu_custom_call" | custom-call | bytes 72000000 | tf_op jit(solution)/shard_map/encode_second/pallas_call | solution.py:369
  91.4 1.8 %collective-permute-done.14.refs_0_ = bf16[256,384]{1,0:T(8,128)(2,1)S(1)} collective-permute-done((bf16[256,384]{1,0:T(8,128)(2,1)S(1)}, bf16[256,384]{1,0:T(8,128)(2,1)S(1)}, u32[]{:S(2)}, u32[]{:S(2)}) %collective-permute-start.14) | collective-permute-done | bytes 196640 | tf_op jit(solution)/shard_map/ppermute | solution.py:574
  93.2 0.3 collective-permute-done.16.refs_2_
  93.6 1.0 collective-permute-start.17
  94.5 3.2 %collective-permute-start.18 = (bf16[256,384]{1,0:T(8,128)(2,1)S(1)}, bf16[256,384]{1,0:T(8,128)(2,1)S(1)}, u32[]{:S(2)}, u32[]{:S(2)}) collective-permute-start(bf16[256,384]{1,0:T(8,128)(2,1)S(1)} %get-tuple-element.57), channel_id=1, source_target_pairs={{0,2},{1,3},{2,0},{3,1},{4,6},{5,7},{6,4},{7,5},{8,10},{9,11},{10,... | collective-permute-start | bytes 589832 | tf_op jit(solution)/shard_map/ppermute | solution.py:574
  97.7 0.0 collective-permute-start.19
  97.7 4.1 %fast_query.1 = (bf16[512,384]{1,0:T(8,128)(2,1)S(1)}, bf16[768,384]{1,0:T(8,128)(2,1)S(1)}, bf16[768,384]{1,0:T(8,128)(2,1)}) custom-call(s32[4]{0:T(128)S(1)} %get-tuple-element.41.flag_ref.head_ref, bf16[256,768]{1,0:T(8,128)(2,1)S(1)} %get-tuple-element.59.x0_ref, bf16[256,768]{1,0:T(8,128)(2,1)S(1)} %get-tuple-element.60.x1_ref, ...), custom_call_target="tpu_custom_call" | custom-call | bytes 14400000 | tf_op jit(solution)/shard_map/fast_query/pallas_call | solution.py:418
  101.8 1.2 fast_grad.3.refs_5_
  102.9 1.7 %fast_grad.4.refs_5_ = f32[3,192,384]{2,1,0:T(8,128)S(1)} custom-call(bf16[256,384]{1,0:T(8,128)(2,1)S(1)} %collective-permute-done.14.refs_0_, bf16[256,384]{1,0:T(8,128)(2,1)S(1)} %collective-permute-done.15.refs_1_, bf16[256,384]{1,0:T(8,128)(2,1)S(1)} %collective-permute-done.16.refs_2_, f32[2,192,384]{2,1,0:T(8,128)S(1)} %bitcast.20, ...), custom_call_target="tpu_custom_call" | custom-call | bytes 10800000 | tf_op jit(solution)/shard_map/fast_grad/pallas_call | solution.py:478
  104.7 0.0 collective-permute-done.17.refs_0_
  104.7 1.6 %collective-permute-done.18.refs_1_ = bf16[256,384]{1,0:T(8,128)(2,1)S(1)} collective-permute-done((bf16[256,384]{1,0:T(8,128)(2,1)S(1)}, bf16[256,384]{1,0:T(8,128)(2,1)S(1)}, u32[]{:S(2)}, u32[]{:S(2)}) %collective-permute-start.18) | collective-permute-done | bytes 196640 | tf_op jit(solution)/shard_map/ppermute | solution.py:574
  106.3 0.0 collective-permute-done.19.refs_2_
  106.3 2.5 %fast_grad.5 = bf16[224,8,128]{2,1,0:T(8,128)(2,1)} custom-call(bf16[256,384]{1,0:T(8,128)(2,1)S(1)} %collective-permute-done.17.refs_0_, bf16[256,384]{1,0:T(8,128)(2,1)S(1)} %collective-permute-done.18.refs_1_, bf16[256,384]{1,0:T(8,128)(2,1)S(1)} %collective-permute-done.19.refs_2_, f32[2,192,384]{2,1,0:T(8,128)S(1)} %bitcast.21, ...), custom_call_target="tpu_custom_call" | custom-call | bytes 10800000 | tf_op jit(solution)/shard_map/fast_grad/pallas_call | solution.py:478
  108.8 5.3 %all-to-all-start.2 = ((bf16[224,8,128]{2,1,0:T(8,128)(2,1)}), bf16[224,8,128]{2,1,0:T(8,128)(2,1)S(1)}, u32[]{:S(2)}, u32[]{:S(2)}) async-start(bf16[224,8,128]{2,1,0:T(8,128)(2,1)} %fast_grad.5), calls=%async_computation.2 | async-start | bytes 917504 | tf_op jit(solution)/shard_map/all_to_all | solution.py:570
  114.1 0.1 collective-permute-start.20
  114.1 2.7 %collective-permute-start.21 = (bf16[768,384]{1,0:T(8,128)(2,1)}, bf16[768,384]{1,0:T(8,128)(2,1)S(1)}, u32[]{:S(2)}, u32[]{:S(2)}) collective-permute-start(bf16[768,384]{1,0:T(8,128)(2,1)} %get-tuple-element.74), channel_id=1, source_target_pairs={{0,3},{1,0},{2,1},{3,2},{4,7},{5,4},{6,5},{7,6},{8,11},{9,8},{10,9... | collective-permute-start | bytes 1769480 | tf_op jit(solution)/shard_map/ppermute | solution.py:574
  116.8 8.3 %all-to-all-done.2 = bf16[224,8,128]{2,1,0:T(8,128)(2,1)S(1)} async-done(((bf16[224,8,128]{2,1,0:T(8,128)(2,1)}), bf16[224,8,128]{2,1,0:T(8,128)(2,1)S(1)}, u32[]{:S(2)}, u32[]{:S(2)}) %all-to-all-start.2) | async-done | bytes 458784 | tf_op jit(solution)/shard_map/all_to_all | solution.py:570
  125.1 0.9 sum_pieces.1
  126.0 3.7 %all-to-all-start.3 = ((bf16[32,7,8,128]{3,2,1,0:T(8,128)(2,1)}), bf16[32,7,8,128]{3,2,1,0:T(8,128)(2,1)S(1)}, u32[]{:S(2)}, u32[]{:S(2)}) async-start(bf16[32,7,8,128]{3,2,1,0:T(8,128)(2,1)} %sum_pieces.1), calls=%async_computation.3 | async-start | bytes 917504 | tf_op jit(solution)/shard_map/all_to_all | solution.py:570
  129.7 0.2 collective-permute-done.20.refs_1_
  129.9 0.1 collective-permute-start.22
  130.0 0.0 collective-permute-done.21.refs_2_
  130.1 2.7 %collective-permute-start.23 = (bf16[256,384]{1,0:T(8,128)(2,1)S(1)}, bf16[256,384]{1,0:T(8,128)(2,1)S(1)}, u32[]{:S(2)}, u32[]{:S(2)}) collective-permute-start(bf16[256,384]{1,0:T(8,128)(2,1)S(1)} %slice.9), channel_id=1, source_target_pairs={{0,3},{1,0},{2,1},{3,2},{4,7},{5,4},{6,5},{7,6},{8,11},{9,8},{10,9... | collective-permute-start | bytes 589832 | tf_op jit(solution)/shard_map/ppermute | solution.py:574
  132.8 3.7 %collective-permute-done.22.refs_3_ = bf16[256,384]{1,0:T(8,128)(2,1)S(1)} collective-permute-done((bf16[256,384]{1,0:T(8,128)(2,1)S(1)}, bf16[256,384]{1,0:T(8,128)(2,1)S(1)}, u32[]{:S(2)}, u32[]{:S(2)}) %collective-permute-start.22) | collective-permute-done | bytes 196640 | tf_op jit(solution)/shard_map/ppermute | solution.py:574
  136.4 0.0 collective-permute-done.23.refs_4_
  136.4 4.1 %all-to-all-done.3 = bf16[32,7,8,128]{3,2,1,0:T(8,128)(2,1)S(1)} async-done(((bf16[32,7,8,128]{3,2,1,0:T(8,128)(2,1)}), bf16[32,7,8,128]{3,2,1,0:T(8,128)(2,1)S(1)}, u32[]{:S(2)}, u32[]{:S(2)}) %all-to-all-start.3) | async-done | bytes 458784 | tf_op jit(solution)/shard_map/all_to_all | solution.py:570
  140.5 4.0 %apply_fast.1 = bf16[192,2048]{1,0:T(8,128)(2,1)} custom-call(s32[4]{0:T(128)S(1)} %get-tuple-element.41.flag_ref.head_ref, bf16[224,8,128]{2,1,0:T(8,128)(2,1)S(1)} %bitcast.28, f32[2,192,384]{2,1,0:T(8,128)S(1)} %bitcast.22, f32[192,384]{1,0:T(8,128)S(1)} %bitcast.26, bf16[512,384]{1,0:T(8,128)(2,1)S(1)} %get-tuple-element.72.refs_0_, ...), custom_call_target="tpu_custom_call" | custom-call | bytes 10800000 | tf_op jit(solution)/shard_map/apply_fast/pallas_call | solution.py:552
  (31 shorter events, 0.1 us)
Async XLA Ops:
  4.1 9.6 %copy-start.2 = (bf16[352,768]{1,0:T(8,128)(2,1)S(1)}, bf16[352,768]{1,0:T(8,128)(2,1)}, u32[]{:S(2)}) copy-start(bf16[352,768]{1,0:T(8,128)(2,1)} %get-tuple-element.43.refs_0_) | copy-start | bytes 1622020
  4.2 38.9 %all-to-all-start = ((bf16[32,25,8,128]{3,2,1,0:T(8,128)(2,1)}), bf16[32,25,8,128]{3,2,1,0:T(8,128)(2,1)S(1)}, u32[]{:S(2)}, u32[]{:S(2)}) async-start(bf16[32,25,8,128]{3,2,1,0:T(8,128)(2,1)} %get-tuple-element.40), calls=%async_computation | async-start | bytes 3276800 | tf_op jit(solution)/shard_map/all_to_all | solution.py:570
  13.7 43.7 %copy-start.10 = (f32[768]{0:T(1024)S(1)}, f32[768]{0:T(1024)}, u32[]{:S(2)}) copy-start(f32[768]{0:T(1024)} %param.17) | copy-start | bytes 9220
  13.8 43.6 %copy-start.11 = (f32[768]{0:T(1024)S(1)}, f32[768]{0:T(1024)}, u32[]{:S(2)}) copy-start(f32[768]{0:T(1024)} %param.14) | copy-start | bytes 9220
  13.8 15.1 %collective-permute-start.2 = (bf16[352,768]{1,0:T(8,128)(2,1)S(1)}, bf16[352,768]{1,0:T(8,128)(2,1)S(1)}, u32[]{:S(2)}, u32[]{:S(2)}) collective-permute-start(bf16[352,768]{1,0:T(8,128)(2,1)S(1)} %copy-done.2), channel_id=1, source_target_pairs={{0,1},{1,2},{2,3},{3,0},{4,5},{5,6},{6,7},{7,4},{8,9},{9,10},{10,1... | collective-permute-start | bytes 1622024 | tf_op jit(solution)/shard_map/ppermute | solution.py:574
  15.1 3.8 %collective-permute-start.7 = (bf16[336,768]{1,0:T(8,128)(2,1)}, bf16[336,768]{1,0:T(8,128)(2,1)S(1)}, u32[]{:S(2)}, u32[]{:S(2)}) collective-permute-start(bf16[336,768]{1,0:T(8,128)(2,1)} %get-tuple-element.44.refs_1_), channel_id=1, source_target_pairs={{0,4},{4,0},{1,5},{5,1},{2,6},{6,2},{3,7},{7,3},{8,12},{12,8},{9,1... | collective-permute-start | bytes 1548296 | tf_op jit(solution)/shard_map/ppermute | solution.py:578
  15.7 24.3 %collective-permute-start.5 = (bf16[336,768]{1,0:T(8,128)(2,1)}, bf16[336,768]{1,0:T(8,128)(2,1)}, u32[]{:S(2)}, u32[]{:S(2)}) collective-permute-start(bf16[336,768]{1,0:T(8,128)(2,1)} %get-tuple-element.44.refs_1_), channel_id=1, source_target_pairs={{0,1},{1,2},{2,3},{3,0},{4,5},{5,6},{6,7},{7,4},{8,9},{9,10},{10,1... | collective-permute-start | bytes 1548296 | tf_op jit(solution)/shard_map/ppermute | solution.py:574
  17.0 24.6 %collective-permute-start.1 = (bf16[336,768]{1,0:T(8,128)(2,1)}, bf16[336,768]{1,0:T(8,128)(2,1)}, u32[]{:S(2)}, u32[]{:S(2)}) collective-permute-start(bf16[336,768]{1,0:T(8,128)(2,1)} %get-tuple-element.44.refs_1_), channel_id=1, source_target_pairs={{0,3},{1,0},{2,1},{3,2},{4,7},{5,4},{6,5},{7,6},{8,11},{9,8},{10,9... | collective-permute-start | bytes 1548296 | tf_op jit(solution)/shard_map/ppermute | solution.py:574
  18.3 35.2 %collective-permute-start.6 = (bf16[352,768]{1,0:T(8,128)(2,1)S(1)}, bf16[352,768]{1,0:T(8,128)(2,1)S(1)}, u32[]{:S(2)}, u32[]{:S(2)}) collective-permute-start(bf16[352,768]{1,0:T(8,128)(2,1)S(1)} %copy-done.2), channel_id=1, source_target_pairs={{0,4},{4,0},{1,5},{5,1},{2,6},{6,2},{3,7},{7,3},{8,12},{12,8},{9,1... | collective-permute-start | bytes 1622024 | tf_op jit(solution)/shard_map/ppermute | solution.py:578
  18.9 22.7 %copy-start.7 = (bf16[336,768]{1,0:T(8,128)(2,1)}, bf16[336,768]{1,0:T(8,128)(2,1)S(1)}, u32[]{:S(2)}) copy-start(bf16[336,768]{1,0:T(8,128)(2,1)S(1)} %collective-permute-done.7.refs_9_) | copy-start | bytes 1548292
  18.9 35.8 %collective-permute-start = (bf16[352,768]{1,0:T(8,128)(2,1)S(1)}, bf16[352,768]{1,0:T(8,128)(2,1)}, u32[]{:S(2)}, u32[]{:S(2)}) collective-permute-start(bf16[352,768]{1,0:T(8,128)(2,1)S(1)} %copy-done.2), channel_id=1, source_target_pairs={{0,3},{1,0},{2,1},{3,2},{4,7},{5,4},{6,5},{7,6},{8,11},{9,8},{10,9... | collective-permute-start | bytes 1622024 | tf_op jit(solution)/shard_map/ppermute | solution.py:574
  28.8 41.7 %copy-start.3 = (bf16[352,768]{1,0:T(8,128)(2,1)}, bf16[352,768]{1,0:T(8,128)(2,1)S(1)}, u32[]{:S(2)}) copy-start(bf16[352,768]{1,0:T(8,128)(2,1)S(1)} %collective-permute-done.2.refs_6_) | copy-start | bytes 1622020
  28.8 26.0 %collective-permute-start.3 = (bf16[352,768]{1,0:T(8,128)(2,1)S(1)}, bf16[352,768]{1,0:T(8,128)(2,1)}, u32[]{:S(2)}, u32[]{:S(2)}) collective-permute-start(bf16[352,768]{1,0:T(8,128)(2,1)S(1)} %collective-permute-done.2.refs_6_), channel_id=1, source_target_pairs={{0,1},{1,2},{2,3},{3,0},{4,5},{5,6},{6,7},{7,4},{8,9},{9,10},{10,1... | collective-permute-start | bytes 1622024 | tf_op jit(solution)/shard_map/ppermute | solution.py:574
  40.0 15.3 %collective-permute-start.13 = (bf16[336,768]{1,0:T(8,128)(2,1)}, bf16[336,768]{1,0:T(8,128)(2,1)}, u32[]{:S(2)}, u32[]{:S(2)}) collective-permute-start(bf16[336,768]{1,0:T(8,128)(2,1)} %collective-permute-done.5.refs_7_), channel_id=1, source_target_pairs={{0,4},{4,0},{1,5},{5,1},{2,6},{6,2},{3,7},{7,3},{8,12},{12,8},{9,1... | collective-permute-start | bytes 1548296 | tf_op jit(solution)/shard_map/ppermute | solution.py:578
  41.6 13.8 %collective-permute-start.4 = (bf16[336,768]{1,0:T(8,128)(2,1)}, bf16[336,768]{1,0:T(8,128)(2,1)}, u32[]{:S(2)}, u32[]{:S(2)}) collective-permute-start(bf16[336,768]{1,0:T(8,128)(2,1)} %collective-permute-done.1.refs_3_), channel_id=1, source_target_pairs={{0,3},{1,0},{2,1},{3,2},{4,7},{5,4},{6,5},{7,6},{8,11},{9,8},{10,9... | collective-permute-start | bytes 1548296 | tf_op jit(solution)/shard_map/ppermute | solution.py:574
  46.4 24.1 %all-to-all-start.1 = ((bf16[128,3,8,128]{3,2,1,0:T(8,128)(2,1)}), bf16[128,3,8,128]{3,2,1,0:T(8,128)(2,1)S(1)}, u32[]{:S(2)}, u32[]{:S(2)}) async-start(bf16[128,3,8,128]{3,2,1,0:T(8,128)(2,1)} %get-tuple-element.42), calls=%async_computation.1 | async-start | bytes 1572864 | tf_op jit(solution)/shard_map/all_to_all | solution.py:570
  53.6 16.9 %copy-start.4 = (bf16[352,768]{1,0:T(8,128)(2,1)}, bf16[352,768]{1,0:T(8,128)(2,1)S(1)}, u32[]{:S(2)}) copy-start(bf16[352,768]{1,0:T(8,128)(2,1)S(1)} %collective-permute-done.6.refs_8_) | copy-start | bytes 1622020
  53.6 5.2 %collective-permute-start.12 = (bf16[352,768]{1,0:T(8,128)(2,1)S(1)}, bf16[352,768]{1,0:T(8,128)(2,1)S(1)}, u32[]{:S(2)}, u32[]{:S(2)}) collective-permute-start(bf16[352,768]{1,0:T(8,128)(2,1)S(1)} %collective-permute-done.2.refs_6_), channel_id=1, source_target_pairs={{0,4},{4,0},{1,5},{5,1},{2,6},{6,2},{3,7},{7,3},{8,12},{12,8},{9,1... | collective-permute-start | bytes 1622024 | tf_op jit(solution)/shard_map/ppermute | solution.py:578
  54.7 4.1 %collective-permute-start.8 = (bf16[352,768]{1,0:T(8,128)(2,1)}, bf16[352,768]{1,0:T(8,128)(2,1)S(1)}, u32[]{:S(2)}, u32[]{:S(2)}) collective-permute-start(bf16[352,768]{1,0:T(8,128)(2,1)} %collective-permute-done.refs_2_), channel_id=1, source_target_pairs={{0,4},{4,0},{1,5},{5,1},{2,6},{6,2},{3,7},{7,3},{8,12},{12,8},{9,1... | collective-permute-start | bytes 1622024 | tf_op jit(solution)/shard_map/ppermute | solution.py:578
  54.9 5.7 %collective-permute-start.10 = (bf16[352,768]{1,0:T(8,128)(2,1)}, bf16[352,768]{1,0:T(8,128)(2,1)}, u32[]{:S(2)}, u32[]{:S(2)}) collective-permute-start(bf16[352,768]{1,0:T(8,128)(2,1)} %collective-permute-done.3.refs_4_), channel_id=1, source_target_pairs={{0,4},{4,0},{1,5},{5,1},{2,6},{6,2},{3,7},{7,3},{8,12},{12,8},{9,1... | collective-permute-start | bytes 1622024 | tf_op jit(solution)/shard_map/ppermute | solution.py:578
  55.3 3.5 %collective-permute-start.9 = (bf16[336,768]{1,0:T(8,128)(2,1)}, bf16[336,768]{1,0:T(8,128)(2,1)S(1)}, u32[]{:S(2)}, u32[]{:S(2)}) collective-permute-start(bf16[336,768]{1,0:T(8,128)(2,1)} %collective-permute-done.1.refs_3_), channel_id=1, source_target_pairs={{0,4},{4,0},{1,5},{5,1},{2,6},{6,2},{3,7},{7,3},{8,12},{12,8},{9,1... | collective-permute-start | bytes 1548296 | tf_op jit(solution)/shard_map/ppermute | solution.py:578
  55.4 4.2 %collective-permute-start.11 = (bf16[336,768]{1,0:T(8,128)(2,1)}, bf16[336,768]{1,0:T(8,128)(2,1)S(1)}, u32[]{:S(2)}, u32[]{:S(2)}) collective-permute-start(bf16[336,768]{1,0:T(8,128)(2,1)} %collective-permute-done.4.refs_5_), channel_id=1, source_target_pairs={{0,4},{4,0},{1,5},{5,1},{2,6},{6,2},{3,7},{7,3},{8,12},{12,8},{9,1... | collective-permute-start | bytes 1548296 | tf_op jit(solution)/shard_map/ppermute | solution.py:578
  58.8 0.8 copy-start.8
  58.8 11.7 %copy-start.5 = (bf16[352,768]{1,0:T(8,128)(2,1)}, bf16[352,768]{1,0:T(8,128)(2,1)S(1)}, u32[]{:S(2)}) copy-start(bf16[352,768]{1,0:T(8,128)(2,1)S(1)} %collective-permute-done.12.refs_14_) | copy-start | bytes 1622020
  58.8 11.7 %copy-start.6 = (bf16[352,768]{1,0:T(8,128)(2,1)}, bf16[352,768]{1,0:T(8,128)(2,1)S(1)}, u32[]{:S(2)}) copy-start(bf16[352,768]{1,0:T(8,128)(2,1)S(1)} %collective-permute-done.8.refs_10_) | copy-start | bytes 1622020
  59.6 0.9 copy-start.9
  81.5 11.8 %collective-permute-start.14 = (bf16[256,384]{1,0:T(8,128)(2,1)S(1)}, bf16[256,384]{1,0:T(8,128)(2,1)S(1)}, u32[]{:S(2)}, u32[]{:S(2)}) collective-permute-start(bf16[256,384]{1,0:T(8,128)(2,1)S(1)} %get-tuple-element.53), channel_id=1, source_target_pairs={{0,1},{1,2},{2,3},{3,0},{4,5},{5,6},{6,7},{7,4},{8,9},{9,10},{10,1... | collective-permute-start | bytes 589832 | tf_op jit(solution)/shard_map/ppermute | solution.py:574
  81.9 11.3 %collective-permute-start.15 = (bf16[256,384]{1,0:T(8,128)(2,1)S(1)}, bf16[256,384]{1,0:T(8,128)(2,1)S(1)}, u32[]{:S(2)}, u32[]{:S(2)}) collective-permute-start(bf16[256,384]{1,0:T(8,128)(2,1)S(1)} %get-tuple-element.54), channel_id=1, source_target_pairs={{0,2},{1,3},{2,0},{3,1},{4,6},{5,7},{6,4},{7,5},{8,10},{9,11},{10,... | collective-permute-start | bytes 589832 | tf_op jit(solution)/shard_map/ppermute | solution.py:574
  83.3 10.2 %collective-permute-start.16 = (bf16[256,384]{1,0:T(8,128)(2,1)S(1)}, bf16[256,384]{1,0:T(8,128)(2,1)S(1)}, u32[]{:S(2)}, u32[]{:S(2)}) collective-permute-start(bf16[256,384]{1,0:T(8,128)(2,1)S(1)} %get-tuple-element.55), channel_id=1, source_target_pairs={{0,3},{1,0},{2,1},{3,2},{4,7},{5,4},{6,5},{7,6},{8,11},{9,8},{10,9... | collective-permute-start | bytes 589832 | tf_op jit(solution)/shard_map/ppermute | solution.py:574
  93.6 11.1 %collective-permute-start.17 = (bf16[256,384]{1,0:T(8,128)(2,1)S(1)}, bf16[256,384]{1,0:T(8,128)(2,1)S(1)}, u32[]{:S(2)}, u32[]{:S(2)}) collective-permute-start(bf16[256,384]{1,0:T(8,128)(2,1)S(1)} %get-tuple-element.56), channel_id=1, source_target_pairs={{0,1},{1,2},{2,3},{3,0},{4,5},{5,6},{6,7},{7,4},{8,9},{9,10},{10,1... | collective-permute-start | bytes 589832 | tf_op jit(solution)/shard_map/ppermute | solution.py:574
  94.5 11.7 %collective-permute-start.18 = (bf16[256,384]{1,0:T(8,128)(2,1)S(1)}, bf16[256,384]{1,0:T(8,128)(2,1)S(1)}, u32[]{:S(2)}, u32[]{:S(2)}) collective-permute-start(bf16[256,384]{1,0:T(8,128)(2,1)S(1)} %get-tuple-element.57), channel_id=1, source_target_pairs={{0,2},{1,3},{2,0},{3,1},{4,6},{5,7},{6,4},{7,5},{8,10},{9,11},{10,... | collective-permute-start | bytes 589832 | tf_op jit(solution)/shard_map/ppermute | solution.py:574
  97.7 8.6 %collective-permute-start.19 = (bf16[256,384]{1,0:T(8,128)(2,1)S(1)}, bf16[256,384]{1,0:T(8,128)(2,1)S(1)}, u32[]{:S(2)}, u32[]{:S(2)}) collective-permute-start(bf16[256,384]{1,0:T(8,128)(2,1)S(1)} %get-tuple-element.58), channel_id=1, source_target_pairs={{0,3},{1,0},{2,1},{3,2},{4,7},{5,4},{6,5},{7,6},{8,11},{9,8},{10,9... | collective-permute-start | bytes 589832 | tf_op jit(solution)/shard_map/ppermute | solution.py:574
  97.7 4.1 %copy-start = (f32[1,2,192,384]{3,2,1,0:T(8,128)S(1)}, f32[1,2,192,384]{3,2,1,0:T(8,128)}, u32[]{:S(2)}) copy-start(f32[1,2,192,384]{3,2,1,0:T(8,128)} %param.20) | copy-start | bytes 1769476
  97.7 4.1 %copy-start.1 = (f32[1,384,192]{1,2,0:T(8,128)S(1)}, f32[1,384,192]{1,2,0:T(8,128)}, u32[]{:S(2)}) copy-start(f32[1,384,192]{1,2,0:T(8,128)} %param.21) | copy-start | bytes 884740
  108.8 16.4 %all-to-all-start.2 = ((bf16[224,8,128]{2,1,0:T(8,128)(2,1)}), bf16[224,8,128]{2,1,0:T(8,128)(2,1)S(1)}, u32[]{:S(2)}, u32[]{:S(2)}) async-start(bf16[224,8,128]{2,1,0:T(8,128)(2,1)} %fast_grad.5), calls=%async_computation.2 | async-start | bytes 917504 | tf_op jit(solution)/shard_map/all_to_all | solution.py:570
  114.1 15.8 %collective-permute-start.20 = (bf16[768,384]{1,0:T(8,128)(2,1)S(1)}, bf16[768,384]{1,0:T(8,128)(2,1)S(1)}, u32[]{:S(2)}, u32[]{:S(2)}) collective-permute-start(bf16[768,384]{1,0:T(8,128)(2,1)S(1)} %get-tuple-element.73), channel_id=1, source_target_pairs={{0,1},{1,2},{2,3},{3,0},{4,5},{5,6},{6,7},{7,4},{8,9},{9,10},{10,1... | collective-permute-start | bytes 1769480 | tf_op jit(solution)/shard_map/ppermute | solution.py:574
  114.1 15.9 %collective-permute-start.21 = (bf16[768,384]{1,0:T(8,128)(2,1)}, bf16[768,384]{1,0:T(8,128)(2,1)S(1)}, u32[]{:S(2)}, u32[]{:S(2)}) collective-permute-start(bf16[768,384]{1,0:T(8,128)(2,1)} %get-tuple-element.74), channel_id=1, source_target_pairs={{0,3},{1,0},{2,1},{3,2},{4,7},{5,4},{6,5},{7,6},{8,11},{9,8},{10,9... | collective-permute-start | bytes 1769480 | tf_op jit(solution)/shard_map/ppermute | solution.py:574
  126.0 14.5 %all-to-all-start.3 = ((bf16[32,7,8,128]{3,2,1,0:T(8,128)(2,1)}), bf16[32,7,8,128]{3,2,1,0:T(8,128)(2,1)S(1)}, u32[]{:S(2)}, u32[]{:S(2)}) async-start(bf16[32,7,8,128]{3,2,1,0:T(8,128)(2,1)} %sum_pieces.1), calls=%async_computation.3 | async-start | bytes 917504 | tf_op jit(solution)/shard_map/all_to_all | solution.py:570
  129.9 6.5 %collective-permute-start.22 = (bf16[256,384]{1,0:T(8,128)(2,1)S(1)}, bf16[256,384]{1,0:T(8,128)(2,1)S(1)}, u32[]{:S(2)}, u32[]{:S(2)}) collective-permute-start(bf16[256,384]{1,0:T(8,128)(2,1)S(1)} %slice.8), channel_id=1, source_target_pairs={{0,1},{1,2},{2,3},{3,0},{4,5},{5,6},{6,7},{7,4},{8,9},{9,10},{10,1... | collective-permute-start | bytes 589832 | tf_op jit(solution)/shard_map/ppermute | solution.py:574
  130.1 6.4 %collective-permute-start.23 = (bf16[256,384]{1,0:T(8,128)(2,1)S(1)}, bf16[256,384]{1,0:T(8,128)(2,1)S(1)}, u32[]{:S(2)}, u32[]{:S(2)}) collective-permute-start(bf16[256,384]{1,0:T(8,128)(2,1)S(1)} %slice.9), channel_id=1, source_target_pairs={{0,3},{1,0},{2,1},{3,2},{4,7},{5,4},{6,5},{7,6},{8,11},{9,8},{10,9... | collective-permute-start | bytes 589832 | tf_op jit(solution)/shard_map/ppermute | solution.py:574

commit v6 on v5

--- a/solution.py
+++ b/solution.py
@@ -525,9 +525,9 @@
             )
         init = down_ref[...] if i == 2 else gu_ref[i]
         ws[i] = renorm(init - gs[i], init, 0 if i == 2 else 1).astype(BF)
-    row = lax.broadcasted_iota(jnp.int32, (FW, 2 * FW), 0)
-    col = lax.broadcasted_iota(jnp.int32, (FW, 2 * FW), 1)
-    columns = jnp.where(row + FW == col, 1.0, 0.0).astype(BF)
+    row = lax.broadcasted_iota(jnp.int32, (FW, 2 * FW - 128), 0)
+    col = lax.broadcasted_iota(jnp.int32, (FW, 2 * FW - 128), 1)
+    columns = jnp.where(row + FW - 128 == col, 1.0, 0.0).astype(BF)
     own_ref, up_ref, down_side_ref, far0_ref, far1_ref = qe_refs
     puts = []
     for d in (0, 1, 3, 2):
@@ -539,7 +539,7 @@
         gate = mm(q, ws[0])
         hidden = (gate * jax.nn.sigmoid(gate) * mm(q, ws[1])).astype(BF)
         base = pl.multiple_of(((head_ref[2] + HEADS - d) & (HEADS - 1)) * SPAN, SPAN)
-        o_buf[d] = (mm_nt(columns, qe) + mm_nt(ws[2], hidden)).astype(BF)
+        o_buf[d] = (mm_nt(columns, qe[:, 128:]) + mm_nt(ws[2], hidden)).astype(BF)
         puts.append(
             pltpu.make_async_copy(o_buf.at[d], o_ref.at[:, pl.ds(base, SPAN)], sems.at[d])
         )
@@ -606,8 +606,9 @@
         w_out,
         jnp.transpose(w_fast, (0, 2, 1)).reshape(3 * FW, D),
     )
-    before = (shifted(low, 1), shifted(high, 1))
-    after = (shifted(low, -1), shifted(high, -1))
+    after_high, before_low = shifted(high, -1), shifted(low, 1)
+    after = (shifted(low, -1), after_high)
+    before = (before_low, shifted(high, 1))
     picked, flags = pick(at, exchange(pieces, SEQ_AXES))
     mine = exchange(picked, ALL_AXES)
     far = (shifted(before[0], 1), shifted(after[1], -1))

time: 145 us -> 145 us (level)
  no operation moved by 1% of the time
where the time goes in v6:
time: 145 us
  waiting for transfers between devices  52.9 us (36%)
  starting transfers between devices  50.6 us (35%)
  Pallas kernels  39.5 us (27%)
    ppermute x16, waiting for transfers between devices, shifted(): lax.ppermute(x, 'head', [(i, (i + by) % HEADS) for i in range(HEADS)])  28.3 us
    all_to_all x4, starting transfers between devices, exchange(): return lax.all_to_all(x, axes, split_axis=0, concat_axis=0, tiled=True)  25.7 us
    all_to_all x4, waiting for transfers between devices, exchange(): return lax.all_to_all(x, axes, split_axis=0, concat_axis=0, tiled=True)  22.4 us
    ppermute x16, starting transfers between devices, shifted(): lax.ppermute(x, 'head', [(i, (i + by) % HEADS) for i in range(HEADS)])  18.5 us
    pallas_call x1, Pallas kernels, encode_first(): pl.pallas_call(encode_first_body, out_shape=(jax.ShapeDtypeStruct((BLK, D...  10.9 us
    pallas_call x1, Pallas kernels, encode_second(): pl.pallas_call(encode_second_body, out_shape=(jax.ShapeDtypeStruct((BLK,...  6.99 us
    ppermute x8, starting transfers between devices, swapped(): return lax.ppermute(x, 'core', [(0, 1), (1, 0)])  6.41 us
    pallas_call x3, Pallas kernels, fast(): pl.pallas_call(make_fast_body(len(blocks), first, last), out_shape=jax.Sh...  5.42 us
  transfers between devices with their start and end apart: 28, of which 12 were waited for; matrix products, arithmetic and copies ran while one was open for 0% of the time, Pallas kernels for 13%

profile of v6, /device:TPU:1, one launch (start us, length us, event | category | flops | bytes accessed | tf_op | source)
XLA Modules:
  0.0 144.6 jit_solution(14886463187738889030)
XLA Ops:
  0.0 0.1 pad_add_fusion.at_ref
  0.1 4.1 %spread.1 = (bf16[32,25,8,128]{3,2,1,0:T(8,128)(2,1)}, bf16[352,768]{1,0:T(8,128)(2,1)}, bf16[336,768]{1,0:T(8,128)(2,1)}) custom-call(s32[3]{0:T(128)S(1)} %pad_add_fusion.at_ref, s32[16]{0:T(128)} %dest_hbm.1, s32[16]{0:T(128)} %image_hbm.1, bf16[512,8,768]{2,1,0:T(8,128)(2,1)} %bitcast.30, bf16[1,768]{1,0:T(2,128)(2,1)} %bitcast.33, ...), custom_call_target="tpu_custom_call" | custom-call | bytes 10800000 | tf_op jit(solution)/shard_map/spread/pallas_call | solution.py:142
  4.2 9.6 %all-to-all-start = ((bf16[32,25,8,128]{3,2,1,0:T(8,128)(2,1)}), bf16[32,25,8,128]{3,2,1,0:T(8,128)(2,1)S(1)}, u32[]{:S(2)}, u32[]{:S(2)}) async-start(bf16[32,25,8,128]{3,2,1,0:T(8,128)(2,1)} %get-tuple-element.40), calls=%async_computation | async-start | bytes 3276800 | tf_op jit(solution)/shard_map/all_to_all | solution.py:570
  13.7 0.0 copy-start.10
  13.8 0.0 copy-start.11
  13.8 1.4 collective-permute-start.2
  15.1 0.5 collective-permute-start.7
  15.7 1.3 collective-permute-start.5
  17.0 1.4 collective-permute-start.1
  18.3 0.6 collective-permute-start.6
  18.9 0.0 collective-permute-done.7.refs_9_
  18.9 0.3 collective-permute-start
  19.2 9.6 %collective-permute-done.2.refs_6_ = bf16[352,768]{1,0:T(8,128)(2,1)S(1)} collective-permute-done((bf16[352,768]{1,0:T(8,128)(2,1)S(1)}, bf16[352,768]{1,0:T(8,128)(2,1)S(1)}, u32[]{:S(2)}, u32[]{:S(2)}) %collective-permute-start.2) | collective-permute-done | bytes 540704 | tf_op jit(solution)/shard_map/ppermute | solution.py:574
  28.8 0.1 collective-permute-start.3
  28.9 11.1 %collective-permute-done.5.refs_7_ = bf16[336,768]{1,0:T(8,128)(2,1)} collective-permute-done((bf16[336,768]{1,0:T(8,128)(2,1)}, bf16[336,768]{1,0:T(8,128)(2,1)}, u32[]{:S(2)}, u32[]{:S(2)}) %collective-permute-start.5) | collective-permute-done | bytes 516128 | tf_op jit(solution)/shard_map/ppermute | solution.py:574
  40.0 1.6 %collective-permute-start.13 = (bf16[336,768]{1,0:T(8,128)(2,1)}, bf16[336,768]{1,0:T(8,128)(2,1)}, u32[]{:S(2)}, u32[]{:S(2)}) collective-permute-start(bf16[336,768]{1,0:T(8,128)(2,1)} %collective-permute-done.5.refs_7_), channel_id=1, source_target_pairs={{0,4},{4,0},{1,5},{5,1},{2,6},{6,2},{3,7},{7,3},{8,12},{12,8},{9,1... | collective-permute-start | bytes 1548296 | tf_op jit(solution)/shard_map/ppermute | solution.py:578
  41.6 1.5 %collective-permute-start.4 = (bf16[336,768]{1,0:T(8,128)(2,1)}, bf16[336,768]{1,0:T(8,128)(2,1)}, u32[]{:S(2)}, u32[]{:S(2)}) collective-permute-start(bf16[336,768]{1,0:T(8,128)(2,1)} %collective-permute-done.1.refs_3_), channel_id=1, source_target_pairs={{0,3},{1,0},{2,1},{3,2},{4,7},{5,4},{6,5},{7,6},{8,11},{9,8},{10,9... | collective-permute-start | bytes 1548296 | tf_op jit(solution)/shard_map/ppermute | solution.py:574
  43.1 3.3 %pick.1 = (bf16[128,3,8,128]{3,2,1,0:T(8,128)(2,1)}, s32[4]{0:T(128)S(1)}) custom-call(s32[3]{0:T(128)S(1)} %pad_add_fusion.at_ref, bf16[32,25,8,128]{3,2,1,0:T(8,128)(2,1)S(1)} %all-to-all-done.x_ref), custom_call_target="tpu_custom_call" | custom-call | bytes 10800000 | tf_op jit(solution)/shard_map/pick/pallas_call | solution.py:202
  46.4 7.1 %all-to-all-start.1 = ((bf16[128,3,8,128]{3,2,1,0:T(8,128)(2,1)}), bf16[128,3,8,128]{3,2,1,0:T(8,128)(2,1)S(1)}, u32[]{:S(2)}, u32[]{:S(2)}) async-start(bf16[128,3,8,128]{3,2,1,0:T(8,128)(2,1)} %get-tuple-element.42), calls=%async_computation.1 | async-start | bytes 1572864 | tf_op jit(solution)/shard_map/all_to_all | solution.py:570
  53.6 1.1 collective-permute-start.12
  54.7 0.0 collective-permute-done.refs_2_
  54.7 0.1 collective-permute-start.8
  54.9 0.4 collective-permute-start.10
  55.3 0.0 collective-permute-done.13.refs_15_
  55.3 0.1 collective-permute-start.9
  55.4 2.0 %collective-permute-start.11 = (bf16[336,768]{1,0:T(8,128)(2,1)}, bf16[336,768]{1,0:T(8,128)(2,1)S(1)}, u32[]{:S(2)}, u32[]{:S(2)}) collective-permute-start(bf16[336,768]{1,0:T(8,128)(2,1)} %collective-permute-done.4.refs_5_), channel_id=1, source_target_pairs={{0,4},{4,0},{1,5},{5,1},{2,6},{6,2},{3,7},{7,3},{8,12},{12,8},{9,1... | collective-permute-start | bytes 1548296 | tf_op jit(solution)/shard_map/ppermute | solution.py:578
  57.4 1.4 collective-permute-done.9.refs_11_
  58.8 0.0 collective-permute-done.12.refs_14_
  58.8 0.7 collective-permute-done.11.refs_13_
  59.5 0.1 copy-done.8
  59.6 0.9 copy-done.9
  60.5 0.0 collective-permute-done.10.refs_12_
  60.5 10.0 %all-to-all-done.1 = bf16[128,3,8,128]{3,2,1,0:T(8,128)(2,1)S(1)} async-done(((bf16[128,3,8,128]{3,2,1,0:T(8,128)(2,1)}), bf16[128,3,8,128]{3,2,1,0:T(8,128)(2,1)S(1)}, u32[]{:S(2)}, u32[]{:S(2)}) %all-to-all-start.1) | async-done | bytes 786464 | tf_op jit(solution)/shard_map/all_to_all | solution.py:570
  70.5 10.9 %encode_first.1 = (bf16[256,768]{1,0:T(8,128)(2,1)S(1)}, bf16[256,384]{1,0:T(8,128)(2,1)S(1)}, bf16[256,384]{1,0:T(8,128)(2,1)S(1)}, bf16[256,384]{1,0:T(8,128)(...) custom-call(s32[4]{0:T(128)S(1)} %get-tuple-element.41.flag_ref.head, ...), custom_call_target="tpu_custom_call" | custom-call | bytes 32400000 | tf_op jit(solution)/shard_map/encode_first/pallas_call | solution.py:318
  81.5 0.4 collective-permute-start.14
  81.9 1.4 collective-permute-start.15
  83.3 1.1 collective-permute-start.16
  84.4 7.0 %encode_second.1 = (bf16[256,768]{1,0:T(8,128)(2,1)S(1)}, bf16[256,384]{1,0:T(8,128)(2,1)S(1)}, bf16[256,384]{1,0:T(8,128)(2,1)S(1)}, bf16[256,384]{1,0:T(8,128)(2,1)S(1)}, bf16[256,384]{1,0:T(8,128)(2,1)S(1)}) custom-call(s32[4]{0:T(128)S(1)} %get-tuple-element.41.flag_ref.head_ref, f32[1,768]{1,0:T(1,128)S(1)} %reshape.27.fgain_ref.gain_ref, ...), custom_call_target="tpu_custom_call" | custom-call | bytes 72000000 | tf_op jit(solution)/shard_map/encode_second/pallas_call | solution.py:369
  91.4 1.8 %collective-permute-done.14.refs_0_ = bf16[256,384]{1,0:T(8,128)(2,1)S(1)} collective-permute-done((bf16[256,384]{1,0:T(8,128)(2,1)S(1)}, bf16[256,384]{1,0:T(8,128)(2,1)S(1)}, u32[]{:S(2)}, u32[]{:S(2)}) %collective-permute-start.14) | collective-permute-done | bytes 196640 | tf_op jit(solution)/shard_map/ppermute | solution.py:574
  93.2 0.0 collective-permute-done.15.refs_1_
  93.2 0.3 collective-permute-done.16.refs_2_
  93.6 1.0 collective-permute-start.17
  94.5 3.2 %collective-permute-start.18 = (bf16[256,384]{1,0:T(8,128)(2,1)S(1)}, bf16[256,384]{1,0:T(8,128)(2,1)S(1)}, u32[]{:S(2)}, u32[]{:S(2)}) collective-permute-start(bf16[256,384]{1,0:T(8,128)(2,1)S(1)} %get-tuple-element.57), channel_id=1, source_target_pairs={{0,2},{1,3},{2,0},{3,1},{4,6},{5,7},{6,4},{7,5},{8,10},{9,11},{10,... | collective-permute-start | bytes 589832 | tf_op jit(solution)/shard_map/ppermute | solution.py:574
  97.7 0.0 collective-permute-start.19
  97.7 4.1 %fast_query.1 = (bf16[512,384]{1,0:T(8,128)(2,1)S(1)}, bf16[768,384]{1,0:T(8,128)(2,1)S(1)}, bf16[768,384]{1,0:T(8,128)(2,1)}) custom-call(s32[4]{0:T(128)S(1)} %get-tuple-element.41.flag_ref.head_ref, bf16[256,768]{1,0:T(8,128)(2,1)S(1)} %get-tuple-element.59.x0_ref, bf16[256,768]{1,0:T(8,128)(2,1)S(1)} %get-tuple-element.60.x1_ref, ...), custom_call_target="tpu_custom_call" | custom-call | bytes 14400000 | tf_op jit(solution)/shard_map/fast_query/pallas_call | solution.py:418
  101.8 1.2 fast_grad.3.refs_5_
  102.9 1.7 %fast_grad.4.refs_5_ = f32[3,192,384]{2,1,0:T(8,128)S(1)} custom-call(bf16[256,384]{1,0:T(8,128)(2,1)S(1)} %collective-permute-done.14.refs_0_, bf16[256,384]{1,0:T(8,128)(2,1)S(1)} %collective-permute-done.15.refs_1_, bf16[256,384]{1,0:T(8,128)(2,1)S(1)} %collective-permute-done.16.refs_2_, f32[2,192,384]{2,1,0:T(8,128)S(1)} %bitcast.20, ...), custom_call_target="tpu_custom_call" | custom-call | bytes 10800000 | tf_op jit(solution)/shard_map/fast_grad/pallas_call | solution.py:478
  104.7 0.0 collective-permute-done.17.refs_0_
  104.7 1.6 %collective-permute-done.18.refs_1_ = bf16[256,384]{1,0:T(8,128)(2,1)S(1)} collective-permute-done((bf16[256,384]{1,0:T(8,128)(2,1)S(1)}, bf16[256,384]{1,0:T(8,128)(2,1)S(1)}, u32[]{:S(2)}, u32[]{:S(2)}) %collective-permute-start.18) | collective-permute-done | bytes 196640 | tf_op jit(solution)/shard_map/ppermute | solution.py:574
  106.3 0.0 collective-permute-done.19.refs_2_
  106.3 2.5 %fast_grad.5 = bf16[224,8,128]{2,1,0:T(8,128)(2,1)} custom-call(bf16[256,384]{1,0:T(8,128)(2,1)S(1)} %collective-permute-done.17.refs_0_, bf16[256,384]{1,0:T(8,128)(2,1)S(1)} %collective-permute-done.18.refs_1_, bf16[256,384]{1,0:T(8,128)(2,1)S(1)} %collective-permute-done.19.refs_2_, f32[2,192,384]{2,1,0:T(8,128)S(1)} %bitcast.21, ...), custom_call_target="tpu_custom_call" | custom-call | bytes 10800000 | tf_op jit(solution)/shard_map/fast_grad/pallas_call | solution.py:478
  108.8 5.3 %all-to-all-start.2 = ((bf16[224,8,128]{2,1,0:T(8,128)(2,1)}), bf16[224,8,128]{2,1,0:T(8,128)(2,1)S(1)}, u32[]{:S(2)}, u32[]{:S(2)}) async-start(bf16[224,8,128]{2,1,0:T(8,128)(2,1)} %fast_grad.5), calls=%async_computation.2 | async-start | bytes 917504 | tf_op jit(solution)/shard_map/all_to_all | solution.py:570
  114.1 0.1 collective-permute-start.20
  114.1 2.7 %collective-permute-start.21 = (bf16[768,384]{1,0:T(8,128)(2,1)}, bf16[768,384]{1,0:T(8,128)(2,1)S(1)}, u32[]{:S(2)}, u32[]{:S(2)}) collective-permute-start(bf16[768,384]{1,0:T(8,128)(2,1)} %get-tuple-element.74), channel_id=1, source_target_pairs={{0,3},{1,0},{2,1},{3,2},{4,7},{5,4},{6,5},{7,6},{8,11},{9,8},{10,9... | collective-permute-start | bytes 1769480 | tf_op jit(solution)/shard_map/ppermute | solution.py:574
  116.8 8.3 %all-to-all-done.2 = bf16[224,8,128]{2,1,0:T(8,128)(2,1)S(1)} async-done(((bf16[224,8,128]{2,1,0:T(8,128)(2,1)}), bf16[224,8,128]{2,1,0:T(8,128)(2,1)S(1)}, u32[]{:S(2)}, u32[]{:S(2)}) %all-to-all-start.2) | async-done | bytes 458784 | tf_op jit(solution)/shard_map/all_to_all | solution.py:570
  125.1 0.9 sum_pieces.1
  126.0 3.7 %all-to-all-start.3 = ((bf16[32,7,8,128]{3,2,1,0:T(8,128)(2,1)}), bf16[32,7,8,128]{3,2,1,0:T(8,128)(2,1)S(1)}, u32[]{:S(2)}, u32[]{:S(2)}) async-start(bf16[32,7,8,128]{3,2,1,0:T(8,128)(2,1)} %sum_pieces.1), calls=%async_computation.3 | async-start | bytes 917504 | tf_op jit(solution)/shard_map/all_to_all | solution.py:570
  129.7 0.2 collective-permute-done.20.refs_1_
  129.9 0.1 collective-permute-start.22
  130.0 0.0 collective-permute-done.21.refs_2_
  130.1 2.7 %collective-permute-start.23 = (bf16[256,384]{1,0:T(8,128)(2,1)S(1)}, bf16[256,384]{1,0:T(8,128)(2,1)S(1)}, u32[]{:S(2)}, u32[]{:S(2)}) collective-permute-start(bf16[256,384]{1,0:T(8,128)(2,1)S(1)} %slice.9), channel_id=1, source_target_pairs={{0,3},{1,0},{2,1},{3,2},{4,7},{5,4},{6,5},{7,6},{8,11},{9,8},{10,9... | collective-permute-start | bytes 589832 | tf_op jit(solution)/shard_map/ppermute | solution.py:574
  132.8 3.7 %collective-permute-done.22.refs_3_ = bf16[256,384]{1,0:T(8,128)(2,1)S(1)} collective-permute-done((bf16[256,384]{1,0:T(8,128)(2,1)S(1)}, bf16[256,384]{1,0:T(8,128)(2,1)S(1)}, u32[]{:S(2)}, u32[]{:S(2)}) %collective-permute-start.22) | collective-permute-done | bytes 196640 | tf_op jit(solution)/shard_map/ppermute | solution.py:574
  136.4 4.1 %all-to-all-done.3 = bf16[32,7,8,128]{3,2,1,0:T(8,128)(2,1)S(1)} async-done(((bf16[32,7,8,128]{3,2,1,0:T(8,128)(2,1)}), bf16[32,7,8,128]{3,2,1,0:T(8,128)(2,1)S(1)}, u32[]{:S(2)}, u32[]{:S(2)}) %all-to-all-start.3) | async-done | bytes 458784 | tf_op jit(solution)/shard_map/all_to_all | solution.py:570
  140.5 3.9 %apply_fast.1 = bf16[192,2048]{1,0:T(8,128)(2,1)} custom-call(s32[4]{0:T(128)S(1)} %get-tuple-element.41.flag_ref.head_ref, bf16[224,8,128]{2,1,0:T(8,128)(2,1)S(1)} %bitcast.28, f32[2,192,384]{2,1,0:T(8,128)S(1)} %bitcast.22, f32[192,384]{1,0:T(8,128)S(1)} %bitcast.26, bf16[512,384]{1,0:T(8,128)(2,1)S(1)} %get-tuple-element.72.refs_0_, ...), custom_call_target="tpu_custom_call" | custom-call | bytes 10800000 | tf_op jit(solution)/shard_map/apply_fast/pallas_call | solution.py:552
  (31 shorter events, 0.1 us)
Async XLA Ops:
  4.1 9.6 %copy-start.2 = (bf16[352,768]{1,0:T(8,128)(2,1)S(1)}, bf16[352,768]{1,0:T(8,128)(2,1)}, u32[]{:S(2)}) copy-start(bf16[352,768]{1,0:T(8,128)(2,1)} %get-tuple-element.43.refs_0_) | copy-start | bytes 1622020
  4.2 38.9 %all-to-all-start = ((bf16[32,25,8,128]{3,2,1,0:T(8,128)(2,1)}), bf16[32,25,8,128]{3,2,1,0:T(8,128)(2,1)S(1)}, u32[]{:S(2)}, u32[]{:S(2)}) async-start(bf16[32,25,8,128]{3,2,1,0:T(8,128)(2,1)} %get-tuple-element.40), calls=%async_computation | async-start | bytes 3276800 | tf_op jit(solution)/shard_map/all_to_all | solution.py:570
  13.7 43.7 %copy-start.10 = (f32[768]{0:T(1024)S(1)}, f32[768]{0:T(1024)}, u32[]{:S(2)}) copy-start(f32[768]{0:T(1024)} %param.17) | copy-start | bytes 9220
  13.8 43.6 %copy-start.11 = (f32[768]{0:T(1024)S(1)}, f32[768]{0:T(1024)}, u32[]{:S(2)}) copy-start(f32[768]{0:T(1024)} %param.14) | copy-start | bytes 9220
  13.8 15.1 %collective-permute-start.2 = (bf16[352,768]{1,0:T(8,128)(2,1)S(1)}, bf16[352,768]{1,0:T(8,128)(2,1)S(1)}, u32[]{:S(2)}, u32[]{:S(2)}) collective-permute-start(bf16[352,768]{1,0:T(8,128)(2,1)S(1)} %copy-done.2), channel_id=1, source_target_pairs={{0,1},{1,2},{2,3},{3,0},{4,5},{5,6},{6,7},{7,4},{8,9},{9,10},{10,1... | collective-permute-start | bytes 1622024 | tf_op jit(solution)/shard_map/ppermute | solution.py:574
  15.1 3.8 %collective-permute-start.7 = (bf16[336,768]{1,0:T(8,128)(2,1)}, bf16[336,768]{1,0:T(8,128)(2,1)S(1)}, u32[]{:S(2)}, u32[]{:S(2)}) collective-permute-start(bf16[336,768]{1,0:T(8,128)(2,1)} %get-tuple-element.44.refs_1_), channel_id=1, source_target_pairs={{0,4},{4,0},{1,5},{5,1},{2,6},{6,2},{3,7},{7,3},{8,12},{12,8},{9,1... | collective-permute-start | bytes 1548296 | tf_op jit(solution)/shard_map/ppermute | solution.py:578
  15.7 24.3 %collective-permute-start.5 = (bf16[336,768]{1,0:T(8,128)(2,1)}, bf16[336,768]{1,0:T(8,128)(2,1)}, u32[]{:S(2)}, u32[]{:S(2)}) collective-permute-start(bf16[336,768]{1,0:T(8,128)(2,1)} %get-tuple-element.44.refs_1_), channel_id=1, source_target_pairs={{0,1},{1,2},{2,3},{3,0},{4,5},{5,6},{6,7},{7,4},{8,9},{9,10},{10,1... | collective-permute-start | bytes 1548296 | tf_op jit(solution)/shard_map/ppermute | solution.py:574
  17.0 24.6 %collective-permute-start.1 = (bf16[336,768]{1,0:T(8,128)(2,1)}, bf16[336,768]{1,0:T(8,128)(2,1)}, u32[]{:S(2)}, u32[]{:S(2)}) collective-permute-start(bf16[336,768]{1,0:T(8,128)(2,1)} %get-tuple-element.44.refs_1_), channel_id=1, source_target_pairs={{0,3},{1,0},{2,1},{3,2},{4,7},{5,4},{6,5},{7,6},{8,11},{9,8},{10,9... | collective-permute-start | bytes 1548296 | tf_op jit(solution)/shard_map/ppermute | solution.py:574
  18.3 35.2 %collective-permute-start.6 = (bf16[352,768]{1,0:T(8,128)(2,1)S(1)}, bf16[352,768]{1,0:T(8,128)(2,1)S(1)}, u32[]{:S(2)}, u32[]{:S(2)}) collective-permute-start(bf16[352,768]{1,0:T(8,128)(2,1)S(1)} %copy-done.2), channel_id=1, source_target_pairs={{0,4},{4,0},{1,5},{5,1},{2,6},{6,2},{3,7},{7,3},{8,12},{12,8},{9,1... | collective-permute-start | bytes 1622024 | tf_op jit(solution)/shard_map/ppermute | solution.py:578
  18.9 22.7 %copy-start.7 = (bf16[336,768]{1,0:T(8,128)(2,1)}, bf16[336,768]{1,0:T(8,128)(2,1)S(1)}, u32[]{:S(2)}) copy-start(bf16[336,768]{1,0:T(8,128)(2,1)S(1)} %collective-permute-done.7.refs_9_) | copy-start | bytes 1548292
  18.9 35.8 %collective-permute-start = (bf16[352,768]{1,0:T(8,128)(2,1)S(1)}, bf16[352,768]{1,0:T(8,128)(2,1)}, u32[]{:S(2)}, u32[]{:S(2)}) collective-permute-start(bf16[352,768]{1,0:T(8,128)(2,1)S(1)} %copy-done.2), channel_id=1, source_target_pairs={{0,3},{1,0},{2,1},{3,2},{4,7},{5,4},{6,5},{7,6},{8,11},{9,8},{10,9... | collective-permute-start | bytes 1622024 | tf_op jit(solution)/shard_map/ppermute | solution.py:574
  28.8 41.7 %copy-start.3 = (bf16[352,768]{1,0:T(8,128)(2,1)}, bf16[352,768]{1,0:T(8,128)(2,1)S(1)}, u32[]{:S(2)}) copy-start(bf16[352,768]{1,0:T(8,128)(2,1)S(1)} %collective-permute-done.2.refs_6_) | copy-start | bytes 1622020
  28.8 26.0 %collective-permute-start.3 = (bf16[352,768]{1,0:T(8,128)(2,1)S(1)}, bf16[352,768]{1,0:T(8,128)(2,1)}, u32[]{:S(2)}, u32[]{:S(2)}) collective-permute-start(bf16[352,768]{1,0:T(8,128)(2,1)S(1)} %collective-permute-done.2.refs_6_), channel_id=1, source_target_pairs={{0,1},{1,2},{2,3},{3,0},{4,5},{5,6},{6,7},{7,4},{8,9},{9,10},{10,1... | collective-permute-start | bytes 1622024 | tf_op jit(solution)/shard_map/ppermute | solution.py:574
  40.0 15.3 %collective-permute-start.13 = (bf16[336,768]{1,0:T(8,128)(2,1)}, bf16[336,768]{1,0:T(8,128)(2,1)}, u32[]{:S(2)}, u32[]{:S(2)}) collective-permute-start(bf16[336,768]{1,0:T(8,128)(2,1)} %collective-permute-done.5.refs_7_), channel_id=1, source_target_pairs={{0,4},{4,0},{1,5},{5,1},{2,6},{6,2},{3,7},{7,3},{8,12},{12,8},{9,1... | collective-permute-start | bytes 1548296 | tf_op jit(solution)/shard_map/ppermute | solution.py:578
  41.6 13.8 %collective-permute-start.4 = (bf16[336,768]{1,0:T(8,128)(2,1)}, bf16[336,768]{1,0:T(8,128)(2,1)}, u32[]{:S(2)}, u32[]{:S(2)}) collective-permute-start(bf16[336,768]{1,0:T(8,128)(2,1)} %collective-permute-done.1.refs_3_), channel_id=1, source_target_pairs={{0,3},{1,0},{2,1},{3,2},{4,7},{5,4},{6,5},{7,6},{8,11},{9,8},{10,9... | collective-permute-start | bytes 1548296 | tf_op jit(solution)/shard_map/ppermute | solution.py:574
  46.4 24.1 %all-to-all-start.1 = ((bf16[128,3,8,128]{3,2,1,0:T(8,128)(2,1)}), bf16[128,3,8,128]{3,2,1,0:T(8,128)(2,1)S(1)}, u32[]{:S(2)}, u32[]{:S(2)}) async-start(bf16[128,3,8,128]{3,2,1,0:T(8,128)(2,1)} %get-tuple-element.42), calls=%async_computation.1 | async-start | bytes 1572864 | tf_op jit(solution)/shard_map/all_to_all | solution.py:570
  53.6 16.9 %copy-start.4 = (bf16[352,768]{1,0:T(8,128)(2,1)}, bf16[352,768]{1,0:T(8,128)(2,1)S(1)}, u32[]{:S(2)}) copy-start(bf16[352,768]{1,0:T(8,128)(2,1)S(1)} %collective-permute-done.6.refs_8_) | copy-start | bytes 1622020
  53.6 5.2 %collective-permute-start.12 = (bf16[352,768]{1,0:T(8,128)(2,1)S(1)}, bf16[352,768]{1,0:T(8,128)(2,1)S(1)}, u32[]{:S(2)}, u32[]{:S(2)}) collective-permute-start(bf16[352,768]{1,0:T(8,128)(2,1)S(1)} %collective-permute-done.2.refs_6_), channel_id=1, source_target_pairs={{0,4},{4,0},{1,5},{5,1},{2,6},{6,2},{3,7},{7,3},{8,12},{12,8},{9,1... | collective-permute-start | bytes 1622024 | tf_op jit(solution)/shard_map/ppermute | solution.py:578
  54.7 4.1 %collective-permute-start.8 = (bf16[352,768]{1,0:T(8,128)(2,1)}, bf16[352,768]{1,0:T(8,128)(2,1)S(1)}, u32[]{:S(2)}, u32[]{:S(2)}) collective-permute-start(bf16[352,768]{1,0:T(8,128)(2,1)} %collective-permute-done.refs_2_), channel_id=1, source_target_pairs={{0,4},{4,0},{1,5},{5,1},{2,6},{6,2},{3,7},{7,3},{8,12},{12,8},{9,1... | collective-permute-start | bytes 1622024 | tf_op jit(solution)/shard_map/ppermute | solution.py:578
  54.9 5.7 %collective-permute-start.10 = (bf16[352,768]{1,0:T(8,128)(2,1)}, bf16[352,768]{1,0:T(8,128)(2,1)}, u32[]{:S(2)}, u32[]{:S(2)}) collective-permute-start(bf16[352,768]{1,0:T(8,128)(2,1)} %collective-permute-done.3.refs_4_), channel_id=1, source_target_pairs={{0,4},{4,0},{1,5},{5,1},{2,6},{6,2},{3,7},{7,3},{8,12},{12,8},{9,1... | collective-permute-start | bytes 1622024 | tf_op jit(solution)/shard_map/ppermute | solution.py:578
  55.3 3.5 %collective-permute-start.9 = (bf16[336,768]{1,0:T(8,128)(2,1)}, bf16[336,768]{1,0:T(8,128)(2,1)S(1)}, u32[]{:S(2)}, u32[]{:S(2)}) collective-permute-start(bf16[336,768]{1,0:T(8,128)(2,1)} %collective-permute-done.1.refs_3_), channel_id=1, source_target_pairs={{0,4},{4,0},{1,5},{5,1},{2,6},{6,2},{3,7},{7,3},{8,12},{12,8},{9,1... | collective-permute-start | bytes 1548296 | tf_op jit(solution)/shard_map/ppermute | solution.py:578
  55.4 4.2 %collective-permute-start.11 = (bf16[336,768]{1,0:T(8,128)(2,1)}, bf16[336,768]{1,0:T(8,128)(2,1)S(1)}, u32[]{:S(2)}, u32[]{:S(2)}) collective-permute-start(bf16[336,768]{1,0:T(8,128)(2,1)} %collective-permute-done.4.refs_5_), channel_id=1, source_target_pairs={{0,4},{4,0},{1,5},{5,1},{2,6},{6,2},{3,7},{7,3},{8,12},{12,8},{9,1... | collective-permute-start | bytes 1548296 | tf_op jit(solution)/shard_map/ppermute | solution.py:578
  58.8 0.8 copy-start.8
  58.8 11.7 %copy-start.5 = (bf16[352,768]{1,0:T(8,128)(2,1)}, bf16[352,768]{1,0:T(8,128)(2,1)S(1)}, u32[]{:S(2)}) copy-start(bf16[352,768]{1,0:T(8,128)(2,1)S(1)} %collective-permute-done.12.refs_14_) | copy-start | bytes 1622020
  58.8 11.7 %copy-start.6 = (bf16[352,768]{1,0:T(8,128)(2,1)}, bf16[352,768]{1,0:T(8,128)(2,1)S(1)}, u32[]{:S(2)}) copy-start(bf16[352,768]{1,0:T(8,128)(2,1)S(1)} %collective-permute-done.8.refs_10_) | copy-start | bytes 1622020
  59.6 0.9 copy-start.9
  81.5 11.8 %collective-permute-start.14 = (bf16[256,384]{1,0:T(8,128)(2,1)S(1)}, bf16[256,384]{1,0:T(8,128)(2,1)S(1)}, u32[]{:S(2)}, u32[]{:S(2)}) collective-permute-start(bf16[256,384]{1,0:T(8,128)(2,1)S(1)} %get-tuple-element.53), channel_id=1, source_target_pairs={{0,1},{1,2},{2,3},{3,0},{4,5},{5,6},{6,7},{7,4},{8,9},{9,10},{10,1... | collective-permute-start | bytes 589832 | tf_op jit(solution)/shard_map/ppermute | solution.py:574
  81.9 11.3 %collective-permute-start.15 = (bf16[256,384]{1,0:T(8,128)(2,1)S(1)}, bf16[256,384]{1,0:T(8,128)(2,1)S(1)}, u32[]{:S(2)}, u32[]{:S(2)}) collective-permute-start(bf16[256,384]{1,0:T(8,128)(2,1)S(1)} %get-tuple-element.54), channel_id=1, source_target_pairs={{0,2},{1,3},{2,0},{3,1},{4,6},{5,7},{6,4},{7,5},{8,10},{9,11},{10,... | collective-permute-start | bytes 589832 | tf_op jit(solution)/shard_map/ppermute | solution.py:574
  83.3 10.2 %collective-permute-start.16 = (bf16[256,384]{1,0:T(8,128)(2,1)S(1)}, bf16[256,384]{1,0:T(8,128)(2,1)S(1)}, u32[]{:S(2)}, u32[]{:S(2)}) collective-permute-start(bf16[256,384]{1,0:T(8,128)(2,1)S(1)} %get-tuple-element.55), channel_id=1, source_target_pairs={{0,3},{1,0},{2,1},{3,2},{4,7},{5,4},{6,5},{7,6},{8,11},{9,8},{10,9... | collective-permute-start | bytes 589832 | tf_op jit(solution)/shard_map/ppermute | solution.py:574
  93.6 11.1 %collective-permute-start.17 = (bf16[256,384]{1,0:T(8,128)(2,1)S(1)}, bf16[256,384]{1,0:T(8,128)(2,1)S(1)}, u32[]{:S(2)}, u32[]{:S(2)}) collective-permute-start(bf16[256,384]{1,0:T(8,128)(2,1)S(1)} %get-tuple-element.56), channel_id=1, source_target_pairs={{0,1},{1,2},{2,3},{3,0},{4,5},{5,6},{6,7},{7,4},{8,9},{9,10},{10,1... | collective-permute-start | bytes 589832 | tf_op jit(solution)/shard_map/ppermute | solution.py:574
  94.5 11.7 %collective-permute-start.18 = (bf16[256,384]{1,0:T(8,128)(2,1)S(1)}, bf16[256,384]{1,0:T(8,128)(2,1)S(1)}, u32[]{:S(2)}, u32[]{:S(2)}) collective-permute-start(bf16[256,384]{1,0:T(8,128)(2,1)S(1)} %get-tuple-element.57), channel_id=1, source_target_pairs={{0,2},{1,3},{2,0},{3,1},{4,6},{5,7},{6,4},{7,5},{8,10},{9,11},{10,... | collective-permute-start | bytes 589832 | tf_op jit(solution)/shard_map/ppermute | solution.py:574
  97.7 8.6 %collective-permute-start.19 = (bf16[256,384]{1,0:T(8,128)(2,1)S(1)}, bf16[256,384]{1,0:T(8,128)(2,1)S(1)}, u32[]{:S(2)}, u32[]{:S(2)}) collective-permute-start(bf16[256,384]{1,0:T(8,128)(2,1)S(1)} %get-tuple-element.58), channel_id=1, source_target_pairs={{0,3},{1,0},{2,1},{3,2},{4,7},{5,4},{6,5},{7,6},{8,11},{9,8},{10,9... | collective-permute-start | bytes 589832 | tf_op jit(solution)/shard_map/ppermute | solution.py:574
  97.7 4.1 %copy-start = (f32[1,2,192,384]{3,2,1,0:T(8,128)S(1)}, f32[1,2,192,384]{3,2,1,0:T(8,128)}, u32[]{:S(2)}) copy-start(f32[1,2,192,384]{3,2,1,0:T(8,128)} %param.20) | copy-start | bytes 1769476
  97.7 4.1 %copy-start.1 = (f32[1,384,192]{1,2,0:T(8,128)S(1)}, f32[1,384,192]{1,2,0:T(8,128)}, u32[]{:S(2)}) copy-start(f32[1,384,192]{1,2,0:T(8,128)} %param.21) | copy-start | bytes 884740
  108.8 16.4 %all-to-all-start.2 = ((bf16[224,8,128]{2,1,0:T(8,128)(2,1)}), bf16[224,8,128]{2,1,0:T(8,128)(2,1)S(1)}, u32[]{:S(2)}, u32[]{:S(2)}) async-start(bf16[224,8,128]{2,1,0:T(8,128)(2,1)} %fast_grad.5), calls=%async_computation.2 | async-start | bytes 917504 | tf_op jit(solution)/shard_map/all_to_all | solution.py:570
  114.1 15.8 %collective-permute-start.20 = (bf16[768,384]{1,0:T(8,128)(2,1)S(1)}, bf16[768,384]{1,0:T(8,128)(2,1)S(1)}, u32[]{:S(2)}, u32[]{:S(2)}) collective-permute-start(bf16[768,384]{1,0:T(8,128)(2,1)S(1)} %get-tuple-element.73), channel_id=1, source_target_pairs={{0,1},{1,2},{2,3},{3,0},{4,5},{5,6},{6,7},{7,4},{8,9},{9,10},{10,1... | collective-permute-start | bytes 1769480 | tf_op jit(solution)/shard_map/ppermute | solution.py:574
  114.1 15.9 %collective-permute-start.21 = (bf16[768,384]{1,0:T(8,128)(2,1)}, bf16[768,384]{1,0:T(8,128)(2,1)S(1)}, u32[]{:S(2)}, u32[]{:S(2)}) collective-permute-start(bf16[768,384]{1,0:T(8,128)(2,1)} %get-tuple-element.74), channel_id=1, source_target_pairs={{0,3},{1,0},{2,1},{3,2},{4,7},{5,4},{6,5},{7,6},{8,11},{9,8},{10,9... | collective-permute-start | bytes 1769480 | tf_op jit(solution)/shard_map/ppermute | solution.py:574
  126.0 14.5 %all-to-all-start.3 = ((bf16[32,7,8,128]{3,2,1,0:T(8,128)(2,1)}), bf16[32,7,8,128]{3,2,1,0:T(8,128)(2,1)S(1)}, u32[]{:S(2)}, u32[]{:S(2)}) async-start(bf16[32,7,8,128]{3,2,1,0:T(8,128)(2,1)} %sum_pieces.1), calls=%async_computation.3 | async-start | bytes 917504 | tf_op jit(solution)/shard_map/all_to_all | solution.py:570
  129.9 6.5 %collective-permute-start.22 = (bf16[256,384]{1,0:T(8,128)(2,1)S(1)}, bf16[256,384]{1,0:T(8,128)(2,1)S(1)}, u32[]{:S(2)}, u32[]{:S(2)}) collective-permute-start(bf16[256,384]{1,0:T(8,128)(2,1)S(1)} %slice.8), channel_id=1, source_target_pairs={{0,1},{1,2},{2,3},{3,0},{4,5},{5,6},{6,7},{7,4},{8,9},{9,10},{10,1... | collective-permute-start | bytes 589832 | tf_op jit(solution)/shard_map/ppermute | solution.py:574
  130.1 6.4 %collective-permute-start.23 = (bf16[256,384]{1,0:T(8,128)(2,1)S(1)}, bf16[256,384]{1,0:T(8,128)(2,1)S(1)}, u32[]{:S(2)}, u32[]{:S(2)}) collective-permute-start(bf16[256,384]{1,0:T(8,128)(2,1)S(1)} %slice.9), channel_id=1, source_target_pairs={{0,3},{1,0},{2,1},{3,2},{4,7},{5,4},{6,5},{7,6},{8,11},{9,8},{10,9... | collective-permute-start | bytes 589832 | tf_op jit(solution)/shard_map/ppermute | solution.py:574
